TPU v7x, 32 devices: a whole 2x2x4 slice. The times are simulated.
32 devices in a mesh: seq: 16 (over z, y, core), grp: 2 (over x).
Axes of the slice: x: 2, y: 2, z: 4, core: 2. Of those that a mesh axis runs over, the one named last changes fastest.
Arguments:
- queries: bfloat16 [4096, 2048], P(('seq', 'grp')), may hold values from -6 to 6
- key_vectors: bfloat16 [4096, 2048], P(('seq', 'grp')), may hold values from -6 to 6
- head_value_rows: bfloat16 [4096, 2048], P(('seq', 'grp')), may hold values from -6 to 6
- out_gain: float32 [128], replicated, may hold values from 0.1 to 1.9
Outputs:
- mixed: bfloat16 [4096, 2048], P(('seq', 'grp'))
All inputs are finite; a program needn't handle non-finite values.
Results may differ from a plain program's by a relative error of at most 0.0035.
Values may be sent and summed in bfloat16 or wider, within the bound.
No kernel may reach another device: no remote copies, remote signals or barrier semaphores. Data moves between devices by JAX's collectives and lax.ppermute only.
A program may use at most 64 MiB of HBM per device.

v0:
```python
import jax
import jax.numpy as jnp
from jax import lax
from jax.sharding import PartitionSpec as P

HEAD_DIM = 128
BLOCK = 128


exact_precision = lax.Precision.HIGHEST
key_eps = 1e-06
norm_eps = 1e-05


def from_behind(value, axis, steps):
    count = lax.axis_size(axis)
    initial, last = (max(0, -steps), min(count, count - steps))
    return lax.ppermute(value, axis, [(source, source + steps) for source in range(initial, last)])


def block_terms(key_tile_rows, value_block):
    width = key_tile_rows.shape[0]
    strict_lower = jnp.tril(jnp.ones((width, width), jnp.float32), -1)
    inner = jnp.dot(key_tile_rows, key_tile_rows.T, precision=exact_precision)
    system = jnp.eye(width, dtype=jnp.float32) + 2.0 * strict_lower * inner
    stacked = jnp.concatenate([2.0 * key_tile_rows, 2.0 * value_block], axis=1)
    solved = jax.scipy.linalg.solve_triangular(system, stacked, lower=True, unit_diagonal=True)
    half = key_tile_rows.shape[1]
    return (solved[:, :half], solved[:, half:])


def product(left, right_operand):
    return jnp.einsum("hij,hjk->hik", left, right_operand, precision=exact_precision)


def keys_times(key_tile_rows, right_operand):
    return jnp.einsum("xyp,xyo->xpo", key_tile_rows, right_operand, precision=exact_precision)


def body(queries, key_vectors, head_value_rows, out_gain):
    query_rows, key_rows, value_rows = (
        lax.all_to_all(queries, "grp", split_axis=1, concat_axis=0, tiled=True),
        lax.all_to_all(key_vectors, "grp", split_axis=1, concat_axis=0, tiled=True),
        lax.all_to_all(head_value_rows, "grp", split_axis=1, concat_axis=0, tiled=True),
    )
    tokens = query_rows.shape[0]
    heads_here = query_rows.shape[1] // HEAD_DIM
    blocks = tokens // BLOCK

    def arrange(rows):
        return (
            rows.astype(jnp.float32)
            .reshape(blocks, BLOCK, heads_here, HEAD_DIM)
            .transpose(0, 2, 1, 3)
        )

    query_blocks = arrange(query_rows)
    raw_keys = arrange(key_rows)
    key_blocks = raw_keys / jnp.sqrt(jnp.sum(raw_keys * raw_keys, axis=3, keepdims=True) + key_eps)
    value_blocks = arrange(value_rows)
    key_weights, new_values = jax.vmap(jax.vmap(block_terms))(key_blocks, value_blocks)
    causal = jnp.tril(jnp.ones((BLOCK, BLOCK), jnp.float32))
    scores = causal * jnp.einsum(
        "nhik,nhjk->nhij", query_blocks, key_blocks, precision=exact_precision
    )
    identity = jnp.broadcast_to(
        jnp.eye(HEAD_DIM, dtype=jnp.float32), (heads_here, HEAD_DIM, HEAD_DIM)
    )
    zero_state = jnp.zeros((heads_here, HEAD_DIM, HEAD_DIM), jnp.float32)
    pieces = (query_blocks, key_blocks, key_weights, new_values, scores)

    def collect(carried, piece):
        state, transition = carried
        query_block, key_tile_rows, key_weight, new_value, score = piece
        delta = new_value - product(key_weight, state)
        state = state + keys_times(key_tile_rows, delta)
        transition = transition - keys_times(key_tile_rows, product(key_weight, transition))
        return ((state, transition), None)

    def emit(state, piece):
        query_block, key_tile_rows, key_weight, new_value, score = piece
        delta = new_value - product(key_weight, state)
        output = product(query_block, state) + product(score, delta)
        return (state + keys_times(key_tile_rows, delta), output)

    (shard_state, shard_trans), spare_rows = lax.scan(collect, (zero_state, identity), pieces)

    def relay(hop_index, arriving):
        leaving = product(shard_trans, arriving) + shard_state
        return from_behind(leaving, "seq", 1)

    incoming = lax.fori_loop(0, lax.axis_size("seq") - 1, relay, zero_state)
    final_state, outputs = lax.scan(emit, incoming, pieces)
    scale = lax.rsqrt(jnp.mean(outputs * outputs, axis=3, keepdims=True) + norm_eps)
    normed = (outputs * scale * out_gain).astype(jnp.bfloat16)
    token_major = normed.transpose(0, 2, 1, 3).reshape(tokens, heads_here * HEAD_DIM)
    return lax.all_to_all(token_major, "grp", split_axis=0, concat_axis=1, tiled=True)


def solution(mesh):
    in_specs = (P(("seq", "grp"), None), P(("seq", "grp"), None), P(("seq", "grp"), None), P())
    out_specs = P(("seq", "grp"), None)
    return jax.shard_map(body, mesh=mesh, in_specs=in_specs, out_specs=out_specs, check_vma=False)
```

profile of v0, /device:TPU:16, one launch (start us, length us, event | category | flops | bytes accessed | tf_op | source)
XLA Modules:
  0.0 415.1 jit_solution(9600478841297500460)
XLA Ops:
  0.0 2.1 copy.10
  2.1 3.5 all-to-all-start
  5.8 1.0 copy.12
  6.8 1.0 copy.16
  8.0 5.8 %all-to-all-done = bf16[128,2,1024]{0,2,1:T(8,128)(2,1)S(1)} async-done(((bf16[128,2,1024]{0,2,1:T(8,128)(2,1)}), bf16[128,2,1024]{0,2,1:T(8,128)(2,1)S(1)}, u32[]{:S(2)}, u32[]{:S(2)}) %all-to-all-start) | async-done | bytes 524320 | tf_op jit(solution)/shard_map/all_to_all | solution.py:43
  13.9 3.5 all-to-all-start.1
  18.1 1.3 broadcast_multiply_fusion
  19.8 3.3 fusion.39
  23.1 158.6 %custom-call.4 = f32[2,8,1,128,128]{3,4,2,1,0:T(8,128)} custom-call(f32[2,8,1,128,128]{4,3,2,1,0:T(8,128)} %fusion.39), custom_call_target="InvertDiagBlocksLowerTriangular" | custom-call | tf_op jit(solution)/shard_map/vmap(vmap(jit(_solve_triangular)))/triangular_solve | solution.py:27
  181.8 4.4 %all-to-all-start.2 = ((bf16[128,2,1024]{0,2,1:T(8,128)(2,1)}), bf16[128,2,1024]{0,2,1:T(8,128)(2,1)}, u32[]{:S(2)}, u32[]{:S(2)}) async-start(bf16[128,2,1024]{0,2,1:T(8,128)(2,1)} %bitcast.144), calls=%async_computation.2 | async-start | bytes 1048576 | tf_op jit(solution)/shard_map/all_to_all | solution.py:42
  186.2 1.1 convert_multiply_fusion
  187.3 2.6 copy.13
  189.8 3.5 fusion.32
  193.3 1.2 fusion.48
  194.6 7.9 %while.40 = (s32[]{:T(128)}, f32[8,128,128]{2,1,0:T(8,128)S(1)}, f32[8,128,128]{2,1,0:T(8,128)S(1)}, f32[2,8,128,128]{2,3,1,0:T(8,128)S(1)}, f32[2,8,128,128]{3,2,1,0:T(8,128)}, /*index=5*/f32[2,8,128,128]{3,2,1,0:T(8,128)S(1)}) while((s32[]{:T(128)}, f32[8,128,128]{2,1,0:T(8,128)S(1)}, f32[8,128,128]{2,1,0:T(8,128)S(1)}, ...), condition=%wide.region_2.3_spmd.clone.clone, body=%wide.region_1.2_spmd.clone.sunk.clone | while | flops 805961728 | bytes 7865436 | solution.py:86
  194.6 1.7 convolution_subtract_fusion.10
  197.7 0.8 convolution_subtract_fusion.11
  198.5 1.7 convolution_subtract_fusion.10
  201.7 0.8 convolution_subtract_fusion.11
  202.5 2.4 copy.17
  204.9 2.2 bitcast_convert_fusion
  207.2 3.2 fusion.40
  210.4 180.8 %while.38 = (s32[]{:T(128)}, f32[8,128,128]{2,1,0:T(8,128)S(1)}, f32[8,128,128]{2,1,0:T(8,128)S(1)}, f32[8,128,128]{2,1,0:T(8,128)S(1)}) while((s32[]{:T(128)}, f32[8,128,128]{2,1,0:T(8,128)S(1)}, f32[8,128,128]{2,1,0:T(8,128)S(1)}, f32[8,128,128]{2,1,0:T(8,128)S(1)}) %tuple.67), condition=%wide.region_4.5_spmd.clone, body=%wide.region_3.4_spmd.sunk.clone | while | flops 201457664 | bytes 4194397 | solution.py:92
  211.1 1.9 collective-permute-start
  213.0 9.5 %collective-permute-done = f32[8,128,128]{2,1,0:T(8,128)S(1)} collective-permute-done((f32[8,128,128]{2,1,0:T(8,128)S(1)}, f32[8,128,128]{2,1,0:T(8,128)S(1)}, u32[]{:S(2)}, u32[]{:S(2)}) %collective-permute-start) | collective-permute-done | bytes 524320 | tf_op jit(solution)/shard_map/while/body/eval_jaxpr/ppermute | solution.py:18
  223.1 1.9 collective-permute-start
  225.1 9.5 %collective-permute-done = f32[8,128,128]{2,1,0:T(8,128)S(1)} collective-permute-done((f32[8,128,128]{2,1,0:T(8,128)S(1)}, f32[8,128,128]{2,1,0:T(8,128)S(1)}, u32[]{:S(2)}, u32[]{:S(2)}) %collective-permute-start) | collective-permute-done | bytes 524320 | tf_op jit(solution)/shard_map/while/body/eval_jaxpr/ppermute | solution.py:18
  235.2 1.9 collective-permute-start
  237.1 9.5 %collective-permute-done = f32[8,128,128]{2,1,0:T(8,128)S(1)} collective-permute-done((f32[8,128,128]{2,1,0:T(8,128)S(1)}, f32[8,128,128]{2,1,0:T(8,128)S(1)}, u32[]{:S(2)}, u32[]{:S(2)}) %collective-permute-start) | collective-permute-done | bytes 524320 | tf_op jit(solution)/shard_map/while/body/eval_jaxpr/ppermute | solution.py:18
  247.2 1.9 collective-permute-start
  249.2 9.5 %collective-permute-done = f32[8,128,128]{2,1,0:T(8,128)S(1)} collective-permute-done((f32[8,128,128]{2,1,0:T(8,128)S(1)}, f32[8,128,128]{2,1,0:T(8,128)S(1)}, u32[]{:S(2)}, u32[]{:S(2)}) %collective-permute-start) | collective-permute-done | bytes 524320 | tf_op jit(solution)/shard_map/while/body/eval_jaxpr/ppermute | solution.py:18
  259.3 1.9 collective-permute-start
  261.2 9.5 %collective-permute-done = f32[8,128,128]{2,1,0:T(8,128)S(1)} collective-permute-done((f32[8,128,128]{2,1,0:T(8,128)S(1)}, f32[8,128,128]{2,1,0:T(8,128)S(1)}, u32[]{:S(2)}, u32[]{:S(2)}) %collective-permute-start) | collective-permute-done | bytes 524320 | tf_op jit(solution)/shard_map/while/body/eval_jaxpr/ppermute | solution.py:18
  271.4 1.9 collective-permute-start
  273.3 9.5 %collective-permute-done = f32[8,128,128]{2,1,0:T(8,128)S(1)} collective-permute-done((f32[8,128,128]{2,1,0:T(8,128)S(1)}, f32[8,128,128]{2,1,0:T(8,128)S(1)}, u32[]{:S(2)}, u32[]{:S(2)}) %collective-permute-start) | collective-permute-done | bytes 524320 | tf_op jit(solution)/shard_map/while/body/eval_jaxpr/ppermute | solution.py:18
  283.4 1.9 collective-permute-start
  285.3 9.5 %collective-permute-done = f32[8,128,128]{2,1,0:T(8,128)S(1)} collective-permute-done((f32[8,128,128]{2,1,0:T(8,128)S(1)}, f32[8,128,128]{2,1,0:T(8,128)S(1)}, u32[]{:S(2)}, u32[]{:S(2)}) %collective-permute-start) | collective-permute-done | bytes 524320 | tf_op jit(solution)/shard_map/while/body/eval_jaxpr/ppermute | solution.py:18
  295.5 1.9 collective-permute-start
  297.4 9.5 %collective-permute-done = f32[8,128,128]{2,1,0:T(8,128)S(1)} collective-permute-done((f32[8,128,128]{2,1,0:T(8,128)S(1)}, f32[8,128,128]{2,1,0:T(8,128)S(1)}, u32[]{:S(2)}, u32[]{:S(2)}) %collective-permute-start) | collective-permute-done | bytes 524320 | tf_op jit(solution)/shard_map/while/body/eval_jaxpr/ppermute | solution.py:18
  307.5 1.9 collective-permute-start
  309.4 9.5 %collective-permute-done = f32[8,128,128]{2,1,0:T(8,128)S(1)} collective-permute-done((f32[8,128,128]{2,1,0:T(8,128)S(1)}, f32[8,128,128]{2,1,0:T(8,128)S(1)}, u32[]{:S(2)}, u32[]{:S(2)}) %collective-permute-start) | collective-permute-done | bytes 524320 | tf_op jit(solution)/shard_map/while/body/eval_jaxpr/ppermute | solution.py:18
  319.6 1.9 collective-permute-start
  321.5 9.5 %collective-permute-done = f32[8,128,128]{2,1,0:T(8,128)S(1)} collective-permute-done((f32[8,128,128]{2,1,0:T(8,128)S(1)}, f32[8,128,128]{2,1,0:T(8,128)S(1)}, u32[]{:S(2)}, u32[]{:S(2)}) %collective-permute-start) | collective-permute-done | bytes 524320 | tf_op jit(solution)/shard_map/while/body/eval_jaxpr/ppermute | solution.py:18
  331.6 1.9 collective-permute-start
  333.6 9.5 %collective-permute-done = f32[8,128,128]{2,1,0:T(8,128)S(1)} collective-permute-done((f32[8,128,128]{2,1,0:T(8,128)S(1)}, f32[8,128,128]{2,1,0:T(8,128)S(1)}, u32[]{:S(2)}, u32[]{:S(2)}) %collective-permute-start) | collective-permute-done | bytes 524320 | tf_op jit(solution)/shard_map/while/body/eval_jaxpr/ppermute | solution.py:18
  343.7 1.9 collective-permute-start
  345.6 9.5 %collective-permute-done = f32[8,128,128]{2,1,0:T(8,128)S(1)} collective-permute-done((f32[8,128,128]{2,1,0:T(8,128)S(1)}, f32[8,128,128]{2,1,0:T(8,128)S(1)}, u32[]{:S(2)}, u32[]{:S(2)}) %collective-permute-start) | collective-permute-done | bytes 524320 | tf_op jit(solution)/shard_map/while/body/eval_jaxpr/ppermute | solution.py:18
  355.7 1.9 collective-permute-start
  357.7 9.5 %collective-permute-done = f32[8,128,128]{2,1,0:T(8,128)S(1)} collective-permute-done((f32[8,128,128]{2,1,0:T(8,128)S(1)}, f32[8,128,128]{2,1,0:T(8,128)S(1)}, u32[]{:S(2)}, u32[]{:S(2)}) %collective-permute-start) | collective-permute-done | bytes 524320 | tf_op jit(solution)/shard_map/while/body/eval_jaxpr/ppermute | solution.py:18
  367.8 1.9 collective-permute-start
  369.7 9.5 %collective-permute-done = f32[8,128,128]{2,1,0:T(8,128)S(1)} collective-permute-done((f32[8,128,128]{2,1,0:T(8,128)S(1)}, f32[8,128,128]{2,1,0:T(8,128)S(1)}, u32[]{:S(2)}, u32[]{:S(2)}) %collective-permute-start) | collective-permute-done | bytes 524320 | tf_op jit(solution)/shard_map/while/body/eval_jaxpr/ppermute | solution.py:18
  379.8 1.9 collective-permute-start
  381.8 9.5 %collective-permute-done = f32[8,128,128]{2,1,0:T(8,128)S(1)} collective-permute-done((f32[8,128,128]{2,1,0:T(8,128)S(1)}, f32[8,128,128]{2,1,0:T(8,128)S(1)}, u32[]{:S(2)}, u32[]{:S(2)}) %collective-permute-start) | collective-permute-done | bytes 524320 | tf_op jit(solution)/shard_map/while/body/eval_jaxpr/ppermute | solution.py:18
  391.2 11.0 %while.39 = (s32[]{:T(128)}, f32[8,128,128]{2,1,0:T(8,128)S(1)}, f32[2,8,128,128]{3,2,1,0:T(8,128)}, f32[2,8,128,128]{2,3,1,0:T(8,128)S(1)}, f32[2,8,128,128]{3,...) while((s32[]{:T(128)}, f32[8,128,128]{2,1,0:T(8,128)S(1)}, ...), condition=%wide.region_6.7_spmd.clone, body=%wide.region_5.6_spmd.sunk.clone | while | flops 805699584 | bytes 24643788 | solution.py:93
  391.2 2.0 convolution_subtract_fusion.9
  393.9 1.0 fusion.114
  395.0 1.0 copy-done.7
  396.8 2.0 convolution_subtract_fusion.9
  399.5 1.0 fusion.114
  400.5 1.0 copy-done.7
  401.5 0.8 convolution_add_fusion.11
  402.3 1.6 copy.21
  404.5 9.6 %all_to_all.64 = bf16[2,128,1024]{1,2,0:T(8,128)(2,1)S(1)} all-to-all(bf16[2,128,1024]{1,2,0:T(8,128)(2,1)S(1)} %bitcast.145), channel_id=1, replica_groups=mesh['seq'=16,'grp'=2] {'grp'}, dimensions={0} | all-to-all | bytes 1048576 | tf_op jit(solution)/shard_map/all_to_all | solution.py:97
  414.1 1.0 copy.22
  (72 shorter events, 16.6 us)
Async XLA Ops:
  0.0 5.8 %copy-start.9 = (bf16[128,2048]{1,0:T(8,128)(2,1)S(1)}, bf16[128,2048]{1,0:T(8,128)(2,1)}, u32[]{:S(2)}) copy-start(bf16[128,2048]{1,0:T(8,128)(2,1)} %param.12) | copy-start | bytes 1572868
  0.0 6.8 %copy-start.10 = (bf16[128,2048]{1,0:T(8,128)(2,1)S(1)}, bf16[128,2048]{1,0:T(8,128)(2,1)}, u32[]{:S(2)}) copy-start(bf16[128,2048]{1,0:T(8,128)(2,1)} %param.10) | copy-start | bytes 1572868
  2.1 11.7 %all-to-all-start = ((bf16[128,2,1024]{0,2,1:T(8,128)(2,1)}), bf16[128,2,1024]{0,2,1:T(8,128)(2,1)S(1)}, u32[]{:S(2)}, u32[]{:S(2)}) async-start(bf16[128,2,1024]{0,2,1:T(8,128)(2,1)} %bitcast.6), calls=%async_computation | async-start | bytes 1048576 | tf_op jit(solution)/shard_map/all_to_all | solution.py:43
  13.9 167.9 %all-to-all-start.1 = ((bf16[128,2,1024]{0,2,1:T(8,128)(2,1)}), bf16[128,2,1024]{0,2,1:T(8,128)(2,1)S(1)}, u32[]{:S(2)}, u32[]{:S(2)}) async-start(bf16[128,2,1024]{0,2,1:T(8,128)(2,1)} %bitcast.12), calls=%async_computation.1 | async-start | bytes 1048576 | tf_op jit(solution)/shard_map/all_to_all | solution.py:44
  19.5 3.6 copy-start.1
  181.8 20.7 %all-to-all-start.2 = ((bf16[128,2,1024]{0,2,1:T(8,128)(2,1)}), bf16[128,2,1024]{0,2,1:T(8,128)(2,1)}, u32[]{:S(2)}, u32[]{:S(2)}) async-start(bf16[128,2,1024]{0,2,1:T(8,128)(2,1)} %bitcast.144), calls=%async_computation.2 | async-start | bytes 1048576 | tf_op jit(solution)/shard_map/all_to_all | solution.py:42
  186.2 3.6 copy-start.5
  202.5 7.9 %copy-start = (f32[2,8,128,128]{3,2,1,0:T(8,128)}, f32[2,8,128,128]{3,2,1,0:T(8,128)S(1)}, u32[]{:S(2)}) copy-start(f32[2,8,128,128]{3,2,1,0:T(8,128)S(1)} %get-tuple-element.407) | copy-start | bytes 3145732
  204.9 2.2 copy-start.2
  211.1 11.4 %collective-permute-start = (f32[8,128,128]{2,1,0:T(8,128)S(1)}, f32[8,128,128]{2,1,0:T(8,128)S(1)}, u32[]{:S(2)}, u32[]{:S(2)}) collective-permute-start(f32[8,128,128]{2,1,0:T(8,128)S(1)} %convolution_add_fusion.10), channel_id=1, source_target_pairs={{0,2},{2,4},{4,6},{6,8},{8,10},{10,12},{12,14},{14,16},{16,18},{18... | collective-permute-start | bytes 1572872 | tf_op jit(solution)/shard_map/while/body/eval_jaxpr/ppermute | solution.py:18
  223.1 11.4 %collective-permute-start = (f32[8,128,128]{2,1,0:T(8,128)S(1)}, f32[8,128,128]{2,1,0:T(8,128)S(1)}, u32[]{:S(2)}, u32[]{:S(2)}) collective-permute-start(f32[8,128,128]{2,1,0:T(8,128)S(1)} %convolution_add_fusion.10), channel_id=1, source_target_pairs={{0,2},{2,4},{4,6},{6,8},{8,10},{10,12},{12,14},{14,16},{16,18},{18... | collective-permute-start | bytes 1572872 | tf_op jit(solution)/shard_map/while/body/eval_jaxpr/ppermute | solution.py:18
  235.2 11.4 %collective-permute-start = (f32[8,128,128]{2,1,0:T(8,128)S(1)}, f32[8,128,128]{2,1,0:T(8,128)S(1)}, u32[]{:S(2)}, u32[]{:S(2)}) collective-permute-start(f32[8,128,128]{2,1,0:T(8,128)S(1)} %convolution_add_fusion.10), channel_id=1, source_target_pairs={{0,2},{2,4},{4,6},{6,8},{8,10},{10,12},{12,14},{14,16},{16,18},{18... | collective-permute-start | bytes 1572872 | tf_op jit(solution)/shard_map/while/body/eval_jaxpr/ppermute | solution.py:18
  247.2 11.4 %collective-permute-start = (f32[8,128,128]{2,1,0:T(8,128)S(1)}, f32[8,128,128]{2,1,0:T(8,128)S(1)}, u32[]{:S(2)}, u32[]{:S(2)}) collective-permute-start(f32[8,128,128]{2,1,0:T(8,128)S(1)} %convolution_add_fusion.10), channel_id=1, source_target_pairs={{0,2},{2,4},{4,6},{6,8},{8,10},{10,12},{12,14},{14,16},{16,18},{18... | collective-permute-start | bytes 1572872 | tf_op jit(solution)/shard_map/while/body/eval_jaxpr/ppermute | solution.py:18
  259.3 11.4 %collective-permute-start = (f32[8,128,128]{2,1,0:T(8,128)S(1)}, f32[8,128,128]{2,1,0:T(8,128)S(1)}, u32[]{:S(2)}, u32[]{:S(2)}) collective-permute-start(f32[8,128,128]{2,1,0:T(8,128)S(1)} %convolution_add_fusion.10), channel_id=1, source_target_pairs={{0,2},{2,4},{4,6},{6,8},{8,10},{10,12},{12,14},{14,16},{16,18},{18... | collective-permute-start | bytes 1572872 | tf_op jit(solution)/shard_map/while/body/eval_jaxpr/ppermute | solution.py:18
  271.4 11.4 %collective-permute-start = (f32[8,128,128]{2,1,0:T(8,128)S(1)}, f32[8,128,128]{2,1,0:T(8,128)S(1)}, u32[]{:S(2)}, u32[]{:S(2)}) collective-permute-start(f32[8,128,128]{2,1,0:T(8,128)S(1)} %convolution_add_fusion.10), channel_id=1, source_target_pairs={{0,2},{2,4},{4,6},{6,8},{8,10},{10,12},{12,14},{14,16},{16,18},{18... | collective-permute-start | bytes 1572872 | tf_op jit(solution)/shard_map/while/body/eval_jaxpr/ppermute | solution.py:18
  283.4 11.4 %collective-permute-start = (f32[8,128,128]{2,1,0:T(8,128)S(1)}, f32[8,128,128]{2,1,0:T(8,128)S(1)}, u32[]{:S(2)}, u32[]{:S(2)}) collective-permute-start(f32[8,128,128]{2,1,0:T(8,128)S(1)} %convolution_add_fusion.10), channel_id=1, source_target_pairs={{0,2},{2,4},{4,6},{6,8},{8,10},{10,12},{12,14},{14,16},{16,18},{18... | collective-permute-start | bytes 1572872 | tf_op jit(solution)/shard_map/while/body/eval_jaxpr/ppermute | solution.py:18
  295.5 11.4 %collective-permute-start = (f32[8,128,128]{2,1,0:T(8,128)S(1)}, f32[8,128,128]{2,1,0:T(8,128)S(1)}, u32[]{:S(2)}, u32[]{:S(2)}) collective-permute-start(f32[8,128,128]{2,1,0:T(8,128)S(1)} %convolution_add_fusion.10), channel_id=1, source_target_pairs={{0,2},{2,4},{4,6},{6,8},{8,10},{10,12},{12,14},{14,16},{16,18},{18... | collective-permute-start | bytes 1572872 | tf_op jit(solution)/shard_map/while/body/eval_jaxpr/ppermute | solution.py:18
  307.5 11.4 %collective-permute-start = (f32[8,128,128]{2,1,0:T(8,128)S(1)}, f32[8,128,128]{2,1,0:T(8,128)S(1)}, u32[]{:S(2)}, u32[]{:S(2)}) collective-permute-start(f32[8,128,128]{2,1,0:T(8,128)S(1)} %convolution_add_fusion.10), channel_id=1, source_target_pairs={{0,2},{2,4},{4,6},{6,8},{8,10},{10,12},{12,14},{14,16},{16,18},{18... | collective-permute-start | bytes 1572872 | tf_op jit(solution)/shard_map/while/body/eval_jaxpr/ppermute | solution.py:18
  319.6 11.4 %collective-permute-start = (f32[8,128,128]{2,1,0:T(8,128)S(1)}, f32[8,128,128]{2,1,0:T(8,128)S(1)}, u32[]{:S(2)}, u32[]{:S(2)}) collective-permute-start(f32[8,128,128]{2,1,0:T(8,128)S(1)} %convolution_add_fusion.10), channel_id=1, source_target_pairs={{0,2},{2,4},{4,6},{6,8},{8,10},{10,12},{12,14},{14,16},{16,18},{18... | collective-permute-start | bytes 1572872 | tf_op jit(solution)/shard_map/while/body/eval_jaxpr/ppermute | solution.py:18
  331.6 11.4 %collective-permute-start = (f32[8,128,128]{2,1,0:T(8,128)S(1)}, f32[8,128,128]{2,1,0:T(8,128)S(1)}, u32[]{:S(2)}, u32[]{:S(2)}) collective-permute-start(f32[8,128,128]{2,1,0:T(8,128)S(1)} %convolution_add_fusion.10), channel_id=1, source_target_pairs={{0,2},{2,4},{4,6},{6,8},{8,10},{10,12},{12,14},{14,16},{16,18},{18... | collective-permute-start | bytes 1572872 | tf_op jit(solution)/shard_map/while/body/eval_jaxpr/ppermute | solution.py:18
  343.7 11.4 %collective-permute-start = (f32[8,128,128]{2,1,0:T(8,128)S(1)}, f32[8,128,128]{2,1,0:T(8,128)S(1)}, u32[]{:S(2)}, u32[]{:S(2)}) collective-permute-start(f32[8,128,128]{2,1,0:T(8,128)S(1)} %convolution_add_fusion.10), channel_id=1, source_target_pairs={{0,2},{2,4},{4,6},{6,8},{8,10},{10,12},{12,14},{14,16},{16,18},{18... | collective-permute-start | bytes 1572872 | tf_op jit(solution)/shard_map/while/body/eval_jaxpr/ppermute | solution.py:18
  355.7 11.4 %collective-permute-start = (f32[8,128,128]{2,1,0:T(8,128)S(1)}, f32[8,128,128]{2,1,0:T(8,128)S(1)}, u32[]{:S(2)}, u32[]{:S(2)}) collective-permute-start(f32[8,128,128]{2,1,0:T(8,128)S(1)} %convolution_add_fusion.10), channel_id=1, source_target_pairs={{0,2},{2,4},{4,6},{6,8},{8,10},{10,12},{12,14},{14,16},{16,18},{18... | collective-permute-start | bytes 1572872 | tf_op jit(solution)/shard_map/while/body/eval_jaxpr/ppermute | solution.py:18
  367.8 11.4 %collective-permute-start = (f32[8,128,128]{2,1,0:T(8,128)S(1)}, f32[8,128,128]{2,1,0:T(8,128)S(1)}, u32[]{:S(2)}, u32[]{:S(2)}) collective-permute-start(f32[8,128,128]{2,1,0:T(8,128)S(1)} %convolution_add_fusion.10), channel_id=1, source_target_pairs={{0,2},{2,4},{4,6},{6,8},{8,10},{10,12},{12,14},{14,16},{16,18},{18... | collective-permute-start | bytes 1572872 | tf_op jit(solution)/shard_map/while/body/eval_jaxpr/ppermute | solution.py:18
  379.8 11.4 %collective-permute-start = (f32[8,128,128]{2,1,0:T(8,128)S(1)}, f32[8,128,128]{2,1,0:T(8,128)S(1)}, u32[]{:S(2)}, u32[]{:S(2)}) collective-permute-start(f32[8,128,128]{2,1,0:T(8,128)S(1)} %convolution_add_fusion.10), channel_id=1, source_target_pairs={{0,2},{2,4},{4,6},{6,8},{8,10},{10,12},{12,14},{14,16},{16,18},{18... | collective-permute-start | bytes 1572872 | tf_op jit(solution)/shard_map/while/body/eval_jaxpr/ppermute | solution.py:18
  391.2 2.0 copy-start.3
  391.2 2.7 copy-start.4
  391.2 2.7 copy-start.6
  395.0 1.0 copy-start.7
  396.7 2.0 copy-start.3
  396.8 2.7 copy-start.4
  396.8 2.7 copy-start.6
  400.5 1.0 copy-start.7
  402.3 1.7 copy-start.8
  402.3 2.0 copy-start.11
where the time goes:
time: 416 us; the launch traced here: 415 us
  other arithmetic  164 us (39%)
  waiting for transfers between devices  148 us (36%)
  starting transfers between devices  40.2 us (10%)
  matrix products  36.4 us (9%)
  local copies, waits for them, and re-layouts  15.8 us (4%)
  blocking collectives  9.62 us (2%)
    another operation x5, other arithmetic, block_terms(): jax.scipy.linalg.solve_triangular(system, stacked, lower=True, unit_diago...  159 us
    ppermute x15, waiting for transfers between devices, from_behind(): lax.ppermute(value, axis, [(source, source + steps) for source in range(i...  142 us
    ppermute x15, starting transfers between devices, from_behind(): lax.ppermute(value, axis, [(source, source + steps) for source in range(i...  28.8 us
    dot_general x25, matrix products, product(): jnp.einsum('hij,hjk->hik', left, right_operand, precision=exact_precision)  21.7 us
    all_to_all x1, blocking collectives, body(): lax.all_to_all(token_major, 'grp', split_axis=0, concat_axis=1, tiled=True)  9.62 us
  transfers between devices with their start and end apart: 18, of which 16 were waited for; matrix products, arithmetic and copies ran while one was open for 44% of the time, Pallas kernels for 0%

commit v1 on v0

v1 whole, which is shorter than its diff:
```python
import functools

import jax
import jax.numpy as jnp
from jax import lax
from jax.experimental import pallas as pl
from jax.experimental.pallas import tpu as pltpu
from jax.sharding import Mesh
from jax.sharding import PartitionSpec as P

HEAD_DIM = 128
BLOCK = 128
key_eps = 1e-06
norm_eps = 1e-05
BATCH = 8

f32 = jnp.float32
bf16 = jnp.bfloat16


def mm(left, right):
    return jnp.dot(left, right, preferred_element_type=f32)


def mm_nt(left, right):
    return lax.dot_general(left, right, (((1,), (1,)), ((), ())), preferred_element_type=f32)


def split(value):
    high = value.astype(bf16)
    low = (value - high.astype(f32)).astype(bf16)
    return jnp.concatenate([high, low], axis=1)


def twice(rows):
    return jnp.concatenate([rows, rows], axis=0)


def fold(wide):
    half = wide.shape[1] // 2
    return wide[:, :half] + wide[:, half:]


def product(left_pair, right_pair):
    return fold(mm(left_pair, twice(right_pair)))


def product_wide(left_pair, first_pair, second_pair):
    n = HEAD_DIM
    highs = jnp.concatenate([first_pair[:, :n], second_pair[:, :n]], axis=1)
    lows = jnp.concatenate([first_pair[:, n:], second_pair[:, n:]], axis=1)
    return mm(left_pair, twice(highs)) + mm(left_pair[:, :n], lows)


def iotas():
    row = lax.broadcasted_iota(jnp.int32, (BLOCK, BLOCK), 0)
    col = lax.broadcasted_iota(jnp.int32, (BLOCK, BLOCK), 1)
    return row, col


def batches(count, run):
    size = min(BATCH, count)
    if count == size:
        run([j for j in range(count)])
    else:
        def one(i, carried):
            run([i * size + j for j in range(size)])
            return carried
        lax.fori_loop(0, count // size, one, 0)


def keys_kernel(k_ref, w_ref, tu_ref, a_ref):
    count = k_ref.shape[0]
    row, col = iotas()
    diagonal = row == col
    eye = diagonal.astype(f32)

    def run(blocks):
        keys = [k_ref[j] for j in blocks]
        grams = [mm_nt(k, k) for k in keys]
        coupling, scale_cols, scale_rows = [], [], []
        for g in grams:
            on_diagonal = jnp.where(diagonal, g, 0.0)
            c = 1.0 / jnp.sqrt(jnp.sum(on_diagonal, axis=1, keepdims=True) + key_eps)
            r = 1.0 / jnp.sqrt(jnp.sum(on_diagonal, axis=0, keepdims=True) + key_eps)
            scale_cols.append(c)
            scale_rows.append(r)
            coupling.append(jnp.where(row > col, (2.0 * c) * g * r, 0.0))
        size = 1
        inverses = None
        while size < BLOCK:
            mask = ((row // size) % 2 == 1) & (col // size == row // size - 1)
            parts = [jnp.where(mask, n, 0.0) for n in coupling]
            if inverses is None:
                inverses = [eye - p for p in parts]
            else:
                pairs = [split(t) for t in inverses]
                inner = [product(split(p), t) for p, t in zip(parts, pairs)]
                outer = [product(t, split(z)) for t, z in zip(pairs, inner)]
                inverses = [t - z for t, z in zip(inverses, outer)]
            size *= 2
        for i, j in enumerate(blocks):
            left = (2.0 * scale_cols[i]) * inverses[i]
            tu_ref[j] = split(left)
            weights = mm(split(left * scale_rows[i]), twice(keys[i]))
            weights_pair = split(weights)
            w_ref[j] = weights_pair
            a_ref[j] = split(eye - fold(mm(keys[i].T, weights_pair)))

    batches(count, run)


def tree_offsets(count):
    offsets, at, size = [], 0, count
    while size >= 1:
        offsets.append(at)
        at += size
        size //= 2
    return offsets, at


def values_kernel(k_ref, v_ref, tu_ref, a_leaf_ref, u_ref, a_ref, b_ref, total_ref):
    count = k_ref.shape[0]
    offsets, _ = tree_offsets(count)

    def run(blocks):
        for j in blocks:
            changes = split(mm(tu_ref[j], twice(v_ref[j])))
            u_ref[j] = changes
            a_ref[j] = a_leaf_ref[j]
            b_ref[j] = fold(mm(k_ref[j].T, changes))

    batches(count, run)
    for level in range(1, len(offsets)):
        below, here = offsets[level - 1], offsets[level]
        for i in range(count >> level):
            first, second = below + 2 * i, below + 2 * i + 1
            later = a_ref[second]
            joint = product_wide(later, a_ref[first], split(b_ref[first]))
            a_ref[here + i] = split(joint[:, :HEAD_DIM])
            b_ref[here + i] = joint[:, HEAD_DIM:] + b_ref[second]
    total_ref[...] = b_ref[offsets[-1]]


def queries_kernel(q_ref, k_ref, w_ref, u_ref, a_ref, b_ref, qp_ref, op_ref, pa_ref, pb_ref):
    count = q_ref.shape[0]
    offsets, _ = tree_offsets(count)
    row, col = iotas()
    causal = row >= col
    eye = (row == col).astype(f32)
    levels = len(offsets)
    for level in range(levels - 1, -1, -1):
        here = offsets[level]
        if level == levels - 1:
            pa_ref[here] = split(eye)
            pb_ref[here] = jnp.zeros((HEAD_DIM, HEAD_DIM), f32)
            continue
        above = offsets[level + 1]
        for i in range(count >> (level + 1)):
            left, right, parent = here + 2 * i, here + 2 * i + 1, above + i
            pa_ref[left] = pa_ref[parent]
            pb_ref[left] = pb_ref[parent]
            if i == 0:
                pa_ref[right] = a_ref[left]
                pb_ref[right] = b_ref[left]
            else:
                joint = product_wide(a_ref[left], pa_ref[parent], split(pb_ref[parent]))
                pa_ref[right] = split(joint[:, :HEAD_DIM])
                pb_ref[right] = joint[:, HEAD_DIM:] + b_ref[left]

    def run(blocks):
        scores = [jnp.where(causal, mm_nt(q_ref[j], k_ref[j]), 0.0) for j in blocks]
        local = [product_wide(split(c), w_ref[j], u_ref[j]) for c, j in zip(scores, blocks)]
        for i, j in enumerate(blocks):
            mixed = q_ref[j].astype(f32) - local[i][:, :HEAD_DIM]
            joint = product_wide(split(mixed), pa_ref[j], split(pb_ref[j]))
            qp_ref[j] = split(joint[:, :HEAD_DIM])
            op_ref[j] = joint[:, HEAD_DIM:] + local[i][:, HEAD_DIM:]

    batches(count, run)


def finish_kernel(qp_ref, op_ref, state_ref, gain_ref, out_ref):
    state = twice(split(state_ref[...]))
    gain = gain_ref[...]
    for j in range(qp_ref.shape[0]):
        output = fold(mm(qp_ref[j], state)) + op_ref[j]
        scale = lax.rsqrt(jnp.mean(output * output, axis=1, keepdims=True) + norm_eps)
        out_ref[j] = (output * scale * gain).astype(bf16)


def call(kernel, name, outs, flops, scratch=()):
    vmem = pl.BlockSpec(memory_space=pltpu.VMEM)
    return pl.pallas_call(
        kernel,
        name=name,
        out_shape=tuple(jax.ShapeDtypeStruct(s, t) for s, t in outs),
        out_specs=tuple(vmem for _ in outs),
        scratch_shapes=list(scratch),
        cost_estimate=pl.CostEstimate(flops=flops, bytes_accessed=4 << 20, transcendentals=0),
    )


def body(groups, lanes, queries, key_vectors, head_value_rows, out_gain):
    tokens, features = queries.shape
    heads = features // HEAD_DIM
    blocks = lanes * tokens // BLOCK

    def to_heads(rows):
        pieces = rows.reshape(tokens, heads, HEAD_DIM).transpose(1, 0, 2)
        arrived = lax.all_to_all(pieces, "lo", split_axis=0, concat_axis=0, tiled=True)
        return arrived.reshape(blocks, BLOCK, HEAD_DIM)

    keys = to_heads(key_vectors)
    values = to_heads(head_value_rows)
    query_blocks = to_heads(queries)
    _, nodes = tree_offsets(blocks)
    one = (HEAD_DIM, HEAD_DIM)
    pair = (HEAD_DIM, 2 * HEAD_DIM)
    unit = 2 * BLOCK**3 * 4
    w, tu, a_leaf = call(
        keys_kernel, "keys",
        [((blocks, *pair), bf16), ((blocks, *pair), bf16), ((blocks, *pair), bf16)],
        unit * blocks * 14,
    )(keys)
    u, a, b, total = call(
        values_kernel, "values",
        [((blocks, *pair), bf16), ((nodes, *pair), bf16), ((nodes, *one), f32), (one, f32)],
        unit * blocks * 4,
    )(keys, values, tu, a_leaf)
    hop = [(source, source + 1) for source in range(groups - 1)]
    incoming = lax.ppermute(total, "hi", hop)
    if groups > 2:
        top = a[nodes - 1].astype(f32)
        transition = top[:, :HEAD_DIM] + top[:, HEAD_DIM:]

        def relay(i, arriving):
            leaving = jnp.dot(transition, arriving, precision=lax.Precision.HIGHEST) + total
            return lax.ppermute(leaving, "hi", hop)

        incoming = lax.fori_loop(0, groups - 2, relay, incoming)
    qp, op = call(
        queries_kernel, "queries",
        [((blocks, *pair), bf16), ((blocks, *one), f32)],
        unit * blocks * 6,
        [pltpu.VMEM((nodes, *pair), bf16), pltpu.VMEM((nodes, *one), f32)],
    )(query_blocks, keys, w, u, a, b)
    (out,) = call(
        finish_kernel, "finish", [((blocks, BLOCK, HEAD_DIM), bf16)], unit * blocks,
    )(qp, op, incoming, out_gain.reshape(1, HEAD_DIM))
    back = lax.all_to_all(out.reshape(lanes, tokens, HEAD_DIM), "lo", split_axis=0, concat_axis=0, tiled=True)
    return back.transpose(1, 0, 2).reshape(tokens, features)


def solution(mesh):
    count = mesh.devices.size

    def run(queries, key_vectors, head_value_rows, out_gain):
        lanes = queries.shape[1] // HEAD_DIM
        regrouped = Mesh(mesh.devices.reshape(count // lanes, lanes), ("hi", "lo"))
        rows = P(("hi", "lo"), None)
        return jax.shard_map(
            functools.partial(body, count // lanes, lanes),
            mesh=regrouped, in_specs=(rows, rows, rows, P()), out_specs=rows, check_vma=False,
        )(queries, key_vectors, head_value_rows, out_gain)

    return run
```

time: 416 us -> 81 us (0.19)
  the two profiles are of different devices: /device:TPU:16 before, /device:TPU:0 now
where the time goes in v1:
time: 81 us; the launch traced here: 80.3 us
  Pallas kernels  24.9 us (31%)
  starting transfers between devices  18.1 us (22%)
  waiting for transfers between devices  15.5 us (19%)
  blocking collectives  14.1 us (17%)
  local copies, waits for them, and re-layouts  7.65 us (9%)
    all_to_all x3, waiting for transfers between devices, to_heads(): lax.all_to_all(pieces, 'lo', split_axis=0, concat_axis=0, tiled=True)  15.5 us
    all_to_all x1, blocking collectives, body(): lax.all_to_all(out.reshape(lanes, tokens, HEAD_DIM), 'lo', split_axis=0,...  14.1 us
    all_to_all x3, starting transfers between devices, to_heads(): lax.all_to_all(pieces, 'lo', split_axis=0, concat_axis=0, tiled=True)  13.6 us
    pallas_call x1, Pallas kernels, body(): call(keys_kernel, 'keys', [((blocks, *pair), bf16), ((blocks, *pair), bf1...  9.16 us
    pallas_call x1, Pallas kernels, body(): call(queries_kernel, 'queries', [((blocks, *pair), bf16), ((blocks, *one)...  7.05 us
    pallas_call x1, Pallas kernels, body(): call(values_kernel, 'values', [((blocks, *pair), bf16), ((nodes, *pair),...  5.84 us
    ppermute x1, starting transfers between devices, body(): incoming = lax.ppermute(total, 'hi', hop)  4.49 us
    unnamed x15, local copies, waits for them, and re-layouts  3.32 us
  transfers between devices with their start and end apart: 4, of which 2 were waited for; matrix products, arithmetic and copies ran while one was open for 3% of the time, Pallas kernels for 27%

profile of v1, /device:TPU:0, one launch (start us, length us, event | category | flops | bytes accessed | tf_op | source)
XLA Modules:
  0.0 80.3 jit_solution(11248552192699413775)
XLA Ops:
  0.0 0.0 copy-start.2
  0.0 1.4 %copy.7 = bf16[128,2048]{0,1:T(8,128)(2,1)S(1)} copy(bf16[128,2048]{1,0:T(8,128)(2,1)} %param.5) | data formatting | bytes 1048576 | tf_op args[1]
  1.4 1.0 %copy.8 = bf16[128,16,128]{2,0,1:T(8,128)(2,1)} copy(bf16[128,16,128]{0,2,1:T(8,128)(2,1)S(1)} %bitcast.11) | data formatting | bytes 1048576 | tf_op jit(solution)/shard_map/reshape | solution.py:210
  2.4 0.0 copy-start.3
  2.4 6.4 %all-to-all-start.1 = ((bf16[16,128,128]{2,1,0:T(8,128)(2,1)}), bf16[16,128,128]{2,1,0:T(8,128)(2,1)S(1)}, u32[]{:S(2)}, u32[]{:S(2)}) async-start(bf16[16,128,128]{2,1,0:T(8,128)(2,1)} %bitcast.3), calls=%async_computation.1 | async-start | bytes 1048576 | tf_op jit(solution)/shard_map/all_to_all | solution.py:211
  8.8 0.0 copy-done.2
  8.9 0.3 copy.9
  9.1 1.0 %copy.10 = bf16[128,16,128]{2,0,1:T(8,128)(2,1)} copy(bf16[128,16,128]{0,2,1:T(8,128)(2,1)S(1)} %bitcast.12) | data formatting | bytes 1048576 | tf_op jit(solution)/shard_map/reshape | solution.py:210
  10.1 7.7 %all-to-all-done.1.k_ref = bf16[16,128,128]{2,1,0:T(8,128)(2,1)S(1)} async-done(((bf16[16,128,128]{2,1,0:T(8,128)(2,1)}), bf16[16,128,128]{2,1,0:T(8,128)(2,1)S(1)}, u32[]{:S(2)}, u32[]{:S(2)}) %all-to-all-start.1) | async-done | bytes 524320 | tf_op jit(solution)/shard_map/all_to_all | solution.py:211
  17.9 0.0 copy-start
  17.9 3.6 %all-to-all-start.2 = ((bf16[16,128,128]{2,1,0:T(8,128)(2,1)}), bf16[16,128,128]{2,1,0:T(8,128)(2,1)S(1)}, u32[]{:S(2)}, u32[]{:S(2)}) async-start(bf16[16,128,128]{2,1,0:T(8,128)(2,1)} %bitcast.5), calls=%async_computation.2 | async-start | bytes 1048576 | tf_op jit(solution)/shard_map/all_to_all | solution.py:211
  21.5 0.0 copy-done.3
  21.5 0.3 copy.5
  21.8 1.0 %copy.6 = bf16[128,16,128]{2,0,1:T(8,128)(2,1)} copy(bf16[128,16,128]{0,2,1:T(8,128)(2,1)S(1)} %bitcast.13) | data formatting | bytes 1048576 | tf_op jit(solution)/shard_map/reshape | solution.py:210
  22.8 7.7 %all-to-all-done.2.v_ref = bf16[16,128,128]{2,1,0:T(8,128)(2,1)S(1)} async-done(((bf16[16,128,128]{2,1,0:T(8,128)(2,1)}), bf16[16,128,128]{2,1,0:T(8,128)(2,1)S(1)}, u32[]{:S(2)}, u32[]{:S(2)}) %all-to-all-start.2) | async-done | bytes 524320 | tf_op jit(solution)/shard_map/all_to_all | solution.py:211
  30.5 0.0 copy-start.4
  30.5 0.0 copy-done
  30.5 3.6 %all-to-all-start = ((bf16[16,128,128]{2,1,0:T(8,128)(2,1)}), bf16[16,128,128]{2,1,0:T(8,128)(2,1)S(1)}, u32[]{:S(2)}, u32[]{:S(2)}) async-start(bf16[16,128,128]{2,1,0:T(8,128)(2,1)} %bitcast.1), calls=%async_computation | async-start | bytes 1048576 | tf_op jit(solution)/shard_map/all_to_all | solution.py:211
  34.1 9.2 %keys.1 = (bf16[16,128,256]{2,1,0:T(8,128)(2,1)}, bf16[16,128,256]{2,1,0:T(8,128)(2,1)}, bf16[16,128,256]{2,1,0:T(8,128)(2,1)}) custom-call(bf16[16,128,128]{2,1,0:T(8,128)(2,1)} %copy-done), custom_call_target="tpu_custom_call" | custom-call | flops 3758096384 | bytes 4194304 | tf_op jit(solution)/shard_map/keys/pallas_call | solution.py:221
  43.2 0.0 copy-done.4
  43.2 5.8 %values.1 = (bf16[16,128,256]{2,1,0:T(8,128)(2,1)}, bf16[31,128,256]{2,1,0:T(8,128)(2,1)}, f32[31,128,128]{2,1,0:T(8,128)}, f32[128,128]{1,0:T(8,128)}) custom-call(bf16[16,128,128]{2,1,0:T(8,128)(2,1)} %copy-done, bf16[16,128,128]{2,1,0:T(8,128)(2,1)} %copy-done.4, bf16[16,128,256]{2,1,0:T(8,128)(2,1)} %get-tuple-element.15.tu_ref, ...), custom_call_target="tpu_custom_call" | custom-call | flops 1073741824 | bytes 4194304 | tf_op jit(solution)/shard_map/values/pallas_call | solution.py:226
  49.1 4.5 %collective-permute-start = (f32[128,128]{1,0:T(8,128)}, f32[128,128]{1,0:T(8,128)S(1)}, u32[]{:S(2)}, u32[]{:S(2)}) collective-permute-start(f32[128,128]{1,0:T(8,128)} %get-tuple-element.22), channel_id=1, source_target_pairs={{0,16},{1,17},{2,18},{3,19},{4,20},{5,21},{6,22},{7,23},{8,24},{9,... | collective-permute-start | bytes 196616 | tf_op jit(solution)/shard_map/ppermute | solution.py:232
  53.6 0.0 all-to-all-done.q_ref
  53.6 0.0 copy-start.1
  53.6 0.8 copy-done.1
  54.4 7.1 %queries.1 = (bf16[16,128,256]{2,1,0:T(8,128)(2,1)}, f32[16,128,128]{2,1,0:T(8,128)}) custom-call(bf16[16,128,128]{2,1,0:T(8,128)(2,1)} %copy-done.1, bf16[16,128,128]{2,1,0:T(8,128)(2,1)} %copy-done, bf16[16,128,256]{2,1,0:T(8,128)(2,1)} %get-tuple-element.14.w_ref, bf16[16,128,256]{2,1,0:T(8,128)(2,1)} %get-tuple-element.17.u_ref, ...), custom_call_target="tpu_custom_call" | custom-call | flops 1610612736 | bytes 4194304 | tf_op jit(solution)/shard_map/queries/pallas_call | solution.py:242
  61.4 0.0 collective-permute-done.state_ref
  61.4 0.0 copy-start.5
  61.4 0.6 copy-done.5
  62.0 2.9 %finish.1 = bf16[16,128,128]{2,1,0:T(8,128)(2,1)} custom-call(bf16[16,128,256]{2,1,0:T(8,128)(2,1)} %get-tuple-element.20.qp_ref, f32[16,128,128]{2,1,0:T(8,128)} %get-tuple-element.21.op_ref, f32[128,128]{1,0:T(8,128)} %copy-done.5, f32[1,128]{1,0:T(1,128)} %bitcast.14), custom_call_target="tpu_custom_call" | custom-call | flops 268435456 | bytes 4194304 | tf_op jit(solution)/shard_map/finish/pallas_call | solution.py:248
  64.9 14.1 %all_to_all.20 = bf16[16,128,128]{2,1,0:T(8,128)(2,1)S(1)} all-to-all(bf16[16,128,128]{2,1,0:T(8,128)(2,1)} %finish.1), channel_id=1, replica_groups=mesh['seq'=16,'grp'=2] {'seq':(2)8,'grp'}, dimensions={0} | all-to-all | bytes 1048576 | tf_op jit(solution)/shard_map/all_to_all | solution.py:251
  79.0 0.3 copy.11
  79.3 1.0 %copy.12 = bf16[128,2048]{1,0:T(8,128)(2,1)} copy(bf16[128,2048]{0,1:T(8,128)(2,1)S(1)} %bitcast.10) | data formatting | bytes 1048576 | tf_op jit(solution)/shard_map/reshape | solution.py:252
Async XLA Ops:
  0.0 8.8 %copy-start.2 = (bf16[128,2048]{1,0:T(8,128)(2,1)S(1)}, bf16[128,2048]{1,0:T(8,128)(2,1)}, u32[]{:S(2)}) copy-start(bf16[128,2048]{1,0:T(8,128)(2,1)} %param.6) | copy-start | bytes 1572868
  2.4 19.1 %copy-start.3 = (bf16[128,2048]{1,0:T(8,128)(2,1)S(1)}, bf16[128,2048]{1,0:T(8,128)(2,1)}, u32[]{:S(2)}) copy-start(bf16[128,2048]{1,0:T(8,128)(2,1)} %param.4) | copy-start | bytes 1572868
  2.4 15.5 %all-to-all-start.1 = ((bf16[16,128,128]{2,1,0:T(8,128)(2,1)}), bf16[16,128,128]{2,1,0:T(8,128)(2,1)S(1)}, u32[]{:S(2)}, u32[]{:S(2)}) async-start(bf16[16,128,128]{2,1,0:T(8,128)(2,1)} %bitcast.3), calls=%async_computation.1 | async-start | bytes 1048576 | tf_op jit(solution)/shard_map/all_to_all | solution.py:211
  17.9 12.6 %copy-start = (bf16[16,128,128]{2,1,0:T(8,128)(2,1)}, bf16[16,128,128]{2,1,0:T(8,128)(2,1)S(1)}, u32[]{:S(2)}) copy-start(bf16[16,128,128]{2,1,0:T(8,128)(2,1)S(1)} %all-to-all-done.1.k_ref) | copy-start | bytes 1572868
  17.9 12.6 %all-to-all-start.2 = ((bf16[16,128,128]{2,1,0:T(8,128)(2,1)}), bf16[16,128,128]{2,1,0:T(8,128)(2,1)S(1)}, u32[]{:S(2)}, u32[]{:S(2)}) async-start(bf16[16,128,128]{2,1,0:T(8,128)(2,1)} %bitcast.5), calls=%async_computation.2 | async-start | bytes 1048576 | tf_op jit(solution)/shard_map/all_to_all | solution.py:211
  30.5 12.8 %copy-start.4 = (bf16[16,128,128]{2,1,0:T(8,128)(2,1)}, bf16[16,128,128]{2,1,0:T(8,128)(2,1)S(1)}, u32[]{:S(2)}) copy-start(bf16[16,128,128]{2,1,0:T(8,128)(2,1)S(1)} %all-to-all-done.2.v_ref) | copy-start | bytes 1572868
  30.5 23.1 %all-to-all-start = ((bf16[16,128,128]{2,1,0:T(8,128)(2,1)}), bf16[16,128,128]{2,1,0:T(8,128)(2,1)S(1)}, u32[]{:S(2)}, u32[]{:S(2)}) async-start(bf16[16,128,128]{2,1,0:T(8,128)(2,1)} %bitcast.1), calls=%async_computation | async-start | bytes 1048576 | tf_op jit(solution)/shard_map/all_to_all | solution.py:211
  49.1 12.4 %collective-permute-start = (f32[128,128]{1,0:T(8,128)}, f32[128,128]{1,0:T(8,128)S(1)}, u32[]{:S(2)}, u32[]{:S(2)}) collective-permute-start(f32[128,128]{1,0:T(8,128)} %get-tuple-element.22), channel_id=1, source_target_pairs={{0,16},{1,17},{2,18},{3,19},{4,20},{5,21},{6,22},{7,23},{8,24},{9,... | collective-permute-start | bytes 196616 | tf_op jit(solution)/shard_map/ppermute | solution.py:232
  53.6 0.8 copy-start.1
  61.4 0.6 copy-start.5

commit v2 on v1

v2 whole, which is shorter than its diff:
```python
import functools

import jax
import jax.numpy as jnp
from jax import lax
from jax.experimental import pallas as pl
from jax.experimental.pallas import tpu as pltpu
from jax.sharding import Mesh
from jax.sharding import PartitionSpec as P

HEAD_DIM = 128
BLOCK = 128
key_eps = 1e-06
norm_eps = 1e-05
BATCH = 8

f32 = jnp.float32
bf16 = jnp.bfloat16


def mm(left, right):
    return jnp.dot(left, right, preferred_element_type=f32)


def mm_nt(left, right):
    return lax.dot_general(left, right, (((1,), (1,)), ((), ())), preferred_element_type=f32)


def split(value):
    high = value.astype(bf16)
    low = (value - high.astype(f32)).astype(bf16)
    return jnp.concatenate([high, low], axis=1)


def twice(rows):
    return jnp.concatenate([rows, rows], axis=0)


def fold(wide):
    half = wide.shape[1] // 2
    return wide[:, :half] + wide[:, half:]


def product(left_pair, right_pair):
    return fold(mm(left_pair, twice(right_pair)))


def product_wide(left_pair, first_pair, second_pair):
    n = HEAD_DIM
    highs = jnp.concatenate([first_pair[:, :n], second_pair[:, :n]], axis=1)
    lows = jnp.concatenate([first_pair[:, n:], second_pair[:, n:]], axis=1)
    return mm(left_pair, twice(highs)) + mm(left_pair[:, :n], lows)


def iotas():
    row = lax.broadcasted_iota(jnp.int32, (BLOCK, BLOCK), 0)
    col = lax.broadcasted_iota(jnp.int32, (BLOCK, BLOCK), 1)
    return row, col


def batches(count, run):
    size = min(BATCH, count)
    if count == size:
        run([j for j in range(count)])
    else:
        def one(i, carried):
            run([i * size + j for j in range(size)])
            return carried
        lax.fori_loop(0, count // size, one, 0)


def node_offsets(count):
    offsets, at, size = [], 0, count
    while size >= 1:
        offsets.append(at)
        at += size
        size //= 2
    return offsets, at


def pack_kernel(*refs):
    *ins, out_ref = refs
    for i, ref in enumerate(ins):
        for h in range(out_ref.shape[0]):
            out_ref[h, i] = ref[:, h * HEAD_DIM : (h + 1) * HEAD_DIM]


def unpack_kernel(in_ref, out_ref):
    for h in range(in_ref.shape[0]):
        out_ref[:, h * HEAD_DIM : (h + 1) * HEAD_DIM] = in_ref[h]


def keys_kernel(k_ref, w_ref, tu_ref, a_ref, pa_ref):
    count = k_ref.shape[0]
    offsets, _ = node_offsets(count)
    row, col = iotas()
    diagonal = row == col
    eye = diagonal.astype(f32)

    def run(blocks):
        keys = [k_ref[j, 0] for j in blocks]
        grams = [mm_nt(k, k) for k in keys]
        coupling, scale_cols, scale_rows = [], [], []
        for g in grams:
            on_diagonal = jnp.where(diagonal, g, 0.0)
            c = 1.0 / jnp.sqrt(jnp.sum(on_diagonal, axis=1, keepdims=True) + key_eps)
            r = 1.0 / jnp.sqrt(jnp.sum(on_diagonal, axis=0, keepdims=True) + key_eps)
            scale_cols.append(c)
            scale_rows.append(r)
            coupling.append(jnp.where(row > col, (2.0 * c) * g * r, 0.0))
        size = 1
        inverses = None
        while size < BLOCK:
            mask = ((row // size) % 2 == 1) & (col // size == row // size - 1)
            parts = [jnp.where(mask, n, 0.0) for n in coupling]
            if inverses is None:
                inverses = [eye - p for p in parts]
            else:
                pairs = [split(t) for t in inverses]
                inner = [product(split(p), t) for p, t in zip(parts, pairs)]
                outer = [product(t, split(z)) for t, z in zip(pairs, inner)]
                inverses = [t - z for t, z in zip(inverses, outer)]
            size *= 2
        for i, j in enumerate(blocks):
            left = (2.0 * scale_cols[i]) * inverses[i]
            tu_ref[j] = split(left)
            weights = split(mm(split(left * scale_rows[i]), twice(keys[i])))
            w_ref[j] = weights
            a_ref[j] = split(eye - fold(mm(keys[i].T, weights)))

    batches(count, run)
    for level in range(1, len(offsets)):
        below, here = offsets[level - 1], offsets[level]
        for i in range(count >> level):
            a_ref[here + i] = split(product(a_ref[below + 2 * i + 1], a_ref[below + 2 * i]))
    for (target, left, parent) in prefix_steps(count):
        if parent is None:
            pa_ref[target] = split(eye) if left is None else a_ref[left]
        elif left is None:
            pa_ref[target] = pa_ref[parent]
        else:
            pa_ref[target] = split(product(a_ref[left], pa_ref[parent]))


def prefix_steps(count):
    offsets, _ = node_offsets(count)
    steps = []
    for level in range(len(offsets) - 2, -1, -1):
        here, above = offsets[level], offsets[level + 1]
        for i in range(count >> (level + 1)):
            parent = above + i if i > 0 else None
            if i > 0 or level == 0:
                steps.append((here + 2 * i, None, parent))
            steps.append((here + 2 * i + 1, here + 2 * i, parent))
    return steps


def values_kernel(k_ref, vq_ref, tu_ref, a_ref, u_ref, b_ref, total_ref):
    count = k_ref.shape[0]
    offsets, _ = node_offsets(count)

    def run(blocks):
        changes = [split(mm(tu_ref[j], twice(vq_ref[j, 0]))) for j in blocks]
        for i, j in enumerate(blocks):
            u_ref[j] = changes[i]
            b_ref[j] = fold(mm(k_ref[j, 0].T, changes[i]))

    batches(count, run)
    for level in range(1, len(offsets)):
        below, here = offsets[level - 1], offsets[level]
        for i in range(count >> level):
            first, second = below + 2 * i, below + 2 * i + 1
            b_ref[here + i] = product(a_ref[second], split(b_ref[first])) + b_ref[second]
    total_ref[...] = b_ref[offsets[-1]]


def queries_kernel(k_ref, vq_ref, w_ref, u_ref, a_ref, b_ref, qt_ref, ol_ref, pb_ref):
    count = k_ref.shape[0]
    row, col = iotas()
    causal = row >= col

    def run(blocks):
        scores = [jnp.where(causal, mm_nt(vq_ref[j, 1], k_ref[j, 0]), 0.0) for j in blocks]
        local = [product_wide(split(c), w_ref[j], u_ref[j]) for c, j in zip(scores, blocks)]
        for i, j in enumerate(blocks):
            qt_ref[j] = split(vq_ref[j, 1].astype(f32) - local[i][:, :HEAD_DIM])
            ol_ref[j] = local[i][:, HEAD_DIM:]

    batches(count, run)
    for (target, left, parent) in prefix_steps(count):
        if parent is None:
            pb_ref[target] = jnp.zeros((HEAD_DIM, HEAD_DIM), f32) if left is None else b_ref[left]
        elif left is None:
            pb_ref[target] = pb_ref[parent]
        else:
            pb_ref[target] = product(a_ref[left], split(pb_ref[parent])) + b_ref[left]


def finish_kernel(qt_ref, ol_ref, pa_ref, pb_ref, state_ref, gain_ref, out_ref):
    arrived = jnp.where(lax.axis_index("hi") > 0, state_ref[...], 0.0)
    state = twice(split(arrived))
    gain = gain_ref[...]

    def run(blocks):
        starts = [fold(mm(pa_ref[j], state)) + pb_ref[j] for j in blocks]
        outputs = [product(qt_ref[j], split(s)) + ol_ref[j] for j, s in zip(blocks, starts)]
        for j, output in zip(blocks, outputs):
            scale = lax.rsqrt(jnp.mean(output * output, axis=1, keepdims=True) + norm_eps)
            out_ref[j] = (output * scale * gain).astype(bf16)

    batches(out_ref.shape[0], run)


def call(kernel, name, outs, flops, kept=True, limit=24 << 20):
    vmem = pl.BlockSpec(memory_space=pltpu.VMEM)
    make = pltpu.VMEM if kept else jax.ShapeDtypeStruct
    return pl.pallas_call(
        kernel,
        name=name,
        out_shape=tuple(make(s, t) for s, t in outs),
        out_specs=tuple(vmem for _ in outs),
        compiler_params=pltpu.CompilerParams(vmem_limit_bytes=limit),
        cost_estimate=pl.CostEstimate(flops=flops, bytes_accessed=4 << 20, transcendentals=0),
    )


def near(*values):
    return [pltpu.with_memory_space_constraint(v, pltpu.VMEM) for v in values]


def body(groups, lanes, queries, key_vectors, head_value_rows, out_gain):
    tokens, features = queries.shape
    if tokens != BLOCK or features != lanes * HEAD_DIM:
        raise ValueError("unsupported sizes")
    blocks = lanes

    def to_heads(*rows):
        shape = (lanes, len(rows), BLOCK, HEAD_DIM)
        (pieces,) = call(pack_kernel, "pack", [(shape, bf16)], 0, kept=False)(*rows)
        return lax.all_to_all(pieces, "lo", split_axis=0, concat_axis=0, tiled=True)

    keys = to_heads(key_vectors)
    vq = to_heads(head_value_rows, queries)
    _, nodes = node_offsets(blocks)
    one = (HEAD_DIM, HEAD_DIM)
    pair = (HEAD_DIM, 2 * HEAD_DIM)
    unit = 2 * BLOCK**3 * 4
    w, tu, a, pa = call(
        keys_kernel, "keys",
        [((blocks, *pair), bf16), ((blocks, *pair), bf16), ((nodes, *pair), bf16), ((nodes, *pair), bf16)],
        unit * blocks * 20,
    )(keys)
    u, b, total = call(
        values_kernel, "values",
        [((blocks, *pair), bf16), ((nodes, *one), f32), (one, f32)],
        unit * blocks * 4,
    )(keys, vq, *near(tu, a))
    hop = [(source, (source + 1) % groups) for source in range(groups)]
    incoming = lax.ppermute(total, "hi", hop)
    if groups > 2:
        top = a[nodes - 1].astype(f32)
        transition = top[:, :HEAD_DIM] + top[:, HEAD_DIM:]

        def relay(i, arriving):
            arriving = jnp.where(lax.axis_index("hi") > 0, arriving, 0.0)
            leaving = jnp.dot(transition, arriving, precision=lax.Precision.HIGHEST) + total
            return lax.ppermute(leaving, "hi", hop)

        incoming = lax.fori_loop(0, groups - 2, relay, incoming)
    qt, ol, pb = call(
        queries_kernel, "queries",
        [((blocks, *pair), bf16), ((blocks, *one), f32), ((nodes, *one), f32)],
        unit * blocks * 6,
    )(keys, vq, *near(w, u, a, b))
    (out,) = call(
        finish_kernel, "finish", [((blocks, BLOCK, HEAD_DIM), bf16)], unit * blocks * 2, kept=False,
    )(*near(qt, ol, pa, pb), incoming, out_gain.reshape(1, HEAD_DIM))
    back = lax.all_to_all(out, "lo", split_axis=0, concat_axis=0, tiled=True)
    (mixed,) = call(unpack_kernel, "unpack", [((tokens, features), bf16)], 0, kept=False)(back)
    return mixed


def solution(mesh):
    count = mesh.devices.size

    def run(queries, key_vectors, head_value_rows, out_gain):
        lanes = queries.shape[1] // HEAD_DIM
        regrouped = Mesh(mesh.devices.reshape(count // lanes, lanes), ("hi", "lo"))
        rows = P(("hi", "lo"), None)
        return jax.shard_map(
            functools.partial(body, count // lanes, lanes),
            mesh=regrouped, in_specs=(rows, rows, rows, P()), out_specs=rows, check_vma=False,
        )(queries, key_vectors, head_value_rows, out_gain)

    return run
```

time: 81 us -> 61.9 us (0.76)
  Pallas kernels: 24.9 us -> 15.5 us
  starting transfers between devices: 18.1 us -> 12.6 us
  waiting for transfers between devices: 15.5 us -> 11.8 us
  blocking collectives: 14.1 us -> 12.9 us
  local copies, waits for them, and re-layouts: 7.65 us -> 8.46 us
    pallas_call x1, Pallas kernels: 7.05 us -> 1.76 us  [body(): call(queries_kernel, 'queries', [((blocks, *pair), bf16), ((blocks, *one)...]
    all_to_all x3 -> x2, waiting for transfers between devices: 15.5 us -> 10.2 us  [to_heads(): return lax.all_to_all(pieces, 'lo', split_axis=0, concat_axis=0, tiled=True)]
    unnamed x15 -> x26, local copies, waits for them, and re-layouts: 3.32 us -> 8.46 us
    reshape x4 -> x0, local copies, waits for them, and re-layouts: 4.05 us -> none  [the longest x3 3.04 us: to_heads(): pieces = rows.reshape(tokens, heads, HEAD_DIM).transpose(1, 0, 2)]
    all_to_all x3 -> x2, starting transfers between devices: 13.6 us -> 9.97 us  [to_heads(): return lax.all_to_all(pieces, 'lo', split_axis=0, concat_axis=0, tiled=True)]
    ppermute x1, starting transfers between devices: 4.49 us -> 2.65 us  [body(): incoming = lax.ppermute(total, 'hi', hop)]
    pallas_call x1, Pallas kernels: 2.89 us -> 1.23 us  [body(): call(finish_kernel, 'finish', [((blocks, BLOCK, HEAD_DIM), bf16)], unit *...]
    ppermute x1, waiting for transfers between devices: 0.01 us -> 1.58 us  [body(): incoming = lax.ppermute(total, 'hi', hop)]
  transfers between devices with their start and end apart: 4 -> 3, of which waited for: 2 -> 3; matrix products, arithmetic and copies ran while one was open for 3% -> 0% of each run, Pallas kernels for 27% -> 18%
where the time goes in v2:
time: 61.9 us; the launch traced here: 61.4 us
  Pallas kernels  15.5 us (25%)
  blocking collectives  12.9 us (21%)
  starting transfers between devices  12.6 us (20%)
  waiting for transfers between devices  11.8 us (19%)
  local copies, waits for them, and re-layouts  8.46 us (14%)
    all_to_all x1, blocking collectives, body(): back = lax.all_to_all(out, 'lo', split_axis=0, concat_axis=0, tiled=True)  12.9 us
    all_to_all x2, waiting for transfers between devices, to_heads(): return lax.all_to_all(pieces, 'lo', split_axis=0, concat_axis=0, tiled=True)  10.2 us
    all_to_all x2, starting transfers between devices, to_heads(): return lax.all_to_all(pieces, 'lo', split_axis=0, concat_axis=0, tiled=True)  9.97 us
    unnamed x26, local copies, waits for them, and re-layouts  8.46 us
    pallas_call x1, Pallas kernels, body(): call(keys_kernel, 'keys', [((blocks, *pair), bf16), ((blocks, *pair), bf1...  7.92 us
    ppermute x1, starting transfers between devices, body(): incoming = lax.ppermute(total, 'hi', hop)  2.65 us
    pallas_call x2, Pallas kernels, to_heads(): pieces, = call(pack_kernel, 'pack', [(shape, bf16)], 0, kept=False)(*rows)  2.03 us
    pallas_call x1, Pallas kernels, body(): call(queries_kernel, 'queries', [((blocks, *pair), bf16), ((blocks, *one)...  1.76 us
  transfers between devices with their start and end apart: 3, of which 3 were waited for; matrix products, arithmetic and copies ran while one was open for 0% of the time, Pallas kernels for 18%

profile of v2, /device:TPU:0, one launch (start us, length us, event | category | flops | bytes accessed | tf_op | source)
XLA Modules:
  0.0 61.4 jit_solution(3989662399213414806)
XLA Ops:
  0.0 0.0 copy-start.9
  0.0 1.0 %copy-done.9 = bf16[128,2048]{1,0:T(8,128)(2,1)S(1)} copy-done((bf16[128,2048]{1,0:T(8,128)(2,1)S(1)}, bf16[128,2048]{1,0:T(8,128)(2,1)}, u32[]{:S(2)}) %copy-start.9) | copy-done | bytes 524312
  1.0 0.0 copy-start.10
  1.0 0.0 copy-start.11
  1.0 0.9 %pack.2 = bf16[16,1,128,128]{3,2,1,0:T(8,128)(2,1)} custom-call(bf16[128,2048]{1,0:T(8,128)(2,1)S(1)} %copy-done.9), custom_call_target="tpu_custom_call" | custom-call | bytes 4194304 | tf_op jit(solution)/shard_map/pack/pallas_call | solution.py:239
  1.9 6.3 %all-to-all-start = ((bf16[16,1,128,128]{3,2,1,0:T(8,128)(2,1)}), bf16[16,1,128,128]{3,2,1,0:T(8,128)(2,1)S(1)}, u32[]{:S(2)}, u32[]{:S(2)}) async-start(bf16[16,1,128,128]{3,2,1,0:T(8,128)(2,1)} %pack.2), calls=%async_computation | async-start | bytes 1048576 | tf_op jit(solution)/shard_map/all_to_all | solution.py:240
  8.3 0.0 copy-done.10
  8.3 0.0 copy-done.11
  8.3 1.1 %pack.3 = bf16[16,2,128,128]{3,2,1,0:T(8,128)(2,1)} custom-call(bf16[128,2048]{1,0:T(8,128)(2,1)S(1)} %copy-done.10, bf16[128,2048]{1,0:T(8,128)(2,1)S(1)} %copy-done.11), custom_call_target="tpu_custom_call" | custom-call | bytes 4194304 | tf_op jit(solution)/shard_map/pack/pallas_call | solution.py:239
  9.4 7.9 %all-to-all-done.k_ref = bf16[16,1,128,128]{3,2,1,0:T(8,128)(2,1)S(1)} async-done(((bf16[16,1,128,128]{3,2,1,0:T(8,128)(2,1)}), bf16[16,1,128,128]{3,2,1,0:T(8,128)(2,1)S(1)}, u32[]{:S(2)}, u32[]{:S(2)}) %all-to-all-start) | async-done | bytes 524320 | tf_op jit(solution)/shard_map/all_to_all | solution.py:240
  17.3 0.0 copy-start
  17.3 0.8 %copy-done = bf16[16,1,128,128]{3,2,1,0:T(8,128)(2,1)} copy-done((bf16[16,1,128,128]{3,2,1,0:T(8,128)(2,1)}, bf16[16,1,128,128]{3,2,1,0:T(8,128)(2,1)S(1)}, u32[]{:S(2)}) %copy-start) | copy-done | bytes 524312
  18.1 3.7 %all-to-all-start.1 = ((bf16[16,2,128,128]{3,2,1,0:T(8,128)(2,1)}), bf16[16,2,128,128]{3,2,1,0:T(8,128)(2,1)S(1)}, u32[]{:S(2)}, u32[]{:S(2)}) async-start(bf16[16,2,128,128]{3,2,1,0:T(8,128)(2,1)} %pack.3), calls=%async_computation.1 | async-start | bytes 2097152 | tf_op jit(solution)/shard_map/all_to_all | solution.py:240
  21.7 0.0 copy-start.1
  21.8 1.0 %copy-done.1 = bf16[16,1,128,128]{3,2,1,0:T(8,128)(2,1)S(1)} copy-done((bf16[16,1,128,128]{3,2,1,0:T(8,128)(2,1)S(1)}, bf16[16,1,128,128]{3,2,1,0:T(8,128)(2,1)}, u32[]{:S(2)}) %copy-start.1) | copy-done | bytes 524312
  22.8 7.9 %keys.1 = (bf16[16,128,256]{2,1,0:T(8,128)(2,1)S(1)}, bf16[16,128,256]{2,1,0:T(8,128)(2,1)S(1)}, bf16[31,128,256]{2,1,0:T(8,128)(2,1)S(1)}, bf16[31,128,256]{2,1,0:T(8,128)(2,1)S(1)}) custom-call(bf16[16,1,128,128]{3,2,1,0:T(8,128)(2,1)S(1)} %copy-done.1), custom_call_target="tpu_custom_call" | custom-call | flops 5368709120 | bytes 4194304 | tf_op jit(solution)/shard_map/keys/pallas_call | solution.py:248
  30.7 0.0 copy-start.3
  30.7 1.3 %copy-done.3 = bf16[31,128,256]{2,1,0:T(8,128)(2,1)} copy-done((bf16[31,128,256]{2,1,0:T(8,128)(2,1)}, bf16[31,128,256]{2,1,0:T(8,128)(2,1)S(1)}, u32[]{:S(2)}) %copy-start.3) | copy-done | bytes 2031640
  32.0 0.0 copy-start.5
  32.0 1.0 %copy-done.5 = bf16[16,128,256]{2,1,0:T(8,128)(2,1)} copy-done((bf16[16,128,256]{2,1,0:T(8,128)(2,1)}, bf16[16,128,256]{2,1,0:T(8,128)(2,1)S(1)}, u32[]{:S(2)}) %copy-start.5) | copy-done | bytes 1048600
  33.0 0.0 copy-start.7
  33.0 1.0 %copy-done.7 = bf16[16,128,256]{2,1,0:T(8,128)(2,1)} copy-done((bf16[16,128,256]{2,1,0:T(8,128)(2,1)}, bf16[16,128,256]{2,1,0:T(8,128)(2,1)S(1)}, u32[]{:S(2)}) %copy-start.7) | copy-done | bytes 1048600
  34.0 2.4 %all-to-all-done.1.vq_ref = bf16[16,2,128,128]{3,2,1,0:T(8,128)(2,1)S(1)} async-done(((bf16[16,2,128,128]{3,2,1,0:T(8,128)(2,1)}), bf16[16,2,128,128]{3,2,1,0:T(8,128)(2,1)S(1)}, u32[]{:S(2)}, u32[]{:S(2)}) %all-to-all-start.1) | async-done | bytes 1048608 | tf_op jit(solution)/shard_map/all_to_all | solution.py:240
  36.4 0.0 copy-start.2
  36.4 1.0 %copy-done.2 = bf16[16,1,128,128]{3,2,1,0:T(8,128)(2,1)S(1)} copy-done((bf16[16,1,128,128]{3,2,1,0:T(8,128)(2,1)S(1)}, bf16[16,1,128,128]{3,2,1,0:T(8,128)(2,1)}, u32[]{:S(2)}) %copy-start.2) | copy-done | bytes 524312
  37.4 0.0 copy-start.6
  37.4 1.2 %copy-done.6 = bf16[16,128,256]{2,1,0:T(8,128)(2,1)S(1)} copy-done((bf16[16,128,256]{2,1,0:T(8,128)(2,1)S(1)}, bf16[16,128,256]{2,1,0:T(8,128)(2,1)}, u32[]{:S(2)}) %copy-start.6) | copy-done | bytes 1048600
  38.6 0.0 copy-start.8
  38.6 1.6 %values.1 = (bf16[16,128,256]{2,1,0:T(8,128)(2,1)S(1)}, f32[31,128,128]{2,1,0:T(8,128)S(1)}, f32[128,128]{1,0:T(8,128)S(1)}) custom-call(bf16[16,1,128,128]{3,2,1,0:T(8,128)(2,1)S(1)} %copy-done.2, bf16[16,2,128,128]{3,2,1,0:T(8,128)(2,1)S(1)} %all-to-all-done.1.vq_ref, bf16[16,128,256]{2,1,0:T(8,128)(2,1)S(1)} %copy-done.6, ...), custom_call_target="tpu_custom_call" | custom-call | flops 1073741824 | bytes 4194304 | tf_op jit(solution)/shard_map/values/pallas_call | solution.py:253
  40.3 2.7 %collective-permute-start = (f32[128,128]{1,0:T(8,128)S(1)}, f32[128,128]{1,0:T(8,128)S(1)}, u32[]{:S(2)}, u32[]{:S(2)}) collective-permute-start(f32[128,128]{1,0:T(8,128)S(1)} %get-tuple-element.24), channel_id=1, source_target_pairs={{0,16},{16,0},{1,17},{17,1},{2,18},{18,2},{3,19},{19,3},{4,20},{20... | collective-permute-start | bytes 196616 | tf_op jit(solution)/shard_map/ppermute | solution.py:259
  42.9 0.0 copy-done.8
  42.9 0.0 copy-start.4
  42.9 0.0 copy-start.12
  42.9 1.8 %queries.1 = (bf16[16,128,256]{2,1,0:T(8,128)(2,1)S(1)}, f32[16,128,128]{2,1,0:T(8,128)S(1)}, f32[31,128,128]{2,1,0:T(8,128)S(1)}) custom-call(bf16[16,1,128,128]{3,2,1,0:T(8,128)(2,1)S(1)} %copy-done.2, bf16[16,2,128,128]{3,2,1,0:T(8,128)(2,1)S(1)} %all-to-all-done.1.vq_ref, bf16[16,128,256]{2,1,0:T(8,128)(2,1)S(1)} %copy-done.8, ...), custom_call_target="tpu_custom_call" | custom-call | flops 1610612736 | bytes 4194304 | tf_op jit(solution)/shard_map/queries/pallas_call | solution.py:270
  44.7 1.6 %collective-permute-done.state_ref = f32[128,128]{1,0:T(8,128)S(1)} collective-permute-done((f32[128,128]{1,0:T(8,128)S(1)}, f32[128,128]{1,0:T(8,128)S(1)}, u32[]{:S(2)}, u32[]{:S(2)}) %collective-permute-start) | collective-permute-done | bytes 65568 | tf_op jit(solution)/shard_map/ppermute | solution.py:259
  46.3 0.0 copy-done.4
  46.3 0.0 copy-done.12
  46.3 1.2 %finish.1 = bf16[16,128,128]{2,1,0:T(8,128)(2,1)S(1)} custom-call(bf16[16,128,256]{2,1,0:T(8,128)(2,1)S(1)} %get-tuple-element.20.qt_ref, f32[16,128,128]{2,1,0:T(8,128)S(1)} %get-tuple-element.21.ol_ref, bf16[31,128,256]{2,1,0:T(8,128)(2,1)S(1)} %copy-done.4, f32[31,128,128]{2,1,0:T(8,128)S(1)} %get-tuple-element.23.pb_ref, ...), custom_call_target="tpu_custom_call" | custom-call | flops 536870912 | bytes 4194304 | tf_op jit(solution)/shard_map/finish/pallas_call | solution.py:275
  47.5 12.9 %all_to_all.15.in_ref = bf16[16,128,128]{2,1,0:T(8,128)(2,1)S(1)} all-to-all(bf16[16,128,128]{2,1,0:T(8,128)(2,1)S(1)} %finish.1), channel_id=1, replica_groups=mesh['seq'=16,'grp'=2] {'seq':(2)8,'grp'}, dimensions={0} | all-to-all | bytes 1048576 | tf_op jit(solution)/shard_map/all_to_all | solution.py:278
  60.4 0.9 %unpack.1 = bf16[128,2048]{1,0:T(8,128)(2,1)} custom-call(bf16[16,128,128]{2,1,0:T(8,128)(2,1)S(1)} %all_to_all.15.in_ref), custom_call_target="tpu_custom_call" | custom-call | bytes 4194304 | tf_op jit(solution)/shard_map/unpack/pallas_call | solution.py:279
Async XLA Ops:
  0.0 1.0 %copy-start.9 = (bf16[128,2048]{1,0:T(8,128)(2,1)S(1)}, bf16[128,2048]{1,0:T(8,128)(2,1)}, u32[]{:S(2)}) copy-start(bf16[128,2048]{1,0:T(8,128)(2,1)} %refs_0_.2) | copy-start | bytes 1572868
  1.0 7.2 %copy-start.10 = (bf16[128,2048]{1,0:T(8,128)(2,1)S(1)}, bf16[128,2048]{1,0:T(8,128)(2,1)}, u32[]{:S(2)}) copy-start(bf16[128,2048]{1,0:T(8,128)(2,1)} %refs_0_.3) | copy-start | bytes 1572868
  1.0 7.2 %copy-start.11 = (bf16[128,2048]{1,0:T(8,128)(2,1)S(1)}, bf16[128,2048]{1,0:T(8,128)(2,1)}, u32[]{:S(2)}) copy-start(bf16[128,2048]{1,0:T(8,128)(2,1)} %refs_1_.1) | copy-start | bytes 1572868
  1.9 15.4 %all-to-all-start = ((bf16[16,1,128,128]{3,2,1,0:T(8,128)(2,1)}), bf16[16,1,128,128]{3,2,1,0:T(8,128)(2,1)S(1)}, u32[]{:S(2)}, u32[]{:S(2)}) async-start(bf16[16,1,128,128]{3,2,1,0:T(8,128)(2,1)} %pack.2), calls=%async_computation | async-start | bytes 1048576 | tf_op jit(solution)/shard_map/all_to_all | solution.py:240
  17.3 0.8 %copy-start = (bf16[16,1,128,128]{3,2,1,0:T(8,128)(2,1)}, bf16[16,1,128,128]{3,2,1,0:T(8,128)(2,1)S(1)}, u32[]{:S(2)}) copy-start(bf16[16,1,128,128]{3,2,1,0:T(8,128)(2,1)S(1)} %all-to-all-done.k_ref) | copy-start | bytes 1572868
  18.1 18.3 %all-to-all-start.1 = ((bf16[16,2,128,128]{3,2,1,0:T(8,128)(2,1)}), bf16[16,2,128,128]{3,2,1,0:T(8,128)(2,1)S(1)}, u32[]{:S(2)}, u32[]{:S(2)}) async-start(bf16[16,2,128,128]{3,2,1,0:T(8,128)(2,1)} %pack.3), calls=%async_computation.1 | async-start | bytes 2097152 | tf_op jit(solution)/shard_map/all_to_all | solution.py:240
  21.7 1.0 %copy-start.1 = (bf16[16,1,128,128]{3,2,1,0:T(8,128)(2,1)S(1)}, bf16[16,1,128,128]{3,2,1,0:T(8,128)(2,1)}, u32[]{:S(2)}) copy-start(bf16[16,1,128,128]{3,2,1,0:T(8,128)(2,1)} %copy-done) | copy-start | bytes 1572868
  30.7 1.3 %copy-start.3 = (bf16[31,128,256]{2,1,0:T(8,128)(2,1)}, bf16[31,128,256]{2,1,0:T(8,128)(2,1)S(1)}, u32[]{:S(2)}) copy-start(bf16[31,128,256]{2,1,0:T(8,128)(2,1)S(1)} %get-tuple-element.22.pa_ref) | copy-start | bytes 6094852
  32.0 1.0 %copy-start.5 = (bf16[16,128,256]{2,1,0:T(8,128)(2,1)}, bf16[16,128,256]{2,1,0:T(8,128)(2,1)S(1)}, u32[]{:S(2)}) copy-start(bf16[16,128,256]{2,1,0:T(8,128)(2,1)S(1)} %get-tuple-element.16.tu_ref) | copy-start | bytes 3145732
  33.0 1.0 %copy-start.7 = (bf16[16,128,256]{2,1,0:T(8,128)(2,1)}, bf16[16,128,256]{2,1,0:T(8,128)(2,1)S(1)}, u32[]{:S(2)}) copy-start(bf16[16,128,256]{2,1,0:T(8,128)(2,1)S(1)} %get-tuple-element.15.w_ref) | copy-start | bytes 3145732
  36.4 1.0 %copy-start.2 = (bf16[16,1,128,128]{3,2,1,0:T(8,128)(2,1)S(1)}, bf16[16,1,128,128]{3,2,1,0:T(8,128)(2,1)}, u32[]{:S(2)}) copy-start(bf16[16,1,128,128]{3,2,1,0:T(8,128)(2,1)} %copy-done) | copy-start | bytes 1572868
  37.4 1.2 %copy-start.6 = (bf16[16,128,256]{2,1,0:T(8,128)(2,1)S(1)}, bf16[16,128,256]{2,1,0:T(8,128)(2,1)}, u32[]{:S(2)}) copy-start(bf16[16,128,256]{2,1,0:T(8,128)(2,1)} %copy-done.5) | copy-start | bytes 3145732
  38.6 4.3 %copy-start.8 = (bf16[16,128,256]{2,1,0:T(8,128)(2,1)S(1)}, bf16[16,128,256]{2,1,0:T(8,128)(2,1)}, u32[]{:S(2)}) copy-start(bf16[16,128,256]{2,1,0:T(8,128)(2,1)} %copy-done.7) | copy-start | bytes 3145732
  40.3 6.0 %collective-permute-start = (f32[128,128]{1,0:T(8,128)S(1)}, f32[128,128]{1,0:T(8,128)S(1)}, u32[]{:S(2)}, u32[]{:S(2)}) collective-permute-start(f32[128,128]{1,0:T(8,128)S(1)} %get-tuple-element.24), channel_id=1, source_target_pairs={{0,16},{16,0},{1,17},{17,1},{2,18},{18,2},{3,19},{19,3},{4,20},{20... | collective-permute-start | bytes 196616 | tf_op jit(solution)/shard_map/ppermute | solution.py:259
  42.9 3.3 %copy-start.4 = (bf16[31,128,256]{2,1,0:T(8,128)(2,1)S(1)}, bf16[31,128,256]{2,1,0:T(8,128)(2,1)}, u32[]{:S(2)}) copy-start(bf16[31,128,256]{2,1,0:T(8,128)(2,1)} %copy-done.3) | copy-start | bytes 6094852
  42.9 3.3 %copy-start.12 = (f32[128]{0:T(128)S(1)}, f32[128]{0:T(128)}, u32[]{:S(2)}) copy-start(f32[128]{0:T(128)} %param.7) | copy-start | bytes 1540

commit v3 on v2

--- a/solution.py
+++ b/solution.py
@@ -90,15 +90,15 @@
         out_ref[:, h * HEAD_DIM : (h + 1) * HEAD_DIM] = in_ref[h]
 
 
-def keys_kernel(k_ref, w_ref, tu_ref, a_ref, pa_ref):
-    count = k_ref.shape[0]
+def keys_kernel(kvq_ref, w_ref, tu_ref, a_ref, pa_ref):
+    count = kvq_ref.shape[0]
     offsets, _ = node_offsets(count)
     row, col = iotas()
     diagonal = row == col
     eye = diagonal.astype(f32)
 
     def run(blocks):
-        keys = [k_ref[j, 0] for j in blocks]
+        keys = [kvq_ref[j, 0] for j in blocks]
         grams = [mm_nt(k, k) for k in keys]
         coupling, scale_cols, scale_rows = [], [], []
         for g in grams:
@@ -155,15 +155,15 @@
     return steps
 
 
-def values_kernel(k_ref, vq_ref, tu_ref, a_ref, u_ref, b_ref, total_ref):
-    count = k_ref.shape[0]
+def values_kernel(kvq_ref, tu_ref, a_ref, u_ref, b_ref, total_ref):
+    count = kvq_ref.shape[0]
     offsets, _ = node_offsets(count)
 
     def run(blocks):
-        changes = [split(mm(tu_ref[j], twice(vq_ref[j, 0]))) for j in blocks]
+        changes = [split(mm(tu_ref[j], twice(kvq_ref[j, 1]))) for j in blocks]
         for i, j in enumerate(blocks):
             u_ref[j] = changes[i]
-            b_ref[j] = fold(mm(k_ref[j, 0].T, changes[i]))
+            b_ref[j] = fold(mm(kvq_ref[j, 0].T, changes[i]))
 
     batches(count, run)
     for level in range(1, len(offsets)):
@@ -174,16 +174,16 @@
     total_ref[...] = b_ref[offsets[-1]]
 
 
-def queries_kernel(k_ref, vq_ref, w_ref, u_ref, a_ref, b_ref, qt_ref, ol_ref, pb_ref):
-    count = k_ref.shape[0]
+def queries_kernel(kvq_ref, w_ref, u_ref, a_ref, b_ref, qt_ref, ol_ref, pb_ref):
+    count = kvq_ref.shape[0]
     row, col = iotas()
     causal = row >= col
 
     def run(blocks):
-        scores = [jnp.where(causal, mm_nt(vq_ref[j, 1], k_ref[j, 0]), 0.0) for j in blocks]
+        scores = [jnp.where(causal, mm_nt(kvq_ref[j, 2], kvq_ref[j, 0]), 0.0) for j in blocks]
         local = [product_wide(split(c), w_ref[j], u_ref[j]) for c, j in zip(scores, blocks)]
         for i, j in enumerate(blocks):
-            qt_ref[j] = split(vq_ref[j, 1].astype(f32) - local[i][:, :HEAD_DIM])
+            qt_ref[j] = split(kvq_ref[j, 2].astype(f32) - local[i][:, :HEAD_DIM])
             ol_ref[j] = local[i][:, HEAD_DIM:]
 
     batches(count, run)
@@ -239,8 +239,7 @@
         (pieces,) = call(pack_kernel, "pack", [(shape, bf16)], 0, kept=False)(*rows)
         return lax.all_to_all(pieces, "lo", split_axis=0, concat_axis=0, tiled=True)
 
-    keys = to_heads(key_vectors)
-    vq = to_heads(head_value_rows, queries)
+    kvq = to_heads(key_vectors, head_value_rows, queries)
     _, nodes = node_offsets(blocks)
     one = (HEAD_DIM, HEAD_DIM)
     pair = (HEAD_DIM, 2 * HEAD_DIM)
@@ -249,12 +248,12 @@
         keys_kernel, "keys",
         [((blocks, *pair), bf16), ((blocks, *pair), bf16), ((nodes, *pair), bf16), ((nodes, *pair), bf16)],
         unit * blocks * 20,
-    )(keys)
+    )(*near(kvq))
     u, b, total = call(
         values_kernel, "values",
         [((blocks, *pair), bf16), ((nodes, *one), f32), (one, f32)],
         unit * blocks * 4,
-    )(keys, vq, *near(tu, a))
+    )(*near(kvq, tu, a))
     hop = [(source, (source + 1) % groups) for source in range(groups)]
     incoming = lax.ppermute(total, "hi", hop)
     if groups > 2:
@@ -271,7 +270,7 @@
         queries_kernel, "queries",
         [((blocks, *pair), bf16), ((blocks, *one), f32), ((nodes, *one), f32)],
         unit * blocks * 6,
-    )(keys, vq, *near(w, u, a, b))
+    )(*near(kvq, w, u, a, b))
     (out,) = call(
         finish_kernel, "finish", [((blocks, BLOCK, HEAD_DIM), bf16)], unit * blocks * 2, kept=False,
     )(*near(qt, ol, pa, pb), incoming, out_gain.reshape(1, HEAD_DIM))

time: 61.9 us -> 60.4 us (0.976)
  blocking collectives: 12.9 us -> 38.1 us
  starting transfers between devices: 12.6 us -> 2.65 us
  waiting for transfers between devices: 11.8 us -> 2.4 us
  local copies, waits for them, and re-layouts: 8.46 us -> 3.13 us
  Pallas kernels: 15.5 us -> 13.8 us
    all_to_all x0 -> x1, blocking collectives: none -> 26.5 us  [to_heads(): return lax.all_to_all(pieces, 'lo', split_axis=0, concat_axis=0, tiled=True)]
    all_to_all x2 -> x0, waiting for transfers between devices: 10.2 us -> none  [to_heads(): return lax.all_to_all(pieces, 'lo', split_axis=0, concat_axis=0, tiled=True)]
    all_to_all x2 -> x0, starting transfers between devices: 9.97 us -> none  [to_heads(): return lax.all_to_all(pieces, 'lo', split_axis=0, concat_axis=0, tiled=True)]
    unnamed x26 -> x8, local copies, waits for them, and re-layouts: 8.46 us -> 3.13 us
    pallas_call x2 -> x1, Pallas kernels: 2.03 us -> 0.27 us  [to_heads(): pieces, = call(pack_kernel, 'pack', [(shape, bf16)], 0, kept=False)(*rows)]
    all_to_all x1, blocking collectives: 12.9 us -> 11.7 us  [body(): back = lax.all_to_all(out, 'lo', split_axis=0, concat_axis=0, tiled=True)]
    ppermute x1, waiting for transfers between devices: 1.58 us -> 2.4 us  [body(): incoming = lax.ppermute(total, 'hi', hop)]
  transfers between devices with their start and end apart: 3 -> 1, of which waited for: 3 -> 1; matrix products, arithmetic and copies ran while one was open for 0% -> 0% of each run, Pallas kernels for 18% -> 3%
where the time goes in v3:
time: 60.4 us; the launch traced here: 60.1 us
  blocking collectives  38.1 us (63%)
  Pallas kernels  13.8 us (23%)
  local copies, waits for them, and re-layouts  3.13 us (5%)
  starting transfers between devices  2.65 us (4%)
  waiting for transfers between devices  2.4 us (4%)
    all_to_all x1, blocking collectives, to_heads(): return lax.all_to_all(pieces, 'lo', split_axis=0, concat_axis=0, tiled=True)  26.5 us
    all_to_all x1, blocking collectives, body(): back = lax.all_to_all(out, 'lo', split_axis=0, concat_axis=0, tiled=True)  11.7 us
    pallas_call x1, Pallas kernels, body(): call(keys_kernel, 'keys', [((blocks, *pair), bf16), ((blocks, *pair), bf1...  7.92 us
    unnamed x8, local copies, waits for them, and re-layouts  3.13 us
    ppermute x1, starting transfers between devices, body(): incoming = lax.ppermute(total, 'hi', hop)  2.65 us
    ppermute x1, waiting for transfers between devices, body(): incoming = lax.ppermute(total, 'hi', hop)  2.4 us
    pallas_call x1, Pallas kernels, body(): call(queries_kernel, 'queries', [((blocks, *pair), bf16), ((blocks, *one)...  1.76 us
    pallas_call x1, Pallas kernels, body(): call(values_kernel, 'values', [((blocks, *pair), bf16), ((nodes, *one), f...  1.63 us
  transfers between devices with their start and end apart: 1, of which 1 were waited for; matrix products, arithmetic and copies ran while one was open for 0% of the time, Pallas kernels for 3%

profile of v3, /device:TPU:0, one launch (start us, length us, event | category | flops | bytes accessed | tf_op | source)
XLA Modules:
  0.0 60.1 jit_solution(12171817474448913183)
XLA Ops:
  0.0 0.0 copy-start
  0.0 1.0 %copy-done = bf16[128,2048]{1,0:T(8,128)(2,1)S(1)} copy-done((bf16[128,2048]{1,0:T(8,128)(2,1)S(1)}, bf16[128,2048]{1,0:T(8,128)(2,1)}, u32[]{:S(2)}) %copy-start) | copy-done | bytes 524312
  1.0 0.0 copy-start.1
  1.0 1.0 %copy-done.1 = bf16[128,2048]{1,0:T(8,128)(2,1)S(1)} copy-done((bf16[128,2048]{1,0:T(8,128)(2,1)S(1)}, bf16[128,2048]{1,0:T(8,128)(2,1)}, u32[]{:S(2)}) %copy-start.1) | copy-done | bytes 524312
  2.1 0.0 copy-start.2
  2.1 1.0 %copy-done.2 = bf16[128,2048]{1,0:T(8,128)(2,1)S(1)} copy-done((bf16[128,2048]{1,0:T(8,128)(2,1)S(1)}, bf16[128,2048]{1,0:T(8,128)(2,1)}, u32[]{:S(2)}) %copy-start.2) | copy-done | bytes 524312
  3.1 0.3 pack.1
  3.4 26.5 %all_to_all.10.kvq_ref = bf16[16,3,128,128]{3,2,1,0:T(8,128)(2,1)S(1)} all-to-all(bf16[16,3,128,128]{3,2,1,0:T(8,128)(2,1)S(1)} %pack.1), channel_id=1, replica_groups=mesh['seq'=16,'grp'=2] {'seq':(2)8,'grp'}, dimensions={0} | all-to-all | bytes 3145728 | tf_op jit(solution)/shard_map/all_to_all | solution.py:240
  29.9 7.9 %keys.1 = (bf16[16,128,256]{2,1,0:T(8,128)(2,1)S(1)}, bf16[16,128,256]{2,1,0:T(8,128)(2,1)S(1)}, bf16[31,128,256]{2,1,0:T(8,128)(2,1)S(1)}, bf16[31,128,256]{2,1,0:T(8,128)(2,1)S(1)}) custom-call(bf16[16,3,128,128]{3,2,1,0:T(8,128)(2,1)S(1)} %all_to_all.10.kvq_ref), custom_call_target="tpu_custom_call" | custom-call | flops 5368709120 | bytes 4194304 | tf_op jit(solution)/shard_map/keys/pallas_call | solution.py:247
  37.8 1.6 %values.1 = (bf16[16,128,256]{2,1,0:T(8,128)(2,1)S(1)}, f32[31,128,128]{2,1,0:T(8,128)S(1)}, f32[128,128]{1,0:T(8,128)S(1)}) custom-call(bf16[16,3,128,128]{3,2,1,0:T(8,128)(2,1)S(1)} %all_to_all.10.kvq_ref, bf16[16,128,256]{2,1,0:T(8,128)(2,1)S(1)} %get-tuple-element.16.tu_ref, bf16[31,128,256]{2,1,0:T(8,128)(2,1)S(1)} %get-tuple-element.17.a_ref), custom_call_target="tpu_custom_call" | custom-call | flops 1073741824 | bytes 4194304 | tf_op jit(solution)/shard_map/values/pallas_call | solution.py:252
  39.4 2.7 %collective-permute-start = (f32[128,128]{1,0:T(8,128)S(1)}, f32[128,128]{1,0:T(8,128)S(1)}, u32[]{:S(2)}, u32[]{:S(2)}) collective-permute-start(f32[128,128]{1,0:T(8,128)S(1)} %get-tuple-element.24), channel_id=1, source_target_pairs={{0,16},{16,0},{1,17},{17,1},{2,18},{18,2},{3,19},{19,3},{4,20},{20... | collective-permute-start | bytes 196616 | tf_op jit(solution)/shard_map/ppermute | solution.py:258
  42.1 0.0 copy-start.3
  42.1 1.8 %queries.1 = (bf16[16,128,256]{2,1,0:T(8,128)(2,1)S(1)}, f32[16,128,128]{2,1,0:T(8,128)S(1)}, f32[31,128,128]{2,1,0:T(8,128)S(1)}) custom-call(bf16[16,3,128,128]{3,2,1,0:T(8,128)(2,1)S(1)} %all_to_all.10.kvq_ref, bf16[16,128,256]{2,1,0:T(8,128)(2,1)S(1)} %get-tuple-element.15.w_ref, bf16[16,128,256]{2,1,0:T(8,128)(2,1)S(1)} %get-tuple-element.18.u_ref, ...), custom_call_target="tpu_custom_call" | custom-call | flops 1610612736 | bytes 4194304 | tf_op jit(solution)/shard_map/queries/pallas_call | solution.py:269
  43.9 2.4 %collective-permute-done.state_ref = f32[128,128]{1,0:T(8,128)S(1)} collective-permute-done((f32[128,128]{1,0:T(8,128)S(1)}, f32[128,128]{1,0:T(8,128)S(1)}, u32[]{:S(2)}, u32[]{:S(2)}) %collective-permute-start) | collective-permute-done | bytes 65568 | tf_op jit(solution)/shard_map/ppermute | solution.py:258
  46.3 0.0 copy-done.3
  46.3 1.2 %finish.1 = bf16[16,128,128]{2,1,0:T(8,128)(2,1)S(1)} custom-call(bf16[16,128,256]{2,1,0:T(8,128)(2,1)S(1)} %get-tuple-element.20.qt_ref, f32[16,128,128]{2,1,0:T(8,128)S(1)} %get-tuple-element.21.ol_ref, bf16[31,128,256]{2,1,0:T(8,128)(2,1)S(1)} %get-tuple-element.22.pa_ref, f32[31,128,128]{2,1,0:T(8,128)S(1)} %get-tuple-element.23.pb_ref, ...), custom_call_target="tpu_custom_call" | custom-call | flops 536870912 | bytes 4194304 | tf_op jit(solution)/shard_map/finish/pallas_call | solution.py:274
  47.5 11.7 %all_to_all.11.in_ref = bf16[16,128,128]{2,1,0:T(8,128)(2,1)S(1)} all-to-all(bf16[16,128,128]{2,1,0:T(8,128)(2,1)S(1)} %finish.1), channel_id=1, replica_groups=mesh['seq'=16,'grp'=2] {'seq':(2)8,'grp'}, dimensions={0} | all-to-all | bytes 1048576 | tf_op jit(solution)/shard_map/all_to_all | solution.py:277
  59.2 0.9 %unpack.1 = bf16[128,2048]{1,0:T(8,128)(2,1)} custom-call(bf16[16,128,128]{2,1,0:T(8,128)(2,1)S(1)} %all_to_all.11.in_ref), custom_call_target="tpu_custom_call" | custom-call | bytes 4194304 | tf_op jit(solution)/shard_map/unpack/pallas_call | solution.py:278
Async XLA Ops:
  0.0 1.0 %copy-start = (bf16[128,2048]{1,0:T(8,128)(2,1)S(1)}, bf16[128,2048]{1,0:T(8,128)(2,1)}, u32[]{:S(2)}) copy-start(bf16[128,2048]{1,0:T(8,128)(2,1)} %refs_0_.1) | copy-start | bytes 1572868
  1.0 1.0 %copy-start.1 = (bf16[128,2048]{1,0:T(8,128)(2,1)S(1)}, bf16[128,2048]{1,0:T(8,128)(2,1)}, u32[]{:S(2)}) copy-start(bf16[128,2048]{1,0:T(8,128)(2,1)} %refs_1_.1) | copy-start | bytes 1572868
  2.1 1.0 %copy-start.2 = (bf16[128,2048]{1,0:T(8,128)(2,1)S(1)}, bf16[128,2048]{1,0:T(8,128)(2,1)}, u32[]{:S(2)}) copy-start(bf16[128,2048]{1,0:T(8,128)(2,1)} %refs_2_.1) | copy-start | bytes 1572868
  39.4 6.8 %collective-permute-start = (f32[128,128]{1,0:T(8,128)S(1)}, f32[128,128]{1,0:T(8,128)S(1)}, u32[]{:S(2)}, u32[]{:S(2)}) collective-permute-start(f32[128,128]{1,0:T(8,128)S(1)} %get-tuple-element.24), channel_id=1, source_target_pairs={{0,16},{16,0},{1,17},{17,1},{2,18},{18,2},{3,19},{19,3},{4,20},{20... | collective-permute-start | bytes 196616 | tf_op jit(solution)/shard_map/ppermute | solution.py:258
  42.1 4.2 %copy-start.3 = (f32[128]{0:T(128)S(1)}, f32[128]{0:T(128)}, u32[]{:S(2)}) copy-start(f32[128]{0:T(128)} %param.7) | copy-start | bytes 1540

commit v4 on v3

v4 whole, which is shorter than its diff:
```python
import functools

import jax
import jax.numpy as jnp
from jax import lax
from jax.experimental import pallas as pl
from jax.experimental.pallas import tpu as pltpu
from jax.sharding import Mesh
from jax.sharding import PartitionSpec as P

HEAD_DIM = 128
BLOCK = 128
key_eps = 1e-06
norm_eps = 1e-05
BATCH = 8
BASE = 8

f32 = jnp.float32
bf16 = jnp.bfloat16


def mm(left, right):
    return jnp.dot(left, right, preferred_element_type=f32)


def mm_nt(left, right):
    return lax.dot_general(left, right, (((1,), (1,)), ((), ())), preferred_element_type=f32)


def split(value):
    high = value.astype(bf16)
    low = (value - high.astype(f32)).astype(bf16)
    return jnp.concatenate([high, low], axis=1)


def twice(rows):
    return jnp.concatenate([rows, rows], axis=0)


def fold(wide):
    half = wide.shape[1] // 2
    return wide[:, :half] + wide[:, half:]


def product(left_pair, right_pair):
    return fold(mm(left_pair, twice(right_pair)))


def product_wide(left_pair, first_pair, second_pair):
    n = HEAD_DIM
    highs = jnp.concatenate([first_pair[:, :n], second_pair[:, :n]], axis=1)
    lows = jnp.concatenate([first_pair[:, n:], second_pair[:, n:]], axis=1)
    return mm(left_pair, twice(highs)) + mm(left_pair[:, :n], lows)


def iotas():
    row = lax.broadcasted_iota(jnp.int32, (BLOCK, BLOCK), 0)
    col = lax.broadcasted_iota(jnp.int32, (BLOCK, BLOCK), 1)
    return row, col


def batches(count, run):
    size = min(BATCH, count)
    if count == size:
        run([j for j in range(count)])
    else:
        def one(i, carried):
            run([i * size + j for j in range(size)])
            return carried
        lax.fori_loop(0, count // size, one, 0)


def node_offsets(count):
    offsets, at, size = [], 0, count
    while size >= 1:
        offsets.append(at)
        at += size
        size //= 2
    return offsets, at


def move(pairs, sem):
    copies = [pltpu.make_async_copy(source, target, sem.at[i]) for i, (source, target) in enumerate(pairs)]
    for copy in copies:
        copy.start()
    for copy in copies:
        copy.wait()


def columns(h):
    return pl.ds(h * HEAD_DIM, HEAD_DIM)


def pack_kernel(*refs):
    *ins, out_ref, sem = refs
    heads = out_ref.shape[0]
    move([(ref.at[:, columns(h)], out_ref.at[h, i]) for i, ref in enumerate(ins) for h in range(heads)], sem)


def unpack_kernel(in_ref, out_ref, sem):
    move([(in_ref.at[h], out_ref.at[:, columns(h)]) for h in range(in_ref.shape[0])], sem)


def base_inverses(coupling):
    count, tiles, lanes = len(coupling), BLOCK // BASE, BLOCK
    tile = lax.broadcasted_iota(jnp.int32, (tiles, BASE, lanes), 0)
    lane = lax.broadcasted_iota(jnp.int32, (tiles, BASE, lanes), 2)
    own = lane // BASE == tile
    packed = [jnp.sum(jnp.where(own, n.reshape(tiles, BASE, lanes), 0.0), axis=0) for n in coupling]
    rows = split(jnp.concatenate(packed, axis=0))
    source = lax.broadcasted_iota(jnp.int32, (lanes, lanes), 0)
    target = lax.broadcasted_iota(jnp.int32, (lanes, lanes), 1)
    same = source // BASE == target // BASE
    spread = jnp.concatenate(
        [(same & (source % BASE == k)).astype(bf16) for k in range(BASE - 1)], axis=1
    )
    factors = mm(rows, twice(spread))
    sub = lax.broadcasted_iota(jnp.int32, (count, BASE, lanes), 1)
    at = lax.broadcasted_iota(jnp.int32, (count, BASE, lanes), 2) % BASE
    solved = (sub == at).astype(f32)
    for k in range(BASE - 1):
        factor = factors[:, k * lanes : (k + 1) * lanes].reshape(count, BASE, lanes)
        solved = solved - factor * solved[:, k : k + 1, :]
    return [
        jnp.where(own, jnp.broadcast_to(solved[i][None], (tiles, BASE, lanes)), 0.0).reshape(BLOCK, lanes)
        for i in range(count)
    ]


def maps_kernel(climb, kvq_ref, w_ref, u_ref, a_ref, b_ref, total_ref):
    count = kvq_ref.shape[0]
    offsets, _ = node_offsets(count)
    row, col = iotas()
    diagonal = row == col
    eye = diagonal.astype(f32)

    def run(blocks):
        keys = [kvq_ref[j, 0] for j in blocks]
        grams = [mm_nt(k, k) for k in keys]
        coupling, scale_cols, scale_rows = [], [], []
        for g in grams:
            on_diagonal = jnp.where(diagonal, g, 0.0)
            c = 1.0 / jnp.sqrt(jnp.sum(on_diagonal, axis=1, keepdims=True) + key_eps)
            r = 1.0 / jnp.sqrt(jnp.sum(on_diagonal, axis=0, keepdims=True) + key_eps)
            scale_cols.append(c)
            scale_rows.append(r)
            coupling.append(jnp.where(row > col, (2.0 * c) * g * r, 0.0))
        inverses = base_inverses(coupling)
        size = BASE
        while size < BLOCK:
            mask = ((row // size) % 2 == 1) & (col // size == row // size - 1)
            parts = [jnp.where(mask, n, 0.0) for n in coupling]
            pairs = [split(t) for t in inverses]
            inner = [product(split(p), t) for p, t in zip(parts, pairs)]
            outer = [product(t, split(z)) for t, z in zip(pairs, inner)]
            inverses = [t - z for t, z in zip(inverses, outer)]
            size *= 2
        lefts = [(2.0 * c) * t for c, t in zip(scale_cols, inverses)]
        weights = [split(mm(split(t * r), twice(k))) for t, r, k in zip(lefts, scale_rows, keys)]
        changes = [split(mm(split(t), twice(kvq_ref[j, 1]))) for t, j in zip(lefts, blocks)]
        for i, j in enumerate(blocks):
            w_ref[j] = weights[i]
            u_ref[j] = changes[i]
            across = keys[i].T
            a_ref[j] = split(eye - fold(mm(across, weights[i])))
            b_ref[j] = fold(mm(across, changes[i]))

    batches(count, run)
    for level in range(1, len(offsets)):
        below, here = offsets[level - 1], offsets[level]
        for i in range(count >> level):
            first, second = below + 2 * i, below + 2 * i + 1
            later = a_ref[second]
            b_ref[here + i] = product(later, split(b_ref[first])) + b_ref[second]
            if climb or level < len(offsets) - 1:
                a_ref[here + i] = split(product(later, a_ref[first]))
    total_ref[...] = b_ref[offsets[-1]]


def prefix_steps(count):
    offsets, _ = node_offsets(count)
    steps = []
    for level in range(len(offsets) - 2, -1, -1):
        here, above = offsets[level], offsets[level + 1]
        for i in range(count >> (level + 1)):
            parent = above + i if i > 0 else None
            if i > 0 or level == 0:
                steps.append((here + 2 * i, None, parent))
            steps.append((here + 2 * i + 1, here + 2 * i, parent))
    return steps


def queries_kernel(kvq_ref, w_ref, u_ref, a_ref, b_ref, qp_ref, op_ref, pa_ref, pb_ref):
    count = kvq_ref.shape[0]
    row, col = iotas()
    causal = row >= col
    for (target, left, parent) in prefix_steps(count):
        if parent is None:
            pa_ref[target] = split((row == col).astype(f32)) if left is None else a_ref[left]
            pb_ref[target] = jnp.zeros((HEAD_DIM, HEAD_DIM), f32) if left is None else b_ref[left]
        elif left is None:
            pa_ref[target] = pa_ref[parent]
            pb_ref[target] = pb_ref[parent]
        else:
            pa_ref[target] = split(product(a_ref[left], pa_ref[parent]))
            pb_ref[target] = product(a_ref[left], split(pb_ref[parent])) + b_ref[left]

    def run(blocks):
        scores = [jnp.where(causal, mm_nt(kvq_ref[j, 2], kvq_ref[j, 0]), 0.0) for j in blocks]
        local = [product_wide(split(c), w_ref[j], u_ref[j]) for c, j in zip(scores, blocks)]
        through = [split(kvq_ref[j, 2].astype(f32) - t[:, :HEAD_DIM]) for t, j in zip(local, blocks)]
        joint = [product_wide(t, pa_ref[j], split(pb_ref[j])) for t, j in zip(through, blocks)]
        for i, j in enumerate(blocks):
            qp_ref[j] = split(joint[i][:, :HEAD_DIM])
            op_ref[j] = joint[i][:, HEAD_DIM:] + local[i][:, HEAD_DIM:]

    batches(count, run)


def finish_kernel(qp_ref, op_ref, state_ref, gain_ref, out_ref):
    arrived = jnp.where(lax.axis_index("hi") > 0, state_ref[...], 0.0)
    state = twice(split(arrived))
    gain = gain_ref[...]

    def run(blocks):
        outputs = [fold(mm(qp_ref[j], state)) + op_ref[j] for j in blocks]
        for j, output in zip(blocks, outputs):
            scale = lax.rsqrt(jnp.mean(output * output, axis=1, keepdims=True) + norm_eps)
            out_ref[j] = (output * scale * gain).astype(bf16)

    batches(out_ref.shape[0], run)


def call(kernel, name, outs, flops, kept=True, limit=24 << 20, scratch=(), in_space=None):
    vmem = pl.BlockSpec(memory_space=pltpu.VMEM)
    far = pl.BlockSpec(memory_space=pltpu.HBM)
    make = pltpu.VMEM if kept else jax.ShapeDtypeStruct
    extra = {} if in_space is None else {"in_specs": [pl.BlockSpec(memory_space=s) for s in in_space]}
    return pl.pallas_call(
        kernel,
        name=name,
        out_shape=tuple(make(s, t) for s, t in outs),
        out_specs=tuple(vmem if kept else far for _ in outs),
        scratch_shapes=list(scratch),
        compiler_params=pltpu.CompilerParams(vmem_limit_bytes=limit),
        cost_estimate=pl.CostEstimate(flops=flops, bytes_accessed=4 << 20, transcendentals=0),
        **extra,
    )


def held(space, *values):
    return [pltpu.with_memory_space_constraint(v, space) for v in values]


def near(*values):
    return held(pltpu.VMEM, *values)


def body(groups, lanes, queries, key_vectors, head_value_rows, out_gain):
    tokens, features = queries.shape
    if tokens != BLOCK or features != lanes * HEAD_DIM:
        raise ValueError("unsupported sizes")
    blocks = lanes
    _, nodes = node_offsets(blocks)
    one = (HEAD_DIM, HEAD_DIM)
    pair = (HEAD_DIM, 2 * HEAD_DIM)
    unit = 2 * BLOCK**3 * 4
    dma = pltpu.SemaphoreType.DMA
    pieces_shape = (lanes, 3, BLOCK, HEAD_DIM)
    (pieces,) = call(
        pack_kernel, "pack", [(pieces_shape, bf16)], 0, scratch=[dma((3 * lanes,))], in_space=[pltpu.HBM] * 3,
    )(*held(pltpu.HBM, key_vectors, head_value_rows, queries))
    kvq = lax.all_to_all(pieces, "lo", split_axis=0, concat_axis=0, tiled=True)
    w, u, a, b, total = call(
        functools.partial(maps_kernel, groups > 2), "maps",
        [((blocks, *pair), bf16), ((blocks, *pair), bf16), ((nodes, *pair), bf16), ((nodes, *one), f32), (one, f32)],
        unit * blocks * 20,
    )(*near(kvq))
    hop = [(source, (source + 1) % groups) for source in range(groups)]
    incoming = lax.ppermute(total, "hi", hop)
    if groups > 2:
        top = a[nodes - 1].astype(f32)
        transition = top[:, :HEAD_DIM] + top[:, HEAD_DIM:]

        def relay(i, arriving):
            arriving = jnp.where(lax.axis_index("hi") > 0, arriving, 0.0)
            leaving = jnp.dot(transition, arriving, precision=lax.Precision.HIGHEST) + total
            return lax.ppermute(leaving, "hi", hop)

        incoming = lax.fori_loop(0, groups - 2, relay, incoming)
    qp, op = call(
        queries_kernel, "queries",
        [((blocks, *pair), bf16), ((blocks, *one), f32)],
        unit * blocks * 6,
        scratch=[pltpu.VMEM((nodes, *pair), bf16), pltpu.VMEM((nodes, *one), f32)],
    )(*near(kvq, w, u, a, b))
    (out,) = call(
        finish_kernel, "finish", [((blocks, BLOCK, HEAD_DIM), bf16)], unit * blocks * 2,
    )(*near(qp, op), incoming, out_gain.reshape(1, HEAD_DIM))
    back = lax.all_to_all(out, "lo", split_axis=0, concat_axis=0, tiled=True)
    (mixed,) = call(
        unpack_kernel, "unpack", [((tokens, features), bf16)], 0, kept=False, scratch=[dma((lanes,))],
    )(*near(back))
    return mixed


def solution(mesh):
    count = mesh.devices.size

    def run(queries, key_vectors, head_value_rows, out_gain):
        lanes = queries.shape[1] // HEAD_DIM
        regrouped = Mesh(mesh.devices.reshape(count // lanes, lanes), ("hi", "lo"))
        rows = P(("hi", "lo"), None)
        return jax.shard_map(
            functools.partial(body, count // lanes, lanes),
            mesh=regrouped, in_specs=(rows, rows, rows, P()), out_specs=rows, check_vma=False,
        )(queries, key_vectors, head_value_rows, out_gain)

    return run
```

time: 60.4 us -> 55.9 us (0.925)
  local copies, waits for them, and re-layouts: 3.13 us -> 0.01 us
  waiting for transfers between devices: 2.4 us -> 1.68 us
  Pallas kernels: 13.8 us -> 13.1 us
    unnamed x8 -> x2, local copies, waits for them, and re-layouts: 3.13 us -> 0.01 us
    pallas_call x4 -> x3, Pallas kernels: 10.7 us -> 9.78 us  [the longest x1 7.08 us: body(): call(functools.partial(maps_kernel, groups > 2), 'maps', [((blocks, *pair...]
    ppermute x1, waiting for transfers between devices: 2.4 us -> 1.68 us  [body(): incoming = lax.ppermute(total, 'hi', hop)]
    pallas_call x1, Pallas kernels: 1.76 us -> 2.47 us  [body(): call(queries_kernel, 'queries', [((blocks, *pair), bf16), ((blocks, *one)...]
  transfers between devices with their start and end apart: 1 -> 1, of which waited for: 1 -> 1; matrix products, arithmetic and copies ran while one was open for 0% -> 0% of each run, Pallas kernels for 3% -> 4%
where the time goes in v4:
time: 55.9 us; the launch traced here: 55.6 us
  blocking collectives  38.1 us (68%)
  Pallas kernels  13.1 us (23%)
  starting transfers between devices  2.67 us (5%)
  waiting for transfers between devices  1.68 us (3%)
    all_to_all x1, blocking collectives, body(): kvq = lax.all_to_all(pieces, 'lo', split_axis=0, concat_axis=0, tiled=True)  26.5 us
    all_to_all x1, blocking collectives, body(): back = lax.all_to_all(out, 'lo', split_axis=0, concat_axis=0, tiled=True)  11.7 us
    pallas_call x1, Pallas kernels, body(): call(functools.partial(maps_kernel, groups > 2), 'maps', [((blocks, *pair...  7.08 us
    ppermute x1, starting transfers between devices, body(): incoming = lax.ppermute(total, 'hi', hop)  2.67 us
    pallas_call x1, Pallas kernels, body(): call(queries_kernel, 'queries', [((blocks, *pair), bf16), ((blocks, *one)...  2.47 us
    pallas_call x1, Pallas kernels, body(): call(pack_kernel, 'pack', [(pieces_shape, bf16)], 0, scratch=[dma((3 * la...  1.78 us
    ppermute x1, waiting for transfers between devices, body(): incoming = lax.ppermute(total, 'hi', hop)  1.68 us
  transfers between devices with their start and end apart: 1, of which 1 were waited for; matrix products, arithmetic and copies ran while one was open for 0% of the time, Pallas kernels for 4%

profile of v4, /device:TPU:0, one launch (start us, length us, event | category | flops | bytes accessed | tf_op | source)
XLA Modules:
  0.0 55.6 jit_solution(11695433876680641924)
XLA Ops:
  0.0 1.8 %pack.1 = bf16[16,3,128,128]{3,2,1,0:T(8,128)(2,1)S(1)} custom-call(bf16[128,2048]{1,0:T(8,128)(2,1)} %refs_0_.1, bf16[128,2048]{1,0:T(8,128)(2,1)} %refs_1_.1, bf16[128,2048]{1,0:T(8,128)(2,1)} %refs_2_.1), custom_call_target="tpu_custom_call" | custom-call | bytes 4194304 | tf_op jit(solution)/shard_map/pack/pallas_call | solution.py:270
  1.8 26.5 %all_to_all.10.kvq_ref = bf16[16,3,128,128]{3,2,1,0:T(8,128)(2,1)S(1)} all-to-all(bf16[16,3,128,128]{3,2,1,0:T(8,128)(2,1)S(1)} %pack.1), channel_id=1, replica_groups=mesh['seq'=16,'grp'=2] {'seq':(2)8,'grp'}, dimensions={0} | all-to-all | bytes 3145728 | tf_op jit(solution)/shard_map/all_to_all | solution.py:273
  28.3 7.1 %maps.1 = (bf16[16,128,256]{2,1,0:T(8,128)(2,1)S(1)}, bf16[16,128,256]{2,1,0:T(8,128)(2,1)S(1)}, bf16[31,128,256]{2,1,0:T(8,128)(2,1)S(1)}, f32[31,128,128]{2,1,0:T(8,128)S(1)}, f32[128,128]{1,0:T(8,128)S(1)}) custom-call(bf16[16,3,128,128]{3,2,1,0:T(8,128)(2,1)S(1)} %all_to_all.10.kvq_ref), custom_call_target="tpu_custom_call" | custom-call | flops 5368709120 | bytes 4194304 | tf_op jit(solution)/shard_map/maps/pallas_call | solution.py:274
  35.4 2.7 %collective-permute-start = (f32[128,128]{1,0:T(8,128)S(1)}, f32[128,128]{1,0:T(8,128)S(1)}, u32[]{:S(2)}, u32[]{:S(2)}) collective-permute-start(f32[128,128]{1,0:T(8,128)S(1)} %get-tuple-element.18), channel_id=1, source_target_pairs={{0,16},{16,0},{1,17},{17,1},{2,18},{18,2},{3,19},{19,3},{4,20},{20... | collective-permute-start | bytes 196616 | tf_op jit(solution)/shard_map/ppermute | solution.py:280
  38.0 0.0 copy-start
  38.0 2.5 %queries.1 = (bf16[16,128,256]{2,1,0:T(8,128)(2,1)S(1)}, f32[16,128,128]{2,1,0:T(8,128)S(1)}) custom-call(bf16[16,3,128,128]{3,2,1,0:T(8,128)(2,1)S(1)} %all_to_all.10.kvq_ref, bf16[16,128,256]{2,1,0:T(8,128)(2,1)S(1)} %get-tuple-element.12.w_ref, bf16[16,128,256]{2,1,0:T(8,128)(2,1)S(1)} %get-tuple-element.13.u_ref, ...), custom_call_target="tpu_custom_call" | custom-call | flops 1610612736 | bytes 4194304 | tf_op jit(solution)/shard_map/queries/pallas_call | solution.py:291
  40.5 1.7 %collective-permute-done.state_ref = f32[128,128]{1,0:T(8,128)S(1)} collective-permute-done((f32[128,128]{1,0:T(8,128)S(1)}, f32[128,128]{1,0:T(8,128)S(1)}, u32[]{:S(2)}, u32[]{:S(2)}) %collective-permute-start) | collective-permute-done | bytes 65568 | tf_op jit(solution)/shard_map/ppermute | solution.py:280
  42.2 0.0 copy-done
  42.2 0.8 %finish.1 = bf16[16,128,128]{2,1,0:T(8,128)(2,1)S(1)} custom-call(bf16[16,128,256]{2,1,0:T(8,128)(2,1)S(1)} %get-tuple-element.16.qp_ref, f32[16,128,128]{2,1,0:T(8,128)S(1)} %get-tuple-element.17.op_ref, f32[128,128]{1,0:T(8,128)S(1)} %collective-permute-done.state_ref, f32[1,128]{1,0:T(1,128)S(1)} %bitcast.1), custom_call_target="tpu_custom_call" | custom-call | flops 536870912 | bytes 4194304 | tf_op jit(solution)/shard_map/finish/pallas_call | solution.py:297
  43.0 11.7 %all_to_all.11.in_ref = bf16[16,128,128]{2,1,0:T(8,128)(2,1)S(1)} all-to-all(bf16[16,128,128]{2,1,0:T(8,128)(2,1)S(1)} %finish.1), channel_id=1, replica_groups=mesh['seq'=16,'grp'=2] {'seq':(2)8,'grp'}, dimensions={0} | all-to-all | bytes 1048576 | tf_op jit(solution)/shard_map/all_to_all | solution.py:300
  54.7 0.9 %unpack.1 = bf16[128,2048]{1,0:T(8,128)(2,1)} custom-call(bf16[16,128,128]{2,1,0:T(8,128)(2,1)S(1)} %all_to_all.11.in_ref), custom_call_target="tpu_custom_call" | custom-call | bytes 4194304 | tf_op jit(solution)/shard_map/unpack/pallas_call | solution.py:301
Async XLA Ops:
  35.4 6.8 %collective-permute-start = (f32[128,128]{1,0:T(8,128)S(1)}, f32[128,128]{1,0:T(8,128)S(1)}, u32[]{:S(2)}, u32[]{:S(2)}) collective-permute-start(f32[128,128]{1,0:T(8,128)S(1)} %get-tuple-element.18), channel_id=1, source_target_pairs={{0,16},{16,0},{1,17},{17,1},{2,18},{18,2},{3,19},{19,3},{4,20},{20... | collective-permute-start | bytes 196616 | tf_op jit(solution)/shard_map/ppermute | solution.py:280
  38.0 4.2 %copy-start = (f32[128]{0:T(128)S(1)}, f32[128]{0:T(128)}, u32[]{:S(2)}) copy-start(f32[128]{0:T(128)} %param.7) | copy-start | bytes 1540

commit v5 on v4

--- a/solution.py
+++ b/solution.py
@@ -12,8 +12,9 @@
 BLOCK = 128
 key_eps = 1e-06
 norm_eps = 1e-05
-BATCH = 8
-BASE = 8
+BATCH = 16
+BASE = 16
+PARTS = 4
 
 f32 = jnp.float32
 bf16 = jnp.bfloat16
@@ -40,6 +41,13 @@
 def fold(wide):
     half = wide.shape[1] // 2
     return wide[:, :half] + wide[:, half:]
+
+
+def stack(first_pair, second_pair):
+    n = HEAD_DIM
+    highs = jnp.concatenate([first_pair[:, :n], second_pair[:, :n]], axis=1)
+    lows = jnp.concatenate([first_pair[:, n:], second_pair[:, n:]], axis=1)
+    return jnp.concatenate([highs, lows], axis=0)
 
 
 def product(left_pair, right_pair):
@@ -79,26 +87,28 @@
     return offsets, at
 
 
-def move(pairs, sem):
-    copies = [pltpu.make_async_copy(source, target, sem.at[i]) for i, (source, target) in enumerate(pairs)]
+def pack_kernel(*refs):
+    *ins, out_ref, held_ref, sem = refs
+    copies = [pltpu.make_async_copy(ref, held_ref.at[i], sem.at[i]) for i, ref in enumerate(ins)]
     for copy in copies:
         copy.start()
+    for i, copy in enumerate(copies):
+        copy.wait()
+        for h in range(out_ref.shape[0]):
+            out_ref[h, i] = held_ref[i, :, h * HEAD_DIM : (h + 1) * HEAD_DIM]
+
+
+def unpack_kernel(in_ref, out_ref, held_ref, sem):
+    size = out_ref.shape[0] // PARTS
+    copies = []
+    for i in range(PARTS):
+        rows = slice(i * size, (i + 1) * size)
+        for h in range(in_ref.shape[0]):
+            held_ref[rows, h * HEAD_DIM : (h + 1) * HEAD_DIM] = in_ref[h, rows]
+        copies.append(pltpu.make_async_copy(held_ref.at[rows], out_ref.at[rows], sem.at[i]))
+        copies[-1].start()
     for copy in copies:
         copy.wait()
-
-
-def columns(h):
-    return pl.ds(h * HEAD_DIM, HEAD_DIM)
-
-
-def pack_kernel(*refs):
-    *ins, out_ref, sem = refs
-    heads = out_ref.shape[0]
-    move([(ref.at[:, columns(h)], out_ref.at[h, i]) for i, ref in enumerate(ins) for h in range(heads)], sem)
-
-
-def unpack_kernel(in_ref, out_ref, sem):
-    move([(in_ref.at[h], out_ref.at[:, columns(h)]) for h in range(in_ref.shape[0])], sem)
 
 
 def base_inverses(coupling):
@@ -162,8 +172,9 @@
             w_ref[j] = weights[i]
             u_ref[j] = changes[i]
             across = keys[i].T
-            a_ref[j] = split(eye - fold(mm(across, weights[i])))
-            b_ref[j] = fold(mm(across, changes[i]))
+            both = mm(jnp.concatenate([across, across], axis=1), stack(weights[i], changes[i]))
+            a_ref[j] = split(eye - both[:, :HEAD_DIM])
+            b_ref[j] = both[:, HEAD_DIM:]
 
     batches(count, run)
     for level in range(1, len(offsets)):
@@ -268,7 +279,7 @@
     dma = pltpu.SemaphoreType.DMA
     pieces_shape = (lanes, 3, BLOCK, HEAD_DIM)
     (pieces,) = call(
-        pack_kernel, "pack", [(pieces_shape, bf16)], 0, scratch=[dma((3 * lanes,))], in_space=[pltpu.HBM] * 3,
+        pack_kernel, "pack", [(pieces_shape, bf16)], 0, scratch=[pltpu.VMEM((3, tokens, features), bf16), dma((3,))], in_space=[pltpu.HBM] * 3,
     )(*held(pltpu.HBM, key_vectors, head_value_rows, queries))
     kvq = lax.all_to_all(pieces, "lo", split_axis=0, concat_axis=0, tiled=True)
     w, u, a, b, total = call(
@@ -299,7 +310,7 @@
     )(*near(qp, op), incoming, out_gain.reshape(1, HEAD_DIM))
     back = lax.all_to_all(out, "lo", split_axis=0, concat_axis=0, tiled=True)
     (mixed,) = call(
-        unpack_kernel, "unpack", [((tokens, features), bf16)], 0, kept=False, scratch=[dma((lanes,))],
+        unpack_kernel, "unpack", [((tokens, features), bf16)], 0, kept=False, scratch=[pltpu.VMEM((tokens, features), bf16), dma((PARTS,))],
     )(*near(back))
     return mixed
 

time: 55.9 us -> 53.3 us (0.953)
  Pallas kernels: 13.1 us -> 10.2 us
    pallas_call x1, Pallas kernels: 7.08 us -> 5.26 us  [body(): call(functools.partial(maps_kernel, groups > 2), 'maps', [((blocks, *pair...]
where the time goes in v5:
time: 53.3 us; the launch traced here: 53.1 us
  blocking collectives  38.1 us (71%)
  Pallas kernels  10.2 us (19%)
  starting transfers between devices  2.66 us (5%)
  waiting for transfers between devices  2.07 us (4%)
    all_to_all x1, blocking collectives, body(): kvq = lax.all_to_all(pieces, 'lo', split_axis=0, concat_axis=0, tiled=True)  26.5 us
    all_to_all x1, blocking collectives, body(): back = lax.all_to_all(out, 'lo', split_axis=0, concat_axis=0, tiled=True)  11.7 us
    pallas_call x1, Pallas kernels, body(): call(functools.partial(maps_kernel, groups > 2), 'maps', [((blocks, *pair...  5.26 us
    ppermute x1, starting transfers between devices, body(): incoming = lax.ppermute(total, 'hi', hop)  2.66 us
    pallas_call x1, Pallas kernels, body(): call(queries_kernel, 'queries', [((blocks, *pair), bf16), ((blocks, *one)...  2.08 us
    ppermute x1, waiting for transfers between devices, body(): incoming = lax.ppermute(total, 'hi', hop)  2.07 us
    pallas_call x1, Pallas kernels, body(): call(pack_kernel, 'pack', [(pieces_shape, bf16)], 0, scratch=[pltpu.VMEM(...  1.47 us
  transfers between devices with their start and end apart: 1, of which 1 were waited for; matrix products, arithmetic and copies ran while one was open for 0% of the time, Pallas kernels for 4%

profile of v5, /device:TPU:0, one launch (start us, length us, event | category | flops | bytes accessed | tf_op | source)
XLA Modules:
  0.0 53.1 jit_solution(12202323872090459531)
XLA Ops:
  0.0 1.5 %pack.1 = bf16[16,3,128,128]{3,2,1,0:T(8,128)(2,1)S(1)} custom-call(bf16[128,2048]{1,0:T(8,128)(2,1)} %refs_0_.1, bf16[128,2048]{1,0:T(8,128)(2,1)} %refs_1_.1, bf16[128,2048]{1,0:T(8,128)(2,1)} %refs_2_.1), custom_call_target="tpu_custom_call" | custom-call | bytes 4194304 | tf_op jit(solution)/shard_map/pack/pallas_call | solution.py:281
  1.5 26.5 %all_to_all.10.kvq_ref = bf16[16,3,128,128]{3,2,1,0:T(8,128)(2,1)S(1)} all-to-all(bf16[16,3,128,128]{3,2,1,0:T(8,128)(2,1)S(1)} %pack.1), channel_id=1, replica_groups=mesh['seq'=16,'grp'=2] {'seq':(2)8,'grp'}, dimensions={0} | all-to-all | bytes 3145728 | tf_op jit(solution)/shard_map/all_to_all | solution.py:284
  28.0 5.3 %maps.1 = (bf16[16,128,256]{2,1,0:T(8,128)(2,1)S(1)}, bf16[16,128,256]{2,1,0:T(8,128)(2,1)S(1)}, bf16[31,128,256]{2,1,0:T(8,128)(2,1)S(1)}, f32[31,128,128]{2,1,0:T(8,128)S(1)}, f32[128,128]{1,0:T(8,128)S(1)}) custom-call(bf16[16,3,128,128]{3,2,1,0:T(8,128)(2,1)S(1)} %all_to_all.10.kvq_ref), custom_call_target="tpu_custom_call" | custom-call | flops 5368709120 | bytes 4194304 | tf_op jit(solution)/shard_map/maps/pallas_call | solution.py:285
  33.2 2.7 %collective-permute-start = (f32[128,128]{1,0:T(8,128)S(1)}, f32[128,128]{1,0:T(8,128)S(1)}, u32[]{:S(2)}, u32[]{:S(2)}) collective-permute-start(f32[128,128]{1,0:T(8,128)S(1)} %get-tuple-element.18), channel_id=1, source_target_pairs={{0,16},{16,0},{1,17},{17,1},{2,18},{18,2},{3,19},{19,3},{4,20},{20... | collective-permute-start | bytes 196616 | tf_op jit(solution)/shard_map/ppermute | solution.py:291
  35.9 0.0 copy-start
  35.9 2.1 %queries.1 = (bf16[16,128,256]{2,1,0:T(8,128)(2,1)S(1)}, f32[16,128,128]{2,1,0:T(8,128)S(1)}) custom-call(bf16[16,3,128,128]{3,2,1,0:T(8,128)(2,1)S(1)} %all_to_all.10.kvq_ref, bf16[16,128,256]{2,1,0:T(8,128)(2,1)S(1)} %get-tuple-element.12.w_ref, bf16[16,128,256]{2,1,0:T(8,128)(2,1)S(1)} %get-tuple-element.13.u_ref, ...), custom_call_target="tpu_custom_call" | custom-call | flops 1610612736 | bytes 4194304 | tf_op jit(solution)/shard_map/queries/pallas_call | solution.py:302
  38.0 2.1 %collective-permute-done.state_ref = f32[128,128]{1,0:T(8,128)S(1)} collective-permute-done((f32[128,128]{1,0:T(8,128)S(1)}, f32[128,128]{1,0:T(8,128)S(1)}, u32[]{:S(2)}, u32[]{:S(2)}) %collective-permute-start) | collective-permute-done | bytes 65568 | tf_op jit(solution)/shard_map/ppermute | solution.py:291
  40.1 0.0 copy-done
  40.1 0.6 %finish.1 = bf16[16,128,128]{2,1,0:T(8,128)(2,1)S(1)} custom-call(bf16[16,128,256]{2,1,0:T(8,128)(2,1)S(1)} %get-tuple-element.16.qp_ref, f32[16,128,128]{2,1,0:T(8,128)S(1)} %get-tuple-element.17.op_ref, f32[128,128]{1,0:T(8,128)S(1)} %collective-permute-done.state_ref, f32[1,128]{1,0:T(1,128)S(1)} %bitcast.1), custom_call_target="tpu_custom_call" | custom-call | flops 536870912 | bytes 4194304 | tf_op jit(solution)/shard_map/finish/pallas_call | solution.py:308
  40.6 11.7 %all_to_all.11.in_ref = bf16[16,128,128]{2,1,0:T(8,128)(2,1)S(1)} all-to-all(bf16[16,128,128]{2,1,0:T(8,128)(2,1)S(1)} %finish.1), channel_id=1, replica_groups=mesh['seq'=16,'grp'=2] {'seq':(2)8,'grp'}, dimensions={0} | all-to-all | bytes 1048576 | tf_op jit(solution)/shard_map/all_to_all | solution.py:311
  52.3 0.8 %unpack.1 = bf16[128,2048]{1,0:T(8,128)(2,1)} custom-call(bf16[16,128,128]{2,1,0:T(8,128)(2,1)S(1)} %all_to_all.11.in_ref), custom_call_target="tpu_custom_call" | custom-call | bytes 4194304 | tf_op jit(solution)/shard_map/unpack/pallas_call | solution.py:312
Async XLA Ops:
  33.2 6.8 %collective-permute-start = (f32[128,128]{1,0:T(8,128)S(1)}, f32[128,128]{1,0:T(8,128)S(1)}, u32[]{:S(2)}, u32[]{:S(2)}) collective-permute-start(f32[128,128]{1,0:T(8,128)S(1)} %get-tuple-element.18), channel_id=1, source_target_pairs={{0,16},{16,0},{1,17},{17,1},{2,18},{18,2},{3,19},{19,3},{4,20},{20... | collective-permute-start | bytes 196616 | tf_op jit(solution)/shard_map/ppermute | solution.py:291
  35.9 4.2 %copy-start = (f32[128]{0:T(128)S(1)}, f32[128]{0:T(128)}, u32[]{:S(2)}) copy-start(f32[128]{0:T(128)} %param.7) | copy-start | bytes 1540

commit v6 on v5

--- a/solution.py
+++ b/solution.py
@@ -137,8 +137,9 @@
     ]
 
 
-def maps_kernel(climb, kvq_ref, w_ref, u_ref, a_ref, b_ref, total_ref):
+def maps_kernel(climb, kvq_ref, k_ref, w_ref, u_far, a_ref, b_ref, total_ref, u_ref, sem):
     count = kvq_ref.shape[0]
+    park = pltpu.make_async_copy(u_ref, u_far, sem.at[0])
     offsets, _ = node_offsets(count)
     row, col = iotas()
     diagonal = row == col
@@ -169,14 +170,17 @@
         weights = [split(mm(split(t * r), twice(k))) for t, r, k in zip(lefts, scale_rows, keys)]
         changes = [split(mm(split(t), twice(kvq_ref[j, 1]))) for t, j in zip(lefts, blocks)]
         for i, j in enumerate(blocks):
+            u_ref[j] = changes[i]
+        park.start()
+        for i, j in enumerate(blocks):
+            k_ref[j] = keys[i]
             w_ref[j] = weights[i]
-            u_ref[j] = changes[i]
             across = keys[i].T
             both = mm(jnp.concatenate([across, across], axis=1), stack(weights[i], changes[i]))
             a_ref[j] = split(eye - both[:, :HEAD_DIM])
             b_ref[j] = both[:, HEAD_DIM:]
 
-    batches(count, run)
+    run(range(count))
     for level in range(1, len(offsets)):
         below, here = offsets[level - 1], offsets[level]
         for i in range(count >> level):
@@ -186,6 +190,7 @@
             if climb or level < len(offsets) - 1:
                 a_ref[here + i] = split(product(later, a_ref[first]))
     total_ref[...] = b_ref[offsets[-1]]
+    park.wait()
 
 
 def prefix_steps(count):
@@ -201,10 +206,10 @@
     return steps
 
 
-def queries_kernel(kvq_ref, w_ref, u_ref, a_ref, b_ref, qp_ref, op_ref, pa_ref, pb_ref):
-    count = kvq_ref.shape[0]
+def sweep_kernel(a_ref, b_ref, pa_out, pb_out, pa_ref, pb_ref, sem):
+    count = pa_out.shape[0]
     row, col = iotas()
-    causal = row >= col
+    copies = []
     for (target, left, parent) in prefix_steps(count):
         if parent is None:
             pa_ref[target] = split((row == col).astype(f32)) if left is None else a_ref[left]
@@ -215,17 +220,36 @@
         else:
             pa_ref[target] = split(product(a_ref[left], pa_ref[parent]))
             pb_ref[target] = product(a_ref[left], split(pb_ref[parent])) + b_ref[left]
-
-    def run(blocks):
-        scores = [jnp.where(causal, mm_nt(kvq_ref[j, 2], kvq_ref[j, 0]), 0.0) for j in blocks]
-        local = [product_wide(split(c), w_ref[j], u_ref[j]) for c, j in zip(scores, blocks)]
-        through = [split(kvq_ref[j, 2].astype(f32) - t[:, :HEAD_DIM]) for t, j in zip(local, blocks)]
-        joint = [product_wide(t, pa_ref[j], split(pb_ref[j])) for t, j in zip(through, blocks)]
-        for i, j in enumerate(blocks):
-            qp_ref[j] = split(joint[i][:, :HEAD_DIM])
-            op_ref[j] = joint[i][:, HEAD_DIM:] + local[i][:, HEAD_DIM:]
-
-    batches(count, run)
+    leaves = pl.ds(0, count)
+    copies = [
+        pltpu.make_async_copy(pa_ref.at[leaves], pa_out, sem.at[0]),
+        pltpu.make_async_copy(pb_ref.at[leaves], pb_out, sem.at[1]),
+    ]
+    for copy in copies:
+        copy.start()
+    for copy in copies:
+        copy.wait()
+
+
+def queries_kernel(q_ref, k_ref, w_ref, u_far, pa_far, pb_far, qp_ref, op_ref, u_ref, pa_ref, pb_ref, sem):
+    count = k_ref.shape[0]
+    row, col = iotas()
+    causal = row >= col
+    loads = [(u_far, u_ref), (pa_far, pa_ref), (pb_far, pb_ref)]
+    copies = [pltpu.make_async_copy(source, target, sem.at[i]) for i, (source, target) in enumerate(loads)]
+    for copy in copies:
+        copy.start()
+    blocks = range(count)
+    scores = [split(jnp.where(causal, mm_nt(q_ref[j, 0], k_ref[j]), 0.0)) for j in blocks]
+    through = [split(q_ref[j, 0].astype(f32) - product(c, w_ref[j])) for c, j in zip(scores, blocks)]
+    copies[0].wait()
+    local = [product(c, u_ref[j]) for c, j in zip(scores, blocks)]
+    for copy in copies[1:]:
+        copy.wait()
+    joint = [product_wide(t, pa_ref[j], split(pb_ref[j])) for t, j in zip(through, blocks)]
+    for j in blocks:
+        qp_ref[j] = split(joint[j][:, :HEAD_DIM])
+        op_ref[j] = joint[j][:, HEAD_DIM:] + local[j]
 
 
 def finish_kernel(qp_ref, op_ref, state_ref, gain_ref, out_ref):
@@ -243,15 +267,13 @@
 
 
 def call(kernel, name, outs, flops, kept=True, limit=24 << 20, scratch=(), in_space=None):
-    vmem = pl.BlockSpec(memory_space=pltpu.VMEM)
-    far = pl.BlockSpec(memory_space=pltpu.HBM)
-    make = pltpu.VMEM if kept else jax.ShapeDtypeStruct
+    spaces = [pltpu.VMEM if kept is True or i in (kept or ()) else pltpu.HBM for i in range(len(outs))]
     extra = {} if in_space is None else {"in_specs": [pl.BlockSpec(memory_space=s) for s in in_space]}
     return pl.pallas_call(
         kernel,
         name=name,
-        out_shape=tuple(make(s, t) for s, t in outs),
-        out_specs=tuple(vmem if kept else far for _ in outs),
+        out_shape=tuple(space(s, t) for space, (s, t) in zip(spaces, outs)),
+        out_specs=tuple(pl.BlockSpec(memory_space=space) for space in spaces),
         scratch_shapes=list(scratch),
         compiler_params=pltpu.CompilerParams(vmem_limit_bytes=limit),
         cost_estimate=pl.CostEstimate(flops=flops, bytes_accessed=4 << 20, transcendentals=0),
@@ -265,6 +287,10 @@
 
 def near(*values):
     return held(pltpu.VMEM, *values)
+
+
+def far(*values):
+    return held(pltpu.HBM, *values)
 
 
 def body(groups, lanes, queries, key_vectors, head_value_rows, out_gain):
@@ -277,18 +303,30 @@
     pair = (HEAD_DIM, 2 * HEAD_DIM)
     unit = 2 * BLOCK**3 * 4
     dma = pltpu.SemaphoreType.DMA
-    pieces_shape = (lanes, 3, BLOCK, HEAD_DIM)
-    (pieces,) = call(
-        pack_kernel, "pack", [(pieces_shape, bf16)], 0, scratch=[pltpu.VMEM((3, tokens, features), bf16), dma((3,))], in_space=[pltpu.HBM] * 3,
-    )(*held(pltpu.HBM, key_vectors, head_value_rows, queries))
-    kvq = lax.all_to_all(pieces, "lo", split_axis=0, concat_axis=0, tiled=True)
-    w, u, a, b, total = call(
-        functools.partial(maps_kernel, groups > 2), "maps",
-        [((blocks, *pair), bf16), ((blocks, *pair), bf16), ((nodes, *pair), bf16), ((nodes, *one), f32), (one, f32)],
-        unit * blocks * 20,
-    )(*near(kvq))
+
+    def to_heads(*rows):
+        count = len(rows)
+        (pieces,) = call(
+            pack_kernel, "pack", [((lanes, count, BLOCK, HEAD_DIM), bf16)], 0,
+            scratch=[pltpu.VMEM((count, tokens, features), bf16), dma((count,))], in_space=[pltpu.HBM] * count,
+        )(*far(*rows))
+        return lax.all_to_all(pieces, "lo", split_axis=0, concat_axis=0, tiled=True)
+
+    with jax.named_scope("kvmove"):
+        kv = to_heads(key_vectors, head_value_rows)
+    with jax.named_scope("qmove"):
+        q = to_heads(queries)
+    with jax.named_scope("maps"):
+        k, w, u, a, b, total = call(
+            functools.partial(maps_kernel, groups > 2), "maps",
+            [((blocks, *one), bf16), ((blocks, *pair), bf16), ((blocks, *pair), bf16),
+             ((nodes, *pair), bf16), ((nodes, *one), f32), (one, f32)],
+            unit * blocks * 20, kept=(0, 1, 3, 4, 5),
+            scratch=[pltpu.VMEM((blocks, *pair), bf16), dma((1,))],
+        )(*near(kv))
     hop = [(source, (source + 1) % groups) for source in range(groups)]
-    incoming = lax.ppermute(total, "hi", hop)
+    with jax.named_scope("hop"):
+        incoming = lax.ppermute(total, "hi", hop)
     if groups > 2:
         top = a[nodes - 1].astype(f32)
         transition = top[:, :HEAD_DIM] + top[:, HEAD_DIM:]
@@ -299,18 +337,24 @@
             return lax.ppermute(leaving, "hi", hop)
 
         incoming = lax.fori_loop(0, groups - 2, relay, incoming)
+    prefixes = [((blocks, *pair), bf16), ((blocks, *one), f32)]
+    with jax.named_scope("sweep"):
+        pa, pb = call(
+            sweep_kernel, "sweep", prefixes, unit * blocks * 2, kept=False,
+            scratch=[pltpu.VMEM((nodes, *pair), bf16), pltpu.VMEM((nodes, *one), f32), dma((2,))],
+        )(*near(a, b))
     qp, op = call(
-        queries_kernel, "queries",
-        [((blocks, *pair), bf16), ((blocks, *one), f32)],
-        unit * blocks * 6,
-        scratch=[pltpu.VMEM((nodes, *pair), bf16), pltpu.VMEM((nodes, *one), f32)],
-    )(*near(kvq, w, u, a, b))
+        queries_kernel, "queries", [((blocks, *pair), bf16), ((blocks, *one), f32)], unit * blocks * 6,
+        scratch=[pltpu.VMEM((blocks, *pair), bf16)] + [pltpu.VMEM(s, t) for s, t in prefixes] + [dma((3,))],
+        in_space=[pltpu.VMEM] * 3 + [pltpu.HBM] * 3,
+    )(*near(q, k, w), *far(u, pa, pb))
     (out,) = call(
         finish_kernel, "finish", [((blocks, BLOCK, HEAD_DIM), bf16)], unit * blocks * 2,
     )(*near(qp, op), incoming, out_gain.reshape(1, HEAD_DIM))
     back = lax.all_to_all(out, "lo", split_axis=0, concat_axis=0, tiled=True)
     (mixed,) = call(
-        unpack_kernel, "unpack", [((tokens, features), bf16)], 0, kept=False, scratch=[pltpu.VMEM((tokens, features), bf16), dma((PARTS,))],
+        unpack_kernel, "unpack", [((tokens, features), bf16)], 0, kept=False,
+        scratch=[pltpu.VMEM((tokens, features), bf16), dma((PARTS,))],
     )(*near(back))
     return mixed
 

time: 53.3 us -> 55.5 us (1.041)
  blocking collectives: 38.1 us -> 13.9 us
  waiting for transfers between devices: 2.07 us -> 12.7 us
  starting transfers between devices: 2.66 us -> 12.7 us
  Pallas kernels: 10.2 us -> 15.6 us
    all_to_all x1 -> x0, blocking collectives: 26.5 us -> none  [body(): kvq = lax.all_to_all(pieces, 'lo', split_axis=0, concat_axis=0, tiled=True)]
    all_to_all x0 -> x2, waiting for transfers between devices: none -> 12.7 us  [to_heads(): return lax.all_to_all(pieces, 'lo', split_axis=0, concat_axis=0, tiled=True)]
    all_to_all x0 -> x2, starting transfers between devices: none -> 10.1 us  [to_heads(): return lax.all_to_all(pieces, 'lo', split_axis=0, concat_axis=0, tiled=True)]
    pallas_call x2 -> x4, Pallas kernels: 6.74 us -> 11.6 us  [the longest x1 5.38 us: body(): call(functools.partial(maps_kernel, groups > 2), 'maps', [((blocks, *one)...]
    all_to_all x1, blocking collectives: 11.7 us -> 13.9 us  [body(): back = lax.all_to_all(out, 'lo', split_axis=0, concat_axis=0, tiled=True)]
    ppermute x1, waiting for transfers between devices: 2.07 us -> 0.01 us  [body(): incoming = lax.ppermute(total, 'hi', hop)]
  transfers between devices with their start and end apart: 1 -> 3, of which waited for: 1 -> 1; matrix products, arithmetic and copies ran while one was open for 0% -> 0% of each run, Pallas kernels for 4% -> 22%
where the time goes in v6:
time: 55.5 us; the launch traced here: 55.1 us
  Pallas kernels  15.6 us (28%)
  blocking collectives  13.9 us (25%)
  starting transfers between devices  12.7 us (23%)
  waiting for transfers between devices  12.7 us (23%)
    all_to_all x1, blocking collectives, body(): back = lax.all_to_all(out, 'lo', split_axis=0, concat_axis=0, tiled=True)  13.9 us
    all_to_all x2, waiting for transfers between devices, to_heads(): return lax.all_to_all(pieces, 'lo', split_axis=0, concat_axis=0, tiled=True)  12.7 us
    all_to_all x2, starting transfers between devices, to_heads(): return lax.all_to_all(pieces, 'lo', split_axis=0, concat_axis=0, tiled=True)  10.1 us
    pallas_call x1, Pallas kernels, body(): call(functools.partial(maps_kernel, groups > 2), 'maps', [((blocks, *one)...  5.38 us
    pallas_call x2, Pallas kernels, to_heads(): call(pack_kernel, 'pack', [((lanes, count, BLOCK, HEAD_DIM), bf16)], 0, s...  4.21 us
    ppermute x1, starting transfers between devices, body(): incoming = lax.ppermute(total, 'hi', hop)  2.66 us
    pallas_call x1, Pallas kernels, body(): call(queries_kernel, 'queries', [((blocks, *pair), bf16), ((blocks, *one)...  2.61 us
    pallas_call x1, Pallas kernels, body(): call(sweep_kernel, 'sweep', prefixes, unit * blocks * 2, kept=False, scra...  2.02 us
  transfers between devices with their start and end apart: 3, of which 1 were waited for; matrix products, arithmetic and copies ran while one was open for 0% of the time, Pallas kernels for 22%

profile of v6, /device:TPU:0, one launch (start us, length us, event | category | flops | bytes accessed | tf_op | source)
XLA Modules:
  0.0 55.1 jit_solution(17214445368302487883)
XLA Ops:
  0.0 2.3 %pack.3 = bf16[16,2,128,128]{3,2,1,0:T(8,128)(2,1)} custom-call(bf16[128,2048]{1,0:T(8,128)(2,1)} %refs_0_.3, bf16[128,2048]{1,0:T(8,128)(2,1)} %refs_1_.1), custom_call_target="tpu_custom_call" | custom-call | bytes 4194304 | tf_op jit(solution)/shard_map/kvmove/pack/pallas_call | solution.py:309
  2.3 6.3 %all-to-all-start.1 = ((bf16[16,2,128,128]{3,2,1,0:T(8,128)(2,1)}), bf16[16,2,128,128]{3,2,1,0:T(8,128)(2,1)S(1)}, u32[]{:S(2)}, u32[]{:S(2)}) async-start(bf16[16,2,128,128]{3,2,1,0:T(8,128)(2,1)} %pack.3), calls=%async_computation.1 | async-start | bytes 2097152 | tf_op jit(solution)/shard_map/kvmove/all_to_all | solution.py:313
  8.6 1.9 %pack.2 = bf16[16,1,128,128]{3,2,1,0:T(8,128)(2,1)} custom-call(bf16[128,2048]{1,0:T(8,128)(2,1)} %refs_0_.2), custom_call_target="tpu_custom_call" | custom-call | bytes 4194304 | tf_op jit(solution)/shard_map/qmove/pack/pallas_call | solution.py:309
  10.6 12.7 %all-to-all-done.1.kvq_ref = bf16[16,2,128,128]{3,2,1,0:T(8,128)(2,1)S(1)} async-done(((bf16[16,2,128,128]{3,2,1,0:T(8,128)(2,1)}), bf16[16,2,128,128]{3,2,1,0:T(8,128)(2,1)S(1)}, u32[]{:S(2)}, u32[]{:S(2)}) %all-to-all-start.1) | async-done | bytes 1048608 | tf_op jit(solution)/shard_map/kvmove/all_to_all | solution.py:313
  23.3 3.7 %all-to-all-start = ((bf16[16,1,128,128]{3,2,1,0:T(8,128)(2,1)}), bf16[16,1,128,128]{3,2,1,0:T(8,128)(2,1)S(1)}, u32[]{:S(2)}, u32[]{:S(2)}) async-start(bf16[16,1,128,128]{3,2,1,0:T(8,128)(2,1)} %pack.2), calls=%async_computation | async-start | bytes 1048576 | tf_op jit(solution)/shard_map/qmove/all_to_all | solution.py:313
  27.0 5.4 %maps.1 = (bf16[16,128,128]{2,1,0:T(8,128)(2,1)S(1)}, bf16[16,128,256]{2,1,0:T(8,128)(2,1)S(1)}, bf16[16,128,256]{2,1,0:T(8,128)(2,1)}, bf16[31,128,256]{2,1,0:T...) custom-call(bf16[16,2,128,128]{3,2,1,0:T(8,128)(2,1)S(1)} %all-to-all-done.1.kvq_ref), custom_call_target="tpu_custom_call" | custom-call | flops 5368709120 | bytes 4194304 | tf_op jit(solution)/shard_map/maps/maps/pallas_call | solution.py:320
  32.4 2.7 %collective-permute-start = (f32[128,128]{1,0:T(8,128)S(1)}, f32[128,128]{1,0:T(8,128)S(1)}, u32[]{:S(2)}, u32[]{:S(2)}) collective-permute-start(f32[128,128]{1,0:T(8,128)S(1)} %get-tuple-element.24), channel_id=1, source_target_pairs={{0,16},{16,0},{1,17},{17,1},{2,18},{18,2},{3,19},{19,3},{4,20},{20... | collective-permute-start | bytes 196616 | tf_op jit(solution)/shard_map/hop/ppermute | solution.py:329
  35.1 2.0 %sweep.1 = (bf16[16,128,256]{2,1,0:T(8,128)(2,1)}, f32[16,128,128]{2,1,0:T(8,128)}) custom-call(bf16[31,128,256]{2,1,0:T(8,128)(2,1)S(1)} %get-tuple-element.18.a_ref, f32[31,128,128]{2,1,0:T(8,128)S(1)} %get-tuple-element.19.b_ref), custom_call_target="tpu_custom_call" | custom-call | flops 536870912 | bytes 4194304 | tf_op jit(solution)/shard_map/sweep/sweep/pallas_call | solution.py:342
  37.1 0.0 all-to-all-done.q_ref
  37.1 0.0 copy-start
  37.1 2.6 %queries.1 = (bf16[16,128,256]{2,1,0:T(8,128)(2,1)S(1)}, f32[16,128,128]{2,1,0:T(8,128)S(1)}) custom-call(bf16[16,1,128,128]{3,2,1,0:T(8,128)(2,1)S(1)} %all-to-all-done.q_ref, bf16[16,128,128]{2,1,0:T(8,128)(2,1)S(1)} %get-tuple-element.15.k_ref, bf16[16,128,256]{2,1,0:T(8,128)(2,1)S(1)} %get-tuple-element.16.w_ref, ...), custom_call_target="tpu_custom_call" | custom-call | flops 1610612736 | bytes 4194304 | tf_op jit(solution)/shard_map/queries/pallas_call | solution.py:346
  39.7 0.0 collective-permute-done.state_ref
  39.7 0.0 copy-done
  39.7 0.6 %finish.1 = bf16[16,128,128]{2,1,0:T(8,128)(2,1)S(1)} custom-call(bf16[16,128,256]{2,1,0:T(8,128)(2,1)S(1)} %get-tuple-element.22.qp_ref, f32[16,128,128]{2,1,0:T(8,128)S(1)} %get-tuple-element.23.op_ref, f32[128,128]{1,0:T(8,128)S(1)} %collective-permute-done.state_ref, f32[1,128]{1,0:T(1,128)S(1)} %bitcast.1), custom_call_target="tpu_custom_call" | custom-call | flops 536870912 | bytes 4194304 | tf_op jit(solution)/shard_map/finish/pallas_call | solution.py:351
  40.3 13.9 %all_to_all.15.in_ref = bf16[16,128,128]{2,1,0:T(8,128)(2,1)S(1)} all-to-all(bf16[16,128,128]{2,1,0:T(8,128)(2,1)S(1)} %finish.1), channel_id=1, replica_groups=mesh['seq'=16,'grp'=2] {'seq':(2)8,'grp'}, dimensions={0} | all-to-all | bytes 1048576 | tf_op jit(solution)/shard_map/all_to_all | solution.py:354
  54.3 0.8 %unpack.1 = bf16[128,2048]{1,0:T(8,128)(2,1)} custom-call(bf16[16,128,128]{2,1,0:T(8,128)(2,1)S(1)} %all_to_all.15.in_ref), custom_call_target="tpu_custom_call" | custom-call | bytes 4194304 | tf_op jit(solution)/shard_map/unpack/pallas_call | solution.py:355
Async XLA Ops:
  2.3 21.0 %all-to-all-start.1 = ((bf16[16,2,128,128]{3,2,1,0:T(8,128)(2,1)}), bf16[16,2,128,128]{3,2,1,0:T(8,128)(2,1)S(1)}, u32[]{:S(2)}, u32[]{:S(2)}) async-start(bf16[16,2,128,128]{3,2,1,0:T(8,128)(2,1)} %pack.3), calls=%async_computation.1 | async-start | bytes 2097152 | tf_op jit(solution)/shard_map/kvmove/all_to_all | solution.py:313
  23.3 13.8 %all-to-all-start = ((bf16[16,1,128,128]{3,2,1,0:T(8,128)(2,1)}), bf16[16,1,128,128]{3,2,1,0:T(8,128)(2,1)S(1)}, u32[]{:S(2)}, u32[]{:S(2)}) async-start(bf16[16,1,128,128]{3,2,1,0:T(8,128)(2,1)} %pack.2), calls=%async_computation | async-start | bytes 1048576 | tf_op jit(solution)/shard_map/qmove/all_to_all | solution.py:313
  32.4 7.3 %collective-permute-start = (f32[128,128]{1,0:T(8,128)S(1)}, f32[128,128]{1,0:T(8,128)S(1)}, u32[]{:S(2)}, u32[]{:S(2)}) collective-permute-start(f32[128,128]{1,0:T(8,128)S(1)} %get-tuple-element.24), channel_id=1, source_target_pairs={{0,16},{16,0},{1,17},{17,1},{2,18},{18,2},{3,19},{19,3},{4,20},{20... | collective-permute-start | bytes 196616 | tf_op jit(solution)/shard_map/hop/ppermute | solution.py:329
  37.1 2.6 %copy-start = (f32[128]{0:T(128)S(1)}, f32[128]{0:T(128)}, u32[]{:S(2)}) copy-start(f32[128]{0:T(128)} %param.7) | copy-start | bytes 1540

commit v7 on v6

--- a/solution.py
+++ b/solution.py
@@ -87,15 +87,23 @@
     return offsets, at
 
 
-def pack_kernel(*refs):
-    *ins, out_ref, held_ref, sem = refs
-    copies = [pltpu.make_async_copy(ref, held_ref.at[i], sem.at[i]) for i, ref in enumerate(ins)]
+def pack_kernel(q_ref, k_ref, v_ref, kv_ref, q_far, rows_ref, moved_ref, sem):
+    ins = (q_ref, k_ref, v_ref)
+    copies = [pltpu.make_async_copy(ref, rows_ref.at[i], sem.at[i]) for i, ref in enumerate(ins)]
+    park = pltpu.make_async_copy(moved_ref, q_far, sem.at[len(ins)])
     for copy in copies:
         copy.start()
     for i, copy in enumerate(copies):
         copy.wait()
-        for h in range(out_ref.shape[0]):
-            out_ref[h, i] = held_ref[i, :, h * HEAD_DIM : (h + 1) * HEAD_DIM]
+        for h in range(kv_ref.shape[0]):
+            piece = rows_ref[i, :, h * HEAD_DIM : (h + 1) * HEAD_DIM]
+            if i == 0:
+                moved_ref[h, 0] = piece
+            else:
+                kv_ref[h, i - 1] = piece
+        if i == 0:
+            park.start()
+    park.wait()
 
 
 def unpack_kernel(in_ref, out_ref, held_ref, sem):
@@ -304,18 +312,16 @@
     unit = 2 * BLOCK**3 * 4
     dma = pltpu.SemaphoreType.DMA
 
-    def to_heads(*rows):
-        count = len(rows)
-        (pieces,) = call(
-            pack_kernel, "pack", [((lanes, count, BLOCK, HEAD_DIM), bf16)], 0,
-            scratch=[pltpu.VMEM((count, tokens, features), bf16), dma((count,))], in_space=[pltpu.HBM] * count,
-        )(*far(*rows))
-        return lax.all_to_all(pieces, "lo", split_axis=0, concat_axis=0, tiled=True)
-
+    kv_shape, q_shape = [(lanes, count, BLOCK, HEAD_DIM) for count in (2, 1)]
+    kv, q = call(
+        pack_kernel, "pack", [(kv_shape, bf16), (q_shape, bf16)], 0, kept=(0,),
+        scratch=[pltpu.VMEM((3, tokens, features), bf16), pltpu.VMEM(q_shape, bf16), dma((4,))],
+        in_space=[pltpu.HBM] * 3,
+    )(*far(queries, key_vectors, head_value_rows))
     with jax.named_scope("kvmove"):
-        kv = to_heads(key_vectors, head_value_rows)
+        kv = lax.all_to_all(kv, "lo", split_axis=0, concat_axis=0, tiled=True)
     with jax.named_scope("qmove"):
-        q = to_heads(queries)
+        q = lax.all_to_all(q, "lo", split_axis=0, concat_axis=0, tiled=True)
     with jax.named_scope("maps"):
         k, w, u, a, b, total = call(
             functools.partial(maps_kernel, groups > 2), "maps",

time: 55.5 us -> 54.8 us (0.987)
  blocking collectives: 13.9 us -> 34.7 us
  waiting for transfers between devices: 12.7 us -> 0.01 us
  starting transfers between devices: 12.7 us -> 6.23 us
  Pallas kernels: 15.6 us -> 13.4 us
    all_to_all x0 -> x1, blocking collectives: none -> 20.8 us  [body(): kv = lax.all_to_all(kv, 'lo', split_axis=0, concat_axis=0, tiled=True)]
    all_to_all x2 -> x1, waiting for transfers between devices: 12.7 us -> 0.01 us  [body(): q = lax.all_to_all(q, 'lo', split_axis=0, concat_axis=0, tiled=True)]
    all_to_all x2 -> x1, starting transfers between devices: 10.1 us -> 3.57 us  [body(): q = lax.all_to_all(q, 'lo', split_axis=0, concat_axis=0, tiled=True)]
    pallas_call x2 -> x1, Pallas kernels: 4.21 us -> 1.96 us  [body(): call(pack_kernel, 'pack', [(kv_shape, bf16), (q_shape, bf16)], 0, kept=(0...]
  transfers between devices with their start and end apart: 3 -> 2, of which waited for: 1 -> 0; matrix products, arithmetic and copies ran while one was open for 0% -> 0% of each run, Pallas kernels for 22% -> 18%
where the time goes in v7:
time: 54.8 us; the launch traced here: 54.4 us
  blocking collectives  34.7 us (63%)
  Pallas kernels  13.4 us (24%)
  starting transfers between devices  6.23 us (11%)
    all_to_all x1, blocking collectives, body(): kv = lax.all_to_all(kv, 'lo', split_axis=0, concat_axis=0, tiled=True)  20.8 us
    all_to_all x1, blocking collectives, body(): back = lax.all_to_all(out, 'lo', split_axis=0, concat_axis=0, tiled=True)  13.9 us
    pallas_call x1, Pallas kernels, body(): call(functools.partial(maps_kernel, groups > 2), 'maps', [((blocks, *one)...  5.39 us
    all_to_all x1, starting transfers between devices, body(): q = lax.all_to_all(q, 'lo', split_axis=0, concat_axis=0, tiled=True)  3.57 us
    ppermute x1, starting transfers between devices, body(): incoming = lax.ppermute(total, 'hi', hop)  2.65 us
    pallas_call x1, Pallas kernels, body(): call(queries_kernel, 'queries', [((blocks, *pair), bf16), ((blocks, *one)...  2.61 us
    pallas_call x1, Pallas kernels, body(): call(sweep_kernel, 'sweep', prefixes, unit * blocks * 2, kept=False, scra...  2.02 us
    pallas_call x1, Pallas kernels, body(): call(pack_kernel, 'pack', [(kv_shape, bf16), (q_shape, bf16)], 0, kept=(0...  1.96 us
  transfers between devices with their start and end apart: 2, of which 0 were waited for; matrix products, arithmetic and copies ran while one was open for 0% of the time, Pallas kernels for 18%

profile of v7, /device:TPU:0, one launch (start us, length us, event | category | flops | bytes accessed | tf_op | source)
XLA Modules:
  0.0 54.4 jit_solution(4061667017932062057)
XLA Ops:
  0.0 2.0 %pack.1 = (bf16[16,2,128,128]{3,2,1,0:T(8,128)(2,1)S(1)}, bf16[16,1,128,128]{3,2,1,0:T(8,128)(2,1)}) custom-call(bf16[128,2048]{1,0:T(8,128)(2,1)} %q_ref.1, bf16[128,2048]{1,0:T(8,128)(2,1)} %k_ref.1, bf16[128,2048]{1,0:T(8,128)(2,1)} %v_ref.1), custom_call_target="tpu_custom_call" | custom-call | bytes 4194304 | tf_op jit(solution)/shard_map/pack/pallas_call | solution.py:316
  2.0 20.8 %all_to_all.15.kvq_ref = bf16[16,2,128,128]{3,2,1,0:T(8,128)(2,1)S(1)} all-to-all(bf16[16,2,128,128]{3,2,1,0:T(8,128)(2,1)S(1)} %get-tuple-element.18), channel_id=1, replica_groups=mesh['seq'=16,'grp'=2] {'seq':(2)8,'grp'}, dimensions={0} | all-to-all | bytes 2097152 | tf_op jit(solution)/shard_map/kvmove/all_to_all | solution.py:322
  22.8 3.6 %all-to-all-start = ((bf16[16,1,128,128]{3,2,1,0:T(8,128)(2,1)}), bf16[16,1,128,128]{3,2,1,0:T(8,128)(2,1)S(1)}, u32[]{:S(2)}, u32[]{:S(2)}) async-start(bf16[16,1,128,128]{3,2,1,0:T(8,128)(2,1)} %get-tuple-element.17), calls=%async_computation | async-start | bytes 1048576 | tf_op jit(solution)/shard_map/qmove/all_to_all | solution.py:324
  26.4 5.4 %maps.1 = (bf16[16,128,128]{2,1,0:T(8,128)(2,1)S(1)}, bf16[16,128,256]{2,1,0:T(8,128)(2,1)S(1)}, bf16[16,128,256]{2,1,0:T(8,128)(2,1)}, bf16[31,128,256]{2,1,0:T...) custom-call(bf16[16,2,128,128]{3,2,1,0:T(8,128)(2,1)S(1)} %all_to_all.15.kvq_ref), custom_call_target="tpu_custom_call" | custom-call | flops 5368709120 | bytes 4194304 | tf_op jit(solution)/shard_map/maps/maps/pallas_call | solution.py:326
  31.8 2.7 %collective-permute-start = (f32[128,128]{1,0:T(8,128)S(1)}, f32[128,128]{1,0:T(8,128)S(1)}, u32[]{:S(2)}, u32[]{:S(2)}) collective-permute-start(f32[128,128]{1,0:T(8,128)S(1)} %get-tuple-element.28), channel_id=1, source_target_pairs={{0,16},{16,0},{1,17},{17,1},{2,18},{18,2},{3,19},{19,3},{4,20},{20... | collective-permute-start | bytes 196616 | tf_op jit(solution)/shard_map/hop/ppermute | solution.py:335
  34.4 2.0 %sweep.1 = (bf16[16,128,256]{2,1,0:T(8,128)(2,1)}, f32[16,128,128]{2,1,0:T(8,128)}) custom-call(bf16[31,128,256]{2,1,0:T(8,128)(2,1)S(1)} %get-tuple-element.22.a_ref, f32[31,128,128]{2,1,0:T(8,128)S(1)} %get-tuple-element.23.b_ref), custom_call_target="tpu_custom_call" | custom-call | flops 536870912 | bytes 4194304 | tf_op jit(solution)/shard_map/sweep/sweep/pallas_call | solution.py:348
  36.4 0.0 all-to-all-done.q_ref
  36.5 0.0 copy-start
  36.5 2.6 %queries.1 = (bf16[16,128,256]{2,1,0:T(8,128)(2,1)S(1)}, f32[16,128,128]{2,1,0:T(8,128)S(1)}) custom-call(bf16[16,1,128,128]{3,2,1,0:T(8,128)(2,1)S(1)} %all-to-all-done.q_ref, bf16[16,128,128]{2,1,0:T(8,128)(2,1)S(1)} %get-tuple-element.19.k_ref, bf16[16,128,256]{2,1,0:T(8,128)(2,1)S(1)} %get-tuple-element.20.w_ref, ...), custom_call_target="tpu_custom_call" | custom-call | flops 1610612736 | bytes 4194304 | tf_op jit(solution)/shard_map/queries/pallas_call | solution.py:352
  39.1 0.0 collective-permute-done.state_ref
  39.1 0.0 copy-done
  39.1 0.6 %finish.1 = bf16[16,128,128]{2,1,0:T(8,128)(2,1)S(1)} custom-call(bf16[16,128,256]{2,1,0:T(8,128)(2,1)S(1)} %get-tuple-element.26.qp_ref, f32[16,128,128]{2,1,0:T(8,128)S(1)} %get-tuple-element.27.op_ref, f32[128,128]{1,0:T(8,128)S(1)} %collective-permute-done.state_ref, f32[1,128]{1,0:T(1,128)S(1)} %bitcast.1), custom_call_target="tpu_custom_call" | custom-call | flops 536870912 | bytes 4194304 | tf_op jit(solution)/shard_map/finish/pallas_call | solution.py:357
  39.7 13.9 %all_to_all.16.in_ref = bf16[16,128,128]{2,1,0:T(8,128)(2,1)S(1)} all-to-all(bf16[16,128,128]{2,1,0:T(8,128)(2,1)S(1)} %finish.1), channel_id=1, replica_groups=mesh['seq'=16,'grp'=2] {'seq':(2)8,'grp'}, dimensions={0} | all-to-all | bytes 1048576 | tf_op jit(solution)/shard_map/all_to_all | solution.py:360
  53.6 0.8 %unpack.1 = bf16[128,2048]{1,0:T(8,128)(2,1)} custom-call(bf16[16,128,128]{2,1,0:T(8,128)(2,1)S(1)} %all_to_all.16.in_ref), custom_call_target="tpu_custom_call" | custom-call | bytes 4194304 | tf_op jit(solution)/shard_map/unpack/pallas_call | solution.py:361
Async XLA Ops:
  22.8 13.7 %all-to-all-start = ((bf16[16,1,128,128]{3,2,1,0:T(8,128)(2,1)}), bf16[16,1,128,128]{3,2,1,0:T(8,128)(2,1)S(1)}, u32[]{:S(2)}, u32[]{:S(2)}) async-start(bf16[16,1,128,128]{3,2,1,0:T(8,128)(2,1)} %get-tuple-element.17), calls=%async_computation | async-start | bytes 1048576 | tf_op jit(solution)/shard_map/qmove/all_to_all | solution.py:324
  31.8 7.3 %collective-permute-start = (f32[128,128]{1,0:T(8,128)S(1)}, f32[128,128]{1,0:T(8,128)S(1)}, u32[]{:S(2)}, u32[]{:S(2)}) collective-permute-start(f32[128,128]{1,0:T(8,128)S(1)} %get-tuple-element.28), channel_id=1, source_target_pairs={{0,16},{16,0},{1,17},{17,1},{2,18},{18,2},{3,19},{19,3},{4,20},{20... | collective-permute-start | bytes 196616 | tf_op jit(solution)/shard_map/hop/ppermute | solution.py:335
  36.5 2.6 %copy-start = (f32[128]{0:T(128)S(1)}, f32[128]{0:T(128)}, u32[]{:S(2)}) copy-start(f32[128]{0:T(128)} %param.7) | copy-start | bytes 1540

commit v8 on v5

--- a/solution.py
+++ b/solution.py
@@ -96,19 +96,6 @@
         copy.wait()
         for h in range(out_ref.shape[0]):
             out_ref[h, i] = held_ref[i, :, h * HEAD_DIM : (h + 1) * HEAD_DIM]
-
-
-def unpack_kernel(in_ref, out_ref, held_ref, sem):
-    size = out_ref.shape[0] // PARTS
-    copies = []
-    for i in range(PARTS):
-        rows = slice(i * size, (i + 1) * size)
-        for h in range(in_ref.shape[0]):
-            held_ref[rows, h * HEAD_DIM : (h + 1) * HEAD_DIM] = in_ref[h, rows]
-        copies.append(pltpu.make_async_copy(held_ref.at[rows], out_ref.at[rows], sem.at[i]))
-        copies[-1].start()
-    for copy in copies:
-        copy.wait()
 
 
 def base_inverses(coupling):
@@ -137,53 +124,59 @@
     ]
 
 
-def maps_kernel(climb, kvq_ref, w_ref, u_ref, a_ref, b_ref, total_ref):
-    count = kvq_ref.shape[0]
+def solve(keys, values):
+    row, col = iotas()
+    diagonal = row == col
+    grams = [mm_nt(k, k) for k in keys]
+    coupling, scale_cols, scale_rows = [], [], []
+    for g in grams:
+        on_diagonal = jnp.where(diagonal, g, 0.0)
+        c = 1.0 / jnp.sqrt(jnp.sum(on_diagonal, axis=1, keepdims=True) + key_eps)
+        r = 1.0 / jnp.sqrt(jnp.sum(on_diagonal, axis=0, keepdims=True) + key_eps)
+        scale_cols.append(c)
+        scale_rows.append(r)
+        coupling.append(jnp.where(row > col, (2.0 * c) * g * r, 0.0))
+    inverses = base_inverses(coupling)
+    size = BASE
+    while size < BLOCK:
+        mask = ((row // size) % 2 == 1) & (col // size == row // size - 1)
+        parts = [jnp.where(mask, n, 0.0) for n in coupling]
+        pairs = [split(t) for t in inverses]
+        inner = [product(split(p), t) for p, t in zip(parts, pairs)]
+        outer = [product(t, split(z)) for t, z in zip(pairs, inner)]
+        inverses = [t - z for t, z in zip(inverses, outer)]
+        size *= 2
+    lefts = [split((2.0 * c) * t) for c, t in zip(scale_cols, inverses)]
+    units = [split(k.astype(f32) * c) for k, c in zip(keys, scale_cols)]
+    firsts = [
+        mm(t, twice(jnp.concatenate([k[:, :HEAD_DIM], v], axis=1)))
+        for t, k, v in zip(lefts, units, values)
+    ]
+    rests = [mm(t[:, :HEAD_DIM], k[:, HEAD_DIM:]) for t, k in zip(lefts, units)]
+    weights = [split(f[:, :HEAD_DIM] + r) for f, r in zip(firsts, rests)]
+    changes = [split(f[:, HEAD_DIM:]) for f in firsts]
+    return weights, changes
+
+
+def maps_kernel(climb, kv_ref, a_ref, b_ref, total_ref):
+    count = kv_ref.shape[0]
     offsets, _ = node_offsets(count)
     row, col = iotas()
-    diagonal = row == col
-    eye = diagonal.astype(f32)
-
-    def run(blocks):
-        keys = [kvq_ref[j, 0] for j in blocks]
-        grams = [mm_nt(k, k) for k in keys]
-        coupling, scale_cols, scale_rows = [], [], []
-        for g in grams:
-            on_diagonal = jnp.where(diagonal, g, 0.0)
-            c = 1.0 / jnp.sqrt(jnp.sum(on_diagonal, axis=1, keepdims=True) + key_eps)
-            r = 1.0 / jnp.sqrt(jnp.sum(on_diagonal, axis=0, keepdims=True) + key_eps)
-            scale_cols.append(c)
-            scale_rows.append(r)
-            coupling.append(jnp.where(row > col, (2.0 * c) * g * r, 0.0))
-        inverses = base_inverses(coupling)
-        size = BASE
-        while size < BLOCK:
-            mask = ((row // size) % 2 == 1) & (col // size == row // size - 1)
-            parts = [jnp.where(mask, n, 0.0) for n in coupling]
-            pairs = [split(t) for t in inverses]
-            inner = [product(split(p), t) for p, t in zip(parts, pairs)]
-            outer = [product(t, split(z)) for t, z in zip(pairs, inner)]
-            inverses = [t - z for t, z in zip(inverses, outer)]
-            size *= 2
-        lefts = [(2.0 * c) * t for c, t in zip(scale_cols, inverses)]
-        weights = [split(mm(split(t * r), twice(k))) for t, r, k in zip(lefts, scale_rows, keys)]
-        changes = [split(mm(split(t), twice(kvq_ref[j, 1]))) for t, j in zip(lefts, blocks)]
-        for i, j in enumerate(blocks):
-            w_ref[j] = weights[i]
-            u_ref[j] = changes[i]
-            across = keys[i].T
-            both = mm(jnp.concatenate([across, across], axis=1), stack(weights[i], changes[i]))
-            a_ref[j] = split(eye - both[:, :HEAD_DIM])
-            b_ref[j] = both[:, HEAD_DIM:]
-
-    batches(count, run)
+    eye = (row == col).astype(f32)
+    keys = [kv_ref[j, 0] for j in range(count)]
+    weights, changes = solve(keys, [kv_ref[j, 1] for j in range(count)])
+    for j in range(count):
+        across = keys[j].T
+        both = mm(jnp.concatenate([across, across], axis=1), stack(weights[j], changes[j]))
+        a_ref[j] = split(eye - both[:, :HEAD_DIM])
+        b_ref[j] = both[:, HEAD_DIM:]
     for level in range(1, len(offsets)):
         below, here = offsets[level - 1], offsets[level]
         for i in range(count >> level):
             first, second = below + 2 * i, below + 2 * i + 1
             later = a_ref[second]
             b_ref[here + i] = product(later, split(b_ref[first])) + b_ref[second]
-            if climb or level < len(offsets) - 1:
+            if climb or (i > 0 and level < len(offsets) - 1):
                 a_ref[here + i] = split(product(later, a_ref[first]))
     total_ref[...] = b_ref[offsets[-1]]
 
@@ -201,13 +194,16 @@
     return steps
 
 
-def queries_kernel(kvq_ref, w_ref, u_ref, a_ref, b_ref, qp_ref, op_ref, pa_ref, pb_ref):
-    count = kvq_ref.shape[0]
+def sweep_kernel(a_ref, b_ref, pa_ref, pb_ref):
+    count = (a_ref.shape[0] + 1) // 2
     row, col = iotas()
-    causal = row >= col
+    offsets, _ = node_offsets(count)
+    first = {0: a_ref[0]}
+    for below, here in zip(offsets[:-2], offsets[1:-1]):
+        first[here] = split(product(a_ref[below + 1], first[below]))
     for (target, left, parent) in prefix_steps(count):
         if parent is None:
-            pa_ref[target] = split((row == col).astype(f32)) if left is None else a_ref[left]
+            pa_ref[target] = split((row == col).astype(f32)) if left is None else first[left]
             pb_ref[target] = jnp.zeros((HEAD_DIM, HEAD_DIM), f32) if left is None else b_ref[left]
         elif left is None:
             pa_ref[target] = pa_ref[parent]
@@ -216,30 +212,51 @@
             pa_ref[target] = split(product(a_ref[left], pa_ref[parent]))
             pb_ref[target] = product(a_ref[left], split(pb_ref[parent])) + b_ref[left]
 
-    def run(blocks):
-        scores = [jnp.where(causal, mm_nt(kvq_ref[j, 2], kvq_ref[j, 0]), 0.0) for j in blocks]
-        local = [product_wide(split(c), w_ref[j], u_ref[j]) for c, j in zip(scores, blocks)]
-        through = [split(kvq_ref[j, 2].astype(f32) - t[:, :HEAD_DIM]) for t, j in zip(local, blocks)]
-        joint = [product_wide(t, pa_ref[j], split(pb_ref[j])) for t, j in zip(through, blocks)]
-        for i, j in enumerate(blocks):
-            qp_ref[j] = split(joint[i][:, :HEAD_DIM])
-            op_ref[j] = joint[i][:, HEAD_DIM:] + local[i][:, HEAD_DIM:]
-
-    batches(count, run)
-
-
-def finish_kernel(qp_ref, op_ref, state_ref, gain_ref, out_ref):
+
+def states_kernel(pa_ref, pb_ref, state_ref, out_ref):
     arrived = jnp.where(lax.axis_index("hi") > 0, state_ref[...], 0.0)
     state = twice(split(arrived))
+    for j in range(out_ref.shape[0]):
+        out_ref[j] = (fold(mm(pa_ref[j], state)) + pb_ref[j]).astype(bf16)
+
+
+def local_kernel(k_far, v_far, q_far, qt_ref, ol_ref, rows_ref, sem):
+    heads = range(qt_ref.shape[0])
+    sources = (k_far, v_far, q_far)
+    copies = [pltpu.make_async_copy(ref, rows_ref.at[i], sem.at[i]) for i, ref in enumerate(sources)]
+    for copy in copies:
+        copy.start()
+    for copy in copies:
+        copy.wait()
+    keys, values, asks = [
+        [rows_ref[i, :, h * HEAD_DIM : (h + 1) * HEAD_DIM] for h in heads] for i in range(len(sources))
+    ]
+    weights, changes = solve(keys, values)
+    row, col = iotas()
+    causal = row >= col
+    scores = [split(jnp.where(causal, mm_nt(q, k), 0.0)) for q, k in zip(asks, keys)]
+    for h in heads:
+        joint = product_wide(scores[h], weights[h], changes[h])
+        qt_ref[h] = split(asks[h].astype(f32) - joint[:, :HEAD_DIM])
+        ol_ref[h] = joint[:, HEAD_DIM:]
+
+
+def final_kernel(qt_ref, ol_ref, state_ref, gain_ref, out_far, rows_ref, sem):
+    heads = qt_ref.shape[0]
     gain = gain_ref[...]
-
-    def run(blocks):
-        outputs = [fold(mm(qp_ref[j], state)) + op_ref[j] for j in blocks]
-        for j, output in zip(blocks, outputs):
-            scale = lax.rsqrt(jnp.mean(output * output, axis=1, keepdims=True) + norm_eps)
-            out_ref[j] = (output * scale * gain).astype(bf16)
-
-    batches(out_ref.shape[0], run)
+    width = heads // PARTS * HEAD_DIM
+    copies = []
+    for h in range(heads):
+        output = mm(qt_ref[h], twice(state_ref[h])) + ol_ref[h]
+        scale = lax.rsqrt(jnp.mean(output * output, axis=1, keepdims=True) + norm_eps)
+        rows_ref[:, h * HEAD_DIM : (h + 1) * HEAD_DIM] = (output * scale * gain).astype(bf16)
+        if (h + 1) % (heads // PARTS) == 0:
+            i = h // (heads // PARTS)
+            part = pl.ds(i * width, width)
+            copies.append(pltpu.make_async_copy(rows_ref.at[:, part], out_far.at[:, part], sem.at[i]))
+            copies[-1].start()
+    for copy in copies:
+        copy.wait()
 
 
 def call(kernel, name, outs, flops, kept=True, limit=24 << 20, scratch=(), in_space=None):
@@ -277,16 +294,15 @@
     pair = (HEAD_DIM, 2 * HEAD_DIM)
     unit = 2 * BLOCK**3 * 4
     dma = pltpu.SemaphoreType.DMA
-    pieces_shape = (lanes, 3, BLOCK, HEAD_DIM)
     (pieces,) = call(
-        pack_kernel, "pack", [(pieces_shape, bf16)], 0, scratch=[pltpu.VMEM((3, tokens, features), bf16), dma((3,))], in_space=[pltpu.HBM] * 3,
-    )(*held(pltpu.HBM, key_vectors, head_value_rows, queries))
-    kvq = lax.all_to_all(pieces, "lo", split_axis=0, concat_axis=0, tiled=True)
-    w, u, a, b, total = call(
+        pack_kernel, "pack", [((lanes, 2, BLOCK, HEAD_DIM), bf16)], 0,
+        scratch=[pltpu.VMEM((2, tokens, features), bf16), dma((2,))], in_space=[pltpu.HBM] * 2,
+    )(*held(pltpu.HBM, key_vectors, head_value_rows))
+    kv = lax.all_to_all(pieces, "lo", split_axis=0, concat_axis=0, tiled=True)
+    a, b, total = call(
         functools.partial(maps_kernel, groups > 2), "maps",
-        [((blocks, *pair), bf16), ((blocks, *pair), bf16), ((nodes, *pair), bf16), ((nodes, *one), f32), (one, f32)],
-        unit * blocks * 20,
-    )(*near(kvq))
+        [((nodes, *pair), bf16), ((nodes, *one), f32), (one, f32)], unit * blocks * 20,
+    )(*near(kv))
     hop = [(source, (source + 1) % groups) for source in range(groups)]
     incoming = lax.ppermute(total, "hi", hop)
     if groups > 2:
@@ -299,19 +315,24 @@
             return lax.ppermute(leaving, "hi", hop)
 
         incoming = lax.fori_loop(0, groups - 2, relay, incoming)
-    qp, op = call(
-        queries_kernel, "queries",
-        [((blocks, *pair), bf16), ((blocks, *one), f32)],
-        unit * blocks * 6,
-        scratch=[pltpu.VMEM((nodes, *pair), bf16), pltpu.VMEM((nodes, *one), f32)],
-    )(*near(kvq, w, u, a, b))
-    (out,) = call(
-        finish_kernel, "finish", [((blocks, BLOCK, HEAD_DIM), bf16)], unit * blocks * 2,
-    )(*near(qp, op), incoming, out_gain.reshape(1, HEAD_DIM))
-    back = lax.all_to_all(out, "lo", split_axis=0, concat_axis=0, tiled=True)
+    pa, pb = call(
+        sweep_kernel, "sweep", [((nodes, *pair), bf16), ((nodes, *one), f32)], unit * blocks * 2,
+    )(*near(a, b))
+    (states,) = call(
+        states_kernel, "states", [((blocks, *one), bf16)], unit * blocks,
+    )(*near(pa, pb), incoming)
+    states, queries, key_vectors, head_value_rows = lax.optimization_barrier(
+        (states, queries, key_vectors, head_value_rows)
+    )
+    back = lax.all_to_all(states, "lo", split_axis=0, concat_axis=0, tiled=True)
+    qt, ol = call(
+        local_kernel, "local", [((lanes, *pair), bf16), ((lanes, *one), f32)], unit * blocks * 20,
+        scratch=[pltpu.VMEM((3, tokens, features), bf16), dma((3,))], in_space=[pltpu.HBM] * 3,
+    )(*held(pltpu.HBM, key_vectors, head_value_rows, queries))
     (mixed,) = call(
-        unpack_kernel, "unpack", [((tokens, features), bf16)], 0, kept=False, scratch=[pltpu.VMEM((tokens, features), bf16), dma((PARTS,))],
-    )(*near(back))
+        final_kernel, "final", [((tokens, features), bf16)], unit * blocks, kept=False,
+        scratch=[pltpu.VMEM((tokens, features), bf16), dma((PARTS,))],
+    )(*near(qt, ol, back), out_gain.reshape(1, HEAD_DIM))
     return mixed
 
 

time: 53.3 us -> 49.7 us (0.932)
  blocking collectives: 38.1 us -> 20.8 us
  Pallas kernels: 10.2 us -> 16.6 us
  starting transfers between devices: 2.66 us -> 6.41 us
  waiting for transfers between devices: 2.07 us -> 5.26 us
    all_to_all x2 -> x1, blocking collectives: 38.1 us -> 20.8 us  [body(): kv = lax.all_to_all(pieces, 'lo', split_axis=0, concat_axis=0, tiled=True)]
    pallas_call x5 -> x6, Pallas kernels: 10.2 us -> 16.6 us  [the longest x1 6.53 us: body(): call(local_kernel, 'local', [((lanes, *pair), bf16), ((lanes, *one), f32)...]
    all_to_all x0 -> x1, starting transfers between devices: none -> 3.75 us  [body(): back = lax.all_to_all(states, 'lo', split_axis=0, concat_axis=0, tiled=True)]
    all_to_all x0 -> x1, waiting for transfers between devices: none -> 2.28 us  [body(): back = lax.all_to_all(states, 'lo', split_axis=0, concat_axis=0, tiled=True)]
    ppermute x1, waiting for transfers between devices: 2.07 us -> 2.98 us  [body(): incoming = lax.ppermute(total, 'hi', hop)]
  transfers between devices with their start and end apart: 1 -> 2, of which waited for: 1 -> 2; matrix products, arithmetic and copies ran while one was open for 0% -> 0% of each run, Pallas kernels for 4% -> 16%
where the time goes in v8:
time: 49.7 us; the launch traced here: 49.4 us
  blocking collectives  20.8 us (42%)
  Pallas kernels  16.6 us (33%)
  starting transfers between devices  6.41 us (13%)
  waiting for transfers between devices  5.26 us (11%)
    all_to_all x1, blocking collectives, body(): kv = lax.all_to_all(pieces, 'lo', split_axis=0, concat_axis=0, tiled=True)  20.8 us
    pallas_call x1, Pallas kernels, body(): call(local_kernel, 'local', [((lanes, *pair), bf16), ((lanes, *one), f32)...  6.53 us
    pallas_call x1, Pallas kernels, body(): call(functools.partial(maps_kernel, groups > 2), 'maps', [((nodes, *pair)...  5.14 us
    all_to_all x1, starting transfers between devices, body(): back = lax.all_to_all(states, 'lo', split_axis=0, concat_axis=0, tiled=True)  3.75 us
    ppermute x1, waiting for transfers between devices, body(): incoming = lax.ppermute(total, 'hi', hop)  2.98 us
    ppermute x1, starting transfers between devices, body(): incoming = lax.ppermute(total, 'hi', hop)  2.66 us
    all_to_all x1, waiting for transfers between devices, body(): back = lax.all_to_all(states, 'lo', split_axis=0, concat_axis=0, tiled=True)  2.28 us
    pallas_call x1, Pallas kernels, body(): call(pack_kernel, 'pack', [((lanes, 2, BLOCK, HEAD_DIM), bf16)], 0, scrat...  1.31 us
  transfers between devices with their start and end apart: 2, of which 2 were waited for; matrix products, arithmetic and copies ran while one was open for 0% of the time, Pallas kernels for 16%

profile of v8, /device:TPU:0, one launch (start us, length us, event | category | flops | bytes accessed | tf_op | source)
XLA Modules:
  0.0 49.4 jit_solution(7772861388179233943)
XLA Ops:
  0.0 1.3 %pack.1 = bf16[16,2,128,128]{3,2,1,0:T(8,128)(2,1)S(1)} custom-call(bf16[128,2048]{1,0:T(8,128)(2,1)} %k_far, bf16[128,2048]{1,0:T(8,128)(2,1)} %v_far), custom_call_target="tpu_custom_call" | custom-call | bytes 4194304 | tf_op jit(solution)/shard_map/pack/pallas_call | solution.py:297
  1.3 20.8 %all_to_all.10.kv_ref = bf16[16,2,128,128]{3,2,1,0:T(8,128)(2,1)S(1)} all-to-all(bf16[16,2,128,128]{3,2,1,0:T(8,128)(2,1)S(1)} %pack.1), channel_id=1, replica_groups=mesh['seq'=16,'grp'=2] {'seq':(2)8,'grp'}, dimensions={0} | all-to-all | bytes 2097152 | tf_op jit(solution)/shard_map/all_to_all | solution.py:301
  22.1 5.1 %maps.1 = (bf16[31,128,256]{2,1,0:T(8,128)(2,1)S(1)}, f32[31,128,128]{2,1,0:T(8,128)S(1)}, f32[128,128]{1,0:T(8,128)S(1)}) custom-call(bf16[16,2,128,128]{3,2,1,0:T(8,128)(2,1)S(1)} %all_to_all.10.kv_ref), custom_call_target="tpu_custom_call" | custom-call | flops 5368709120 | bytes 4194304 | tf_op jit(solution)/shard_map/maps/pallas_call | solution.py:302
  27.3 2.7 %collective-permute-start = (f32[128,128]{1,0:T(8,128)S(1)}, f32[128,128]{1,0:T(8,128)S(1)}, u32[]{:S(2)}, u32[]{:S(2)}) collective-permute-start(f32[128,128]{1,0:T(8,128)S(1)} %get-tuple-element.20), channel_id=1, source_target_pairs={{0,16},{16,0},{1,17},{17,1},{2,18},{18,2},{3,19},{19,3},{4,20},{20... | collective-permute-start | bytes 196616 | tf_op jit(solution)/shard_map/ppermute | solution.py:307
  29.9 1.2 %sweep.1 = (bf16[31,128,256]{2,1,0:T(8,128)(2,1)S(1)}, f32[31,128,128]{2,1,0:T(8,128)S(1)}) custom-call(bf16[31,128,256]{2,1,0:T(8,128)(2,1)S(1)} %get-tuple-element.16.a_ref, f32[31,128,128]{2,1,0:T(8,128)S(1)} %get-tuple-element.17.b_ref), custom_call_target="tpu_custom_call" | custom-call | flops 536870912 | bytes 4194304 | tf_op jit(solution)/shard_map/sweep/pallas_call | solution.py:318
  31.1 3.0 %collective-permute-done.state_ref = f32[128,128]{1,0:T(8,128)S(1)} collective-permute-done((f32[128,128]{1,0:T(8,128)S(1)}, f32[128,128]{1,0:T(8,128)S(1)}, u32[]{:S(2)}, u32[]{:S(2)}) %collective-permute-start) | collective-permute-done | bytes 65568 | tf_op jit(solution)/shard_map/ppermute | solution.py:307
  34.1 1.3 %states.1 = bf16[16,128,128]{2,1,0:T(8,128)(2,1)} custom-call(bf16[31,128,256]{2,1,0:T(8,128)(2,1)S(1)} %get-tuple-element.18.pa_ref, f32[31,128,128]{2,1,0:T(8,128)S(1)} %get-tuple-element.19.pb_ref, f32[128,128]{1,0:T(8,128)S(1)} %collective-permute-done.state_ref), custom_call_target="tpu_custom_call" | custom-call | flops 268435456 | bytes 4194304 | tf_op jit(solution)/shard_map/states/pallas_call | solution.py:321
  35.4 3.8 %all-to-all-start.1 = ((bf16[16,128,128]{2,1,0:T(8,128)(2,1)}), bf16[16,128,128]{2,1,0:T(8,128)(2,1)S(1)}, u32[]{:S(2)}, u32[]{:S(2)}) async-start(bf16[16,128,128]{2,1,0:T(8,128)(2,1)} %states.1), calls=%async_computation.1 | async-start | bytes 1048576 | tf_op jit(solution)/shard_map/all_to_all | solution.py:327
  39.1 0.0 copy-start
  39.1 6.5 %local.1 = (bf16[16,128,256]{2,1,0:T(8,128)(2,1)S(1)}, f32[16,128,128]{2,1,0:T(8,128)S(1)}) custom-call(bf16[128,2048]{1,0:T(8,128)(2,1)} %k_far, bf16[128,2048]{1,0:T(8,128)(2,1)} %v_far, bf16[128,2048]{1,0:T(8,128)(2,1)} %q_far), custom_call_target="tpu_custom_call" | custom-call | flops 5368709120 | bytes 4194304 | tf_op jit(solution)/shard_map/local/pallas_call | solution.py:328
  45.7 2.3 %all-to-all-done.1.state_ref = bf16[16,128,128]{2,1,0:T(8,128)(2,1)S(1)} async-done(((bf16[16,128,128]{2,1,0:T(8,128)(2,1)}), bf16[16,128,128]{2,1,0:T(8,128)(2,1)S(1)}, u32[]{:S(2)}, u32[]{:S(2)}) %all-to-all-start.1) | async-done | bytes 524320 | tf_op jit(solution)/shard_map/all_to_all | solution.py:327
  48.0 0.0 copy-done
  48.0 1.2 %final.1 = bf16[128,2048]{1,0:T(8,128)(2,1)} custom-call(bf16[16,128,256]{2,1,0:T(8,128)(2,1)S(1)} %get-tuple-element.24.qt_ref, f32[16,128,128]{2,1,0:T(8,128)S(1)} %get-tuple-element.25.ol_ref, bf16[16,128,128]{2,1,0:T(8,128)(2,1)S(1)} %all-to-all-done.1.state_ref, f32[1,128]{1,0:T(1,128)S(1)} %bitcast.1), custom_call_target="tpu_custom_call" | custom-call | flops 268435456 | bytes 4194304 | tf_op jit(solution)/shard_map/final/pallas_call | solution.py:332
Async XLA Ops:
  27.3 6.8 %collective-permute-start = (f32[128,128]{1,0:T(8,128)S(1)}, f32[128,128]{1,0:T(8,128)S(1)}, u32[]{:S(2)}, u32[]{:S(2)}) collective-permute-start(f32[128,128]{1,0:T(8,128)S(1)} %get-tuple-element.20), channel_id=1, source_target_pairs={{0,16},{16,0},{1,17},{17,1},{2,18},{18,2},{3,19},{19,3},{4,20},{20... | collective-permute-start | bytes 196616 | tf_op jit(solution)/shard_map/ppermute | solution.py:307
  35.4 12.6 %all-to-all-start.1 = ((bf16[16,128,128]{2,1,0:T(8,128)(2,1)}), bf16[16,128,128]{2,1,0:T(8,128)(2,1)S(1)}, u32[]{:S(2)}, u32[]{:S(2)}) async-start(bf16[16,128,128]{2,1,0:T(8,128)(2,1)} %states.1), calls=%async_computation.1 | async-start | bytes 1048576 | tf_op jit(solution)/shard_map/all_to_all | solution.py:327
  39.1 8.8 %copy-start = (f32[128]{0:T(128)S(1)}, f32[128]{0:T(128)}, u32[]{:S(2)}) copy-start(f32[128]{0:T(128)} %param.7) | copy-start | bytes 1540

commit v9 on v8

--- a/solution.py
+++ b/solution.py
@@ -178,7 +178,7 @@
             b_ref[here + i] = product(later, split(b_ref[first])) + b_ref[second]
             if climb or (i > 0 and level < len(offsets) - 1):
                 a_ref[here + i] = split(product(later, a_ref[first]))
-    total_ref[...] = b_ref[offsets[-1]]
+    total_ref[...] = b_ref[offsets[-1]].astype(total_ref.dtype)
 
 
 def prefix_steps(count):
@@ -214,7 +214,7 @@
 
 
 def states_kernel(pa_ref, pb_ref, state_ref, out_ref):
-    arrived = jnp.where(lax.axis_index("hi") > 0, state_ref[...], 0.0)
+    arrived = jnp.where(lax.axis_index("hi") > 0, state_ref[...].astype(f32), 0.0)
     state = twice(split(arrived))
     for j in range(out_ref.shape[0]):
         out_ref[j] = (fold(mm(pa_ref[j], state)) + pb_ref[j]).astype(bf16)
@@ -301,7 +301,7 @@
     kv = lax.all_to_all(pieces, "lo", split_axis=0, concat_axis=0, tiled=True)
     a, b, total = call(
         functools.partial(maps_kernel, groups > 2), "maps",
-        [((nodes, *pair), bf16), ((nodes, *one), f32), (one, f32)], unit * blocks * 20,
+        [((nodes, *pair), bf16), ((nodes, *one), f32), (one, bf16 if groups == 2 else f32)], unit * blocks * 20,
     )(*near(kv))
     hop = [(source, (source + 1) % groups) for source in range(groups)]
     incoming = lax.ppermute(total, "hi", hop)

time: 49.7 us -> 48.2 us (0.970)
  waiting for transfers between devices: 5.26 us -> 3.86 us
    ppermute x1, waiting for transfers between devices: 2.98 us -> 1.58 us  [body(): incoming = lax.ppermute(total, 'hi', hop)]
where the time goes in v9:
time: 48.2 us; the launch traced here: 47.9 us
  blocking collectives  20.8 us (43%)
  Pallas kernels  16.6 us (34%)
  starting transfers between devices  6.41 us (13%)
  waiting for transfers between devices  3.86 us (8%)
    all_to_all x1, blocking collectives, body(): kv = lax.all_to_all(pieces, 'lo', split_axis=0, concat_axis=0, tiled=True)  20.8 us
    pallas_call x1, Pallas kernels, body(): call(local_kernel, 'local', [((lanes, *pair), bf16), ((lanes, *one), f32)...  6.53 us
    pallas_call x1, Pallas kernels, body(): call(functools.partial(maps_kernel, groups > 2), 'maps', [((nodes, *pair)...  5.14 us
    all_to_all x1, starting transfers between devices, body(): back = lax.all_to_all(states, 'lo', split_axis=0, concat_axis=0, tiled=True)  3.75 us
    ppermute x1, starting transfers between devices, body(): incoming = lax.ppermute(total, 'hi', hop)  2.66 us
    all_to_all x1, waiting for transfers between devices, body(): back = lax.all_to_all(states, 'lo', split_axis=0, concat_axis=0, tiled=True)  2.28 us
    ppermute x1, waiting for transfers between devices, body(): incoming = lax.ppermute(total, 'hi', hop)  1.58 us
    pallas_call x1, Pallas kernels, body(): call(pack_kernel, 'pack', [((lanes, 2, BLOCK, HEAD_DIM), bf16)], 0, scrat...  1.31 us
  transfers between devices with their start and end apart: 2, of which 2 were waited for; matrix products, arithmetic and copies ran while one was open for 0% of the time, Pallas kernels for 16%

profile of v9, /device:TPU:0, one launch (start us, length us, event | category | flops | bytes accessed | tf_op | source)
XLA Modules:
  0.0 47.9 jit_solution(3883797353077124532)
XLA Ops:
  0.0 1.3 %pack.1 = bf16[16,2,128,128]{3,2,1,0:T(8,128)(2,1)S(1)} custom-call(bf16[128,2048]{1,0:T(8,128)(2,1)} %k_far, bf16[128,2048]{1,0:T(8,128)(2,1)} %v_far), custom_call_target="tpu_custom_call" | custom-call | bytes 4194304 | tf_op jit(solution)/shard_map/pack/pallas_call | solution.py:297
  1.3 20.8 %all_to_all.10.kv_ref = bf16[16,2,128,128]{3,2,1,0:T(8,128)(2,1)S(1)} all-to-all(bf16[16,2,128,128]{3,2,1,0:T(8,128)(2,1)S(1)} %pack.1), channel_id=1, replica_groups=mesh['seq'=16,'grp'=2] {'seq':(2)8,'grp'}, dimensions={0} | all-to-all | bytes 2097152 | tf_op jit(solution)/shard_map/all_to_all | solution.py:301
  22.1 5.1 %maps.1 = (bf16[31,128,256]{2,1,0:T(8,128)(2,1)S(1)}, f32[31,128,128]{2,1,0:T(8,128)S(1)}, bf16[128,128]{1,0:T(8,128)(2,1)S(1)}) custom-call(bf16[16,2,128,128]{3,2,1,0:T(8,128)(2,1)S(1)} %all_to_all.10.kv_ref), custom_call_target="tpu_custom_call" | custom-call | flops 5368709120 | bytes 4194304 | tf_op jit(solution)/shard_map/maps/pallas_call | solution.py:302
  27.3 2.7 %collective-permute-start = (bf16[128,128]{1,0:T(8,128)(2,1)S(1)}, bf16[128,128]{1,0:T(8,128)(2,1)S(1)}, u32[]{:S(2)}, u32[]{:S(2)}) collective-permute-start(bf16[128,128]{1,0:T(8,128)(2,1)S(1)} %get-tuple-element.20), channel_id=1, source_target_pairs={{0,16},{16,0},{1,17},{17,1},{2,18},{18,2},{3,19},{19,3},{4,20},{20... | collective-permute-start | bytes 98312 | tf_op jit(solution)/shard_map/ppermute | solution.py:307
  29.9 1.2 %sweep.1 = (bf16[31,128,256]{2,1,0:T(8,128)(2,1)S(1)}, f32[31,128,128]{2,1,0:T(8,128)S(1)}) custom-call(bf16[31,128,256]{2,1,0:T(8,128)(2,1)S(1)} %get-tuple-element.16.a_ref, f32[31,128,128]{2,1,0:T(8,128)S(1)} %get-tuple-element.17.b_ref), custom_call_target="tpu_custom_call" | custom-call | flops 536870912 | bytes 4194304 | tf_op jit(solution)/shard_map/sweep/pallas_call | solution.py:318
  31.1 1.6 %collective-permute-done.state_ref = bf16[128,128]{1,0:T(8,128)(2,1)S(1)} collective-permute-done((bf16[128,128]{1,0:T(8,128)(2,1)S(1)}, bf16[128,128]{1,0:T(8,128)(2,1)S(1)}, u32[]{:S(2)}, u32[]{:S(2)}) %collective-permute-start) | collective-permute-done | bytes 32800 | tf_op jit(solution)/shard_map/ppermute | solution.py:307
  32.7 1.3 %states.1 = bf16[16,128,128]{2,1,0:T(8,128)(2,1)} custom-call(bf16[31,128,256]{2,1,0:T(8,128)(2,1)S(1)} %get-tuple-element.18.pa_ref, f32[31,128,128]{2,1,0:T(8,128)S(1)} %get-tuple-element.19.pb_ref, bf16[128,128]{1,0:T(8,128)(2,1)S(1)} %collective-permute-done.state_ref), custom_call_target="tpu_custom_call" | custom-call | flops 268435456 | bytes 4194304 | tf_op jit(solution)/shard_map/states/pallas_call | solution.py:321
  34.0 3.8 %all-to-all-start.1 = ((bf16[16,128,128]{2,1,0:T(8,128)(2,1)}), bf16[16,128,128]{2,1,0:T(8,128)(2,1)S(1)}, u32[]{:S(2)}, u32[]{:S(2)}) async-start(bf16[16,128,128]{2,1,0:T(8,128)(2,1)} %states.1), calls=%async_computation.1 | async-start | bytes 1048576 | tf_op jit(solution)/shard_map/all_to_all | solution.py:327
  37.7 0.0 copy-start
  37.7 6.5 %local.1 = (bf16[16,128,256]{2,1,0:T(8,128)(2,1)S(1)}, f32[16,128,128]{2,1,0:T(8,128)S(1)}) custom-call(bf16[128,2048]{1,0:T(8,128)(2,1)} %k_far, bf16[128,2048]{1,0:T(8,128)(2,1)} %v_far, bf16[128,2048]{1,0:T(8,128)(2,1)} %q_far), custom_call_target="tpu_custom_call" | custom-call | flops 5368709120 | bytes 4194304 | tf_op jit(solution)/shard_map/local/pallas_call | solution.py:328
  44.3 2.3 %all-to-all-done.1.state_ref = bf16[16,128,128]{2,1,0:T(8,128)(2,1)S(1)} async-done(((bf16[16,128,128]{2,1,0:T(8,128)(2,1)}), bf16[16,128,128]{2,1,0:T(8,128)(2,1)S(1)}, u32[]{:S(2)}, u32[]{:S(2)}) %all-to-all-start.1) | async-done | bytes 524320 | tf_op jit(solution)/shard_map/all_to_all | solution.py:327
  46.6 0.0 copy-done
  46.6 1.2 %final.1 = bf16[128,2048]{1,0:T(8,128)(2,1)} custom-call(bf16[16,128,256]{2,1,0:T(8,128)(2,1)S(1)} %get-tuple-element.24.qt_ref, f32[16,128,128]{2,1,0:T(8,128)S(1)} %get-tuple-element.25.ol_ref, bf16[16,128,128]{2,1,0:T(8,128)(2,1)S(1)} %all-to-all-done.1.state_ref, f32[1,128]{1,0:T(1,128)S(1)} %bitcast.1), custom_call_target="tpu_custom_call" | custom-call | flops 268435456 | bytes 4194304 | tf_op jit(solution)/shard_map/final/pallas_call | solution.py:332
Async XLA Ops:
  27.3 5.4 %collective-permute-start = (bf16[128,128]{1,0:T(8,128)(2,1)S(1)}, bf16[128,128]{1,0:T(8,128)(2,1)S(1)}, u32[]{:S(2)}, u32[]{:S(2)}) collective-permute-start(bf16[128,128]{1,0:T(8,128)(2,1)S(1)} %get-tuple-element.20), channel_id=1, source_target_pairs={{0,16},{16,0},{1,17},{17,1},{2,18},{18,2},{3,19},{19,3},{4,20},{20... | collective-permute-start | bytes 98312 | tf_op jit(solution)/shard_map/ppermute | solution.py:307
  34.0 12.6 %all-to-all-start.1 = ((bf16[16,128,128]{2,1,0:T(8,128)(2,1)}), bf16[16,128,128]{2,1,0:T(8,128)(2,1)S(1)}, u32[]{:S(2)}, u32[]{:S(2)}) async-start(bf16[16,128,128]{2,1,0:T(8,128)(2,1)} %states.1), calls=%async_computation.1 | async-start | bytes 1048576 | tf_op jit(solution)/shard_map/all_to_all | solution.py:327
  37.7 8.8 %copy-start = (f32[128]{0:T(128)S(1)}, f32[128]{0:T(128)}, u32[]{:S(2)}) copy-start(f32[128]{0:T(128)} %param.7) | copy-start | bytes 1540

commit v10 on v9

--- a/solution.py
+++ b/solution.py
@@ -213,11 +213,22 @@
             pb_ref[target] = product(a_ref[left], split(pb_ref[parent])) + b_ref[left]
 
 
-def states_kernel(pa_ref, pb_ref, state_ref, out_ref):
+def states_kernel(pa_ref, pb_ref, state_ref, out_far, rows_ref, sem):
     arrived = jnp.where(lax.axis_index("hi") > 0, state_ref[...].astype(f32), 0.0)
-    state = twice(split(arrived))
-    for j in range(out_ref.shape[0]):
-        out_ref[j] = (fold(mm(pa_ref[j], state)) + pb_ref[j]).astype(bf16)
+    exact = state_ref.dtype == bf16
+    state = twice(arrived.astype(bf16) if exact else split(arrived))
+    count = rows_ref.shape[0]
+    size = count // PARTS
+    copies = []
+    for j in range(count):
+        moved = mm(pa_ref[j], state)
+        rows_ref[j] = ((moved if exact else fold(moved)) + pb_ref[j]).astype(bf16)
+        if (j + 1) % size == 0:
+            part = pl.ds(j + 1 - size, size)
+            copies.append(pltpu.make_async_copy(rows_ref.at[part], out_far.at[part], sem.at[len(copies)]))
+            copies[-1].start()
+    for copy in copies:
+        copy.wait()
 
 
 def local_kernel(k_far, v_far, q_far, qt_ref, ol_ref, rows_ref, sem):
@@ -319,7 +330,8 @@
         sweep_kernel, "sweep", [((nodes, *pair), bf16), ((nodes, *one), f32)], unit * blocks * 2,
     )(*near(a, b))
     (states,) = call(
-        states_kernel, "states", [((blocks, *one), bf16)], unit * blocks,
+        states_kernel, "states", [((blocks, *one), bf16)], unit * blocks, kept=False,
+        scratch=[pltpu.VMEM((blocks, *one), bf16), dma((PARTS,))],
     )(*near(pa, pb), incoming)
     states, queries, key_vectors, head_value_rows = lax.optimization_barrier(
         (states, queries, key_vectors, head_value_rows)

time: 48.2 us -> 48.1 us (level)
  no operation moved by 1% of the time
where the time goes in v10:
time: 48.1 us; the launch traced here: 47.8 us
  blocking collectives  20.8 us (43%)
  Pallas kernels  16.5 us (34%)
  starting transfers between devices  6.42 us (13%)
  waiting for transfers between devices  3.86 us (8%)
    all_to_all x1, blocking collectives, body(): kv = lax.all_to_all(pieces, 'lo', split_axis=0, concat_axis=0, tiled=True)  20.8 us
    pallas_call x1, Pallas kernels, body(): call(local_kernel, 'local', [((lanes, *pair), bf16), ((lanes, *one), f32)...  6.53 us
    pallas_call x1, Pallas kernels, body(): call(functools.partial(maps_kernel, groups > 2), 'maps', [((nodes, *pair)...  5.14 us
    all_to_all x1, starting transfers between devices, body(): back = lax.all_to_all(states, 'lo', split_axis=0, concat_axis=0, tiled=True)  3.77 us
    ppermute x1, starting transfers between devices, body(): incoming = lax.ppermute(total, 'hi', hop)  2.66 us
    all_to_all x1, waiting for transfers between devices, body(): back = lax.all_to_all(states, 'lo', split_axis=0, concat_axis=0, tiled=True)  2.28 us
    ppermute x1, waiting for transfers between devices, body(): incoming = lax.ppermute(total, 'hi', hop)  1.58 us
    pallas_call x1, Pallas kernels, body(): call(pack_kernel, 'pack', [((lanes, 2, BLOCK, HEAD_DIM), bf16)], 0, scrat...  1.31 us
  transfers between devices with their start and end apart: 2, of which 2 were waited for; matrix products, arithmetic and copies ran while one was open for 0% of the time, Pallas kernels for 16%

profile of v10, /device:TPU:0, one launch (start us, length us, event | category | flops | bytes accessed | tf_op | source)
XLA Modules:
  0.0 47.8 jit_solution(10130134930101626339)
XLA Ops:
  0.0 1.3 %pack.1 = bf16[16,2,128,128]{3,2,1,0:T(8,128)(2,1)S(1)} custom-call(bf16[128,2048]{1,0:T(8,128)(2,1)} %k_far, bf16[128,2048]{1,0:T(8,128)(2,1)} %v_far), custom_call_target="tpu_custom_call" | custom-call | bytes 4194304 | tf_op jit(solution)/shard_map/pack/pallas_call | solution.py:308
  1.3 20.8 %all_to_all.10.kv_ref = bf16[16,2,128,128]{3,2,1,0:T(8,128)(2,1)S(1)} all-to-all(bf16[16,2,128,128]{3,2,1,0:T(8,128)(2,1)S(1)} %pack.1), channel_id=1, replica_groups=mesh['seq'=16,'grp'=2] {'seq':(2)8,'grp'}, dimensions={0} | all-to-all | bytes 2097152 | tf_op jit(solution)/shard_map/all_to_all | solution.py:312
  22.1 5.1 %maps.1 = (bf16[31,128,256]{2,1,0:T(8,128)(2,1)S(1)}, f32[31,128,128]{2,1,0:T(8,128)S(1)}, bf16[128,128]{1,0:T(8,128)(2,1)S(1)}) custom-call(bf16[16,2,128,128]{3,2,1,0:T(8,128)(2,1)S(1)} %all_to_all.10.kv_ref), custom_call_target="tpu_custom_call" | custom-call | flops 5368709120 | bytes 4194304 | tf_op jit(solution)/shard_map/maps/pallas_call | solution.py:313
  27.3 2.7 %collective-permute-start = (bf16[128,128]{1,0:T(8,128)(2,1)S(1)}, bf16[128,128]{1,0:T(8,128)(2,1)S(1)}, u32[]{:S(2)}, u32[]{:S(2)}) collective-permute-start(bf16[128,128]{1,0:T(8,128)(2,1)S(1)} %get-tuple-element.20), channel_id=1, source_target_pairs={{0,16},{16,0},{1,17},{17,1},{2,18},{18,2},{3,19},{19,3},{4,20},{20... | collective-permute-start | bytes 98312 | tf_op jit(solution)/shard_map/ppermute | solution.py:318
  29.9 1.2 %sweep.1 = (bf16[31,128,256]{2,1,0:T(8,128)(2,1)S(1)}, f32[31,128,128]{2,1,0:T(8,128)S(1)}) custom-call(bf16[31,128,256]{2,1,0:T(8,128)(2,1)S(1)} %get-tuple-element.16.a_ref, f32[31,128,128]{2,1,0:T(8,128)S(1)} %get-tuple-element.17.b_ref), custom_call_target="tpu_custom_call" | custom-call | flops 536870912 | bytes 4194304 | tf_op jit(solution)/shard_map/sweep/pallas_call | solution.py:329
  31.1 1.6 %collective-permute-done.state_ref = bf16[128,128]{1,0:T(8,128)(2,1)S(1)} collective-permute-done((bf16[128,128]{1,0:T(8,128)(2,1)S(1)}, bf16[128,128]{1,0:T(8,128)(2,1)S(1)}, u32[]{:S(2)}, u32[]{:S(2)}) %collective-permute-start) | collective-permute-done | bytes 32800 | tf_op jit(solution)/shard_map/ppermute | solution.py:318
  32.7 1.1 %states.1 = bf16[16,128,128]{2,1,0:T(8,128)(2,1)} custom-call(bf16[31,128,256]{2,1,0:T(8,128)(2,1)S(1)} %get-tuple-element.18.pa_ref, f32[31,128,128]{2,1,0:T(8,128)S(1)} %get-tuple-element.19.pb_ref, bf16[128,128]{1,0:T(8,128)(2,1)S(1)} %collective-permute-done.state_ref), custom_call_target="tpu_custom_call" | custom-call | flops 268435456 | bytes 4194304 | tf_op jit(solution)/shard_map/states/pallas_call | solution.py:332
  33.8 3.8 %all-to-all-start.1 = ((bf16[16,128,128]{2,1,0:T(8,128)(2,1)}), bf16[16,128,128]{2,1,0:T(8,128)(2,1)S(1)}, u32[]{:S(2)}, u32[]{:S(2)}) async-start(bf16[16,128,128]{2,1,0:T(8,128)(2,1)} %states.1), calls=%async_computation.1 | async-start | bytes 1048576 | tf_op jit(solution)/shard_map/all_to_all | solution.py:339
  37.6 0.0 copy-start
  37.6 6.5 %local.1 = (bf16[16,128,256]{2,1,0:T(8,128)(2,1)S(1)}, f32[16,128,128]{2,1,0:T(8,128)S(1)}) custom-call(bf16[128,2048]{1,0:T(8,128)(2,1)} %k_far, bf16[128,2048]{1,0:T(8,128)(2,1)} %v_far, bf16[128,2048]{1,0:T(8,128)(2,1)} %q_far), custom_call_target="tpu_custom_call" | custom-call | flops 5368709120 | bytes 4194304 | tf_op jit(solution)/shard_map/local/pallas_call | solution.py:340
  44.2 2.3 %all-to-all-done.1.state_ref = bf16[16,128,128]{2,1,0:T(8,128)(2,1)S(1)} async-done(((bf16[16,128,128]{2,1,0:T(8,128)(2,1)}), bf16[16,128,128]{2,1,0:T(8,128)(2,1)S(1)}, u32[]{:S(2)}, u32[]{:S(2)}) %all-to-all-start.1) | async-done | bytes 524320 | tf_op jit(solution)/shard_map/all_to_all | solution.py:339
  46.4 0.0 copy-done
  46.4 1.2 %final.1 = bf16[128,2048]{1,0:T(8,128)(2,1)} custom-call(bf16[16,128,256]{2,1,0:T(8,128)(2,1)S(1)} %get-tuple-element.24.qt_ref, f32[16,128,128]{2,1,0:T(8,128)S(1)} %get-tuple-element.25.ol_ref, bf16[16,128,128]{2,1,0:T(8,128)(2,1)S(1)} %all-to-all-done.1.state_ref, f32[1,128]{1,0:T(1,128)S(1)} %bitcast.1), custom_call_target="tpu_custom_call" | custom-call | flops 268435456 | bytes 4194304 | tf_op jit(solution)/shard_map/final/pallas_call | solution.py:344
Async XLA Ops:
  27.3 5.4 %collective-permute-start = (bf16[128,128]{1,0:T(8,128)(2,1)S(1)}, bf16[128,128]{1,0:T(8,128)(2,1)S(1)}, u32[]{:S(2)}, u32[]{:S(2)}) collective-permute-start(bf16[128,128]{1,0:T(8,128)(2,1)S(1)} %get-tuple-element.20), channel_id=1, source_target_pairs={{0,16},{16,0},{1,17},{17,1},{2,18},{18,2},{3,19},{19,3},{4,20},{20... | collective-permute-start | bytes 98312 | tf_op jit(solution)/shard_map/ppermute | solution.py:318
  33.8 12.6 %all-to-all-start.1 = ((bf16[16,128,128]{2,1,0:T(8,128)(2,1)}), bf16[16,128,128]{2,1,0:T(8,128)(2,1)S(1)}, u32[]{:S(2)}, u32[]{:S(2)}) async-start(bf16[16,128,128]{2,1,0:T(8,128)(2,1)} %states.1), calls=%async_computation.1 | async-start | bytes 1048576 | tf_op jit(solution)/shard_map/all_to_all | solution.py:339
  37.6 8.8 %copy-start = (f32[128]{0:T(128)S(1)}, f32[128]{0:T(128)}, u32[]{:S(2)}) copy-start(f32[128]{0:T(128)} %param.7) | copy-start | bytes 1540
